TPU v7x, 512 devices: a whole 4x4x16 slice. The times are simulated.
512 devices in a mesh: expert: 8 (over y, x_lo), dp: 64 (over z, x_hi, core).
Axes of the slice: x: 4 (x_hi: 2, x_lo: 2; x = x_hi * 2 + x_lo), y: 4, z: 16, core: 2. Of those that a mesh axis runs over, the one named last changes fastest.
Arguments:
- x_new: bfloat16 [512, 4096], P('expert', 'dp'), may hold values from -6 to 6
- routes_new: int32 [512, 2], P('expert'), may hold values from 0 to 7, all different within a row; in each aligned block of 64 rows (0 to 63, 64 to 127, ...) at most 32 rows name the same one
- gates_new: float32 [512, 2], P('expert'), may hold values from 0.2 to 1
- w_gate: bfloat16 [8, 4096, 7168], P('expert', None, 'dp'), may hold values from -0.09375 to 0.09375
- w_up: bfloat16 [8, 4096, 7168], P('expert', None, 'dp'), may hold values from -0.09375 to 0.09375
- w_down: bfloat16 [8, 7168, 4096], P('expert', 'dp'), may hold values from -0.1875 to 0.1875
- grad_out: bfloat16 [1024, 4096], P('expert', 'dp'), may hold values from -6 to 6
- routes_old: int32 [1024, 2], P('expert'), may hold values from 0 to 7, all different within a row; in each aligned block of 128 rows (0 to 127, 128 to 255, ...) at most 64 rows name the same one
- gates_old: float32 [1024, 2], P('expert'), may hold values from 0.2 to 1
- pre_gate: bfloat16 [8, 512, 7168], P('expert', None, 'dp'), may hold values from -8 to 8
- pre_up: bfloat16 [8, 512, 7168], P('expert', None, 'dp'), may hold values from -6 to 6
Outputs:
- mixed: bfloat16 [512, 4096], P('expert', 'dp')
- grad_down: bfloat16 [8, 7168, 4096], P('expert', 'dp')
- grad_gate: bfloat16 [8, 512, 7168], P('expert', None, 'dp')
- grad_up: bfloat16 [8, 512, 7168], P('expert', None, 'dp')
Inputs may be any that keep to these rules, and one draw needn't show every extreme that they name: `routes_new`: in each group of 64 tokens each expert is named by at most 32 tokens, and by exactly 32 tokens in some group; the two experts of a token differ. `routes_old`: in each group of 128 tokens each expert is named by at most 64 tokens, and by exactly 64 tokens in some group; the two experts of a token differ.
All inputs are finite; a program needn't handle non-finite values.
Results may differ from a plain program's by a relative error of at most 0.0078.
Values may be sent and summed in bfloat16 or wider, within the bound.
No kernel may reach another device: no remote copies, remote signals or barrier semaphores. Data moves between devices by JAX's collectives and lax.ppermute only.
A program may use at most 64 MiB of HBM per device.

v0:
```python
import jax
import jax.numpy as jnp
from jax import lax
from jax.sharding import Mesh
from jax.sharding import PartitionSpec as P

CAP_B = 32
CAP_A = 64
EXPERT = ("expert_0", "expert_1")
DP = ("dp_0", "dp_1", "dp_2")


def split_up(array, dim, size):
    before, after = (array.shape[:dim], array.shape[dim + 1 :])
    return jnp.moveaxis(array.reshape(*before, size, -1, *after), dim, 0)


def in_order(parts, dim):
    parts = jnp.moveaxis(parts, 0, dim)
    shape = parts.shape
    return parts.reshape(*shape[:dim], shape[dim] * shape[dim + 1], *shape[dim + 2 :])


def turned_blocks(parts, axes, turns):
    shape = [lax.axis_size(a) for a in axes]
    parts = parts.reshape(*shape, *parts.shape[1:])
    for k in turns:
        parts = lax.all_to_all(parts, axes[k], split_axis=k, concat_axis=k, tiled=True)
    return parts.reshape(-1, *parts.shape[len(axes) :])


def stepwise_exchange(array, axes, turns, split_dim, concat_dim):
    parts = split_up(array, split_dim, lax.axis_size(axes))
    return in_order(turned_blocks(parts, axes, turns), concat_dim)


def sum_at_owner(array, axis, dim):
    parts = split_up(array, dim, lax.axis_size(axis))
    arrived = lax.all_to_all(parts, axis, split_axis=0, concat_axis=0, tiled=True)
    return arrived.astype(jnp.float32).sum(axis=0)


def gather_in_order(array, axes, turns):
    parts = array[None]
    for k in turns:
        parts = lax.all_gather(parts, axes[k], axis=0, tiled=True)
    current = [lax.axis_size(axes[k]) for k in reversed(turns)]
    parts = parts.reshape(*current, *array.shape)
    turned = sorted(range(len(turns)), key=lambda place: turns[len(turns) - 1 - place])
    return parts.transpose(*turned, *range(len(turns), parts.ndim)).reshape(-1, *array.shape)


def gather_axes(array, axes, turns, dim):
    return in_order(gather_in_order(array, axes, turns), dim)


def slot_table(routes, capacity, experts):
    pairs = routes.reshape(-1)
    onehot = (pairs[:, None] == jnp.arange(experts, dtype=jnp.int32)[None, :]).astype(jnp.int32)
    before = jnp.cumsum(onehot, axis=0) - onehot
    slot = jnp.sum(before * onehot, axis=1)
    column = pairs * capacity + slot
    table = (jnp.arange(experts * capacity, dtype=jnp.int32)[:, None] == column[None, :]).astype(
        jnp.float32
    )
    return table.reshape(experts * capacity, routes.shape[0], 2)


def per_device(
    x_new,
    routes_new,
    gates_new,
    w_gate,
    w_up,
    w_down,
    grad_out,
    routes_old,
    gates_old,
    pre_gate,
    pre_up,
):
    experts = lax.axis_size(EXPERT)
    slice_width = x_new.shape[1]
    gate_weight = w_gate[0]
    up_weight = w_up[0]
    down_weight = w_down[0]
    rows_new = experts * CAP_B
    rows_old = experts * CAP_A
    table_new = slot_table(routes_new, CAP_B, experts)
    picks = jnp.sum(table_new, axis=2).astype(jnp.bfloat16)
    outgoing = jnp.dot(picks, x_new, preferred_element_type=jnp.float32).astype(jnp.bfloat16)
    arrived = stepwise_exchange(outgoing.reshape(experts, CAP_B, slice_width), EXPERT, (0, 1), 0, 0)
    arrived = arrived.reshape(rows_new, slice_width)
    piece = lax.all_gather(arrived, DP, axis=1, tiled=True)
    gate_pre = jnp.dot(piece, gate_weight, preferred_element_type=jnp.float32)
    up_pre = jnp.dot(piece, up_weight, preferred_element_type=jnp.float32)
    hidden = (jax.nn.silu(gate_pre) * up_pre).astype(jnp.bfloat16)
    partial_value = jnp.dot(hidden, down_weight, preferred_element_type=jnp.float32)
    result = sum_at_owner(partial_value.astype(jnp.bfloat16), DP, 1).astype(jnp.bfloat16)
    returned = lax.all_to_all(
        result.reshape(experts, CAP_B, slice_width), EXPERT, split_axis=0, concat_axis=0, tiled=True
    )
    returned = returned.reshape(rows_new, slice_width)
    weights_new = jnp.sum(table_new * gates_new[None, :, :], axis=2)
    mixed = jnp.dot(
        weights_new.T, returned.astype(jnp.float32), precision=lax.Precision.HIGHEST
    ).astype(jnp.bfloat16)
    table_old = slot_table(routes_old, CAP_A, experts)
    weights_old = jnp.sum(table_old * gates_old[None, :, :], axis=2)
    cotangent = jnp.dot(
        weights_old, grad_out.astype(jnp.float32), precision=lax.Precision.HIGHEST
    ).astype(jnp.bfloat16)
    landed = stepwise_exchange(cotangent.reshape(experts, CAP_A, slice_width), EXPERT, (0, 1), 0, 0)
    landed = landed.reshape(rows_old, slice_width)
    saved_gate = pre_gate[0].astype(jnp.float32)
    saved_up = pre_up[0].astype(jnp.float32)
    sigma = jax.nn.sigmoid(saved_gate)
    active = saved_gate * sigma
    hidden_old = (active * saved_up).astype(jnp.bfloat16)
    piece = gather_axes(landed, DP, (1, 0, 2), 1)
    grad_hidden = lax.dot_general(
        piece, down_weight, (((1,), (1,)), ((), ())), preferred_element_type=jnp.float32
    )
    block = lax.dot_general(
        hidden_old, piece, (((0,), (0,)), ((), ())), preferred_element_type=jnp.float32
    )
    weight_grad = block
    grad_hidden, weight_grad = (grad_hidden, weight_grad)
    gate_grad = (grad_hidden * saved_up * sigma * (1.0 + saved_gate * (1.0 - sigma))).astype(
        jnp.bfloat16
    )
    up_grad = (grad_hidden * active).astype(jnp.bfloat16)
    return (mixed, weight_grad.astype(jnp.bfloat16)[None], gate_grad[None], up_grad[None])


def solution(mesh):
    torus = Mesh(
        mesh.devices.reshape(4, 2, 16, 2, 2), ("expert_0", "expert_1", "dp_0", "dp_1", "dp_2")
    )
    placed = (
        P(EXPERT, DP),
        P(EXPERT, None),
        P(EXPERT, None),
        P(EXPERT, None, DP),
        P(EXPERT, None, DP),
        P(EXPERT, DP, None),
        P(EXPERT, DP),
        P(EXPERT, None),
        P(EXPERT, None),
        P(EXPERT, None, DP),
        P(EXPERT, None, DP),
    )
    return jax.shard_map(
        per_device,
        mesh=torus,
        in_specs=placed,
        out_specs=(P(EXPERT, DP), P(EXPERT, DP, None), P(EXPERT, None, DP), P(EXPERT, None, DP)),
        check_vma=False,
    )
```

profile of v0, /device:TPU:1, one launch (start us, length us, event | category | flops | bytes accessed | tf_op | source)
XLA Modules:
  0.0 352.6 jit_solution(8660613464620570664)
XLA Ops:
  7.2 0.8 copy.102
  9.6 0.8 convert_reduce_fusion
  10.4 0.9 convolution_convert_fusion.3
  11.5 9.1 %all_to_all.30 = bf16[4,2,2048]{2,1,0:T(2,128)(2,1)S(1)} all-to-all(bf16[4,2,2048]{2,1,0:T(2,128)(2,1)S(1)} %reshape.97), channel_id=1, replica_groups=mesh['expert_0'=4,'expert_1'=2,'dp_0'=16,'dp_1'=2,'dp_2'=2] {'expert_0'}, dimensions={0} | all-to-all | bytes 65536 | tf_op jit(solution)/shard_map/all_to_all | solution.py:28
  20.9 5.2 %all_to_all.31 = bf16[2,2,4096]{2,1,0:T(2,128)(2,1)S(1)} all-to-all(bf16[2,2,4096]{2,1,0:T(2,128)(2,1)S(1)} %reshape.99), channel_id=1, replica_groups=mesh['expert_0'=4,'expert_1'=2,'dp_0'=16,'dp_1'=2,'dp_2'=2] {'expert_1'}, dimensions={0} | all-to-all | bytes 65536 | tf_op jit(solution)/shard_map/all_to_all | solution.py:28
  27.0 0.8 copy.111
  29.9 0.8 select_reduce_fusion
  31.4 6.8 %all_to_all.32 = bf16[4,2,4096]{2,1,0:T(2,128)(2,1)S(1)} all-to-all(bf16[4,2,4096]{2,1,0:T(2,128)(2,1)S(1)} %reshape.103), channel_id=1, replica_groups=mesh['expert_0'=4,'expert_1'=2,'dp_0'=16,'dp_1'=2,'dp_2'=2] {'expert_0'}, dimensions={0} | all-to-all | bytes 131072 | tf_op jit(solution)/shard_map/all_to_all | solution.py:28
  38.6 5.4 %all_to_all.33 = bf16[2,2,8192]{2,1,0:T(2,128)(2,1)S(1)} all-to-all(bf16[2,2,8192]{2,1,0:T(2,128)(2,1)S(1)} %reshape.105), channel_id=1, replica_groups=mesh['expert_0'=4,'expert_1'=2,'dp_0'=16,'dp_1'=2,'dp_2'=2] {'expert_1'}, dimensions={0} | all-to-all | bytes 131072 | tf_op jit(solution)/shard_map/all_to_all | solution.py:28
  44.4 5.7 %all_gather.13 = bf16[2,512,64]{1,2,0:T(8,128)(2,1)} all-gather(bf16[1,512,64]{1,2,0:T(8,128)(2,1)S(1)} %broadcast_in_dim_reshape_reshape_reshape.3), channel_id=1, replica_groups=mesh['expert_0'=4,'expert_1'=2,'dp_0'=16,'dp_1'=2,'dp_2'=2] {'dp_1'}, dimensions={0}, use_global_device_ids=true | all-gather | bytes 196608 | tf_op jit(solution)/shard_map/all_gather | solution.py:46
  50.2 126.3 %all-gather.4.cloned.1.call-done = bf16[256,4096]{0,1:T(8,128)(2,1)} async-done(((bf16[256,64]{0,1:T(8,128)(2,1)}), bf16[256,4096]{0,1:T(8,128)(2,1)}) %all-gather.4.cloned.1.call-update) | async-done | bytes 2097168 | tf_op jit(solution)/shard_map/all_gather | solution.py:94
  176.4 2.5 fusion.7
  178.9 4.2 %convolution_convert_fusion = bf16[256,4096]{1,0:T(8,128)(2,1)} fusion(bf16[256,4096]{0,1:T(8,128)(2,1)S(1)} %copy-done.2, bf16[1,112,4096]{2,1,0:T(8,128)(2,1)S(1)} %copy-done, bf16[1,4096,112]{1,2,0:T(8,128)(2,1)} %param.15, f32[256,112]{0,1:T(8,128)S(1)} %fusion.7), kind=kOutput, calls=%fused_computation | convolution fusion | flops 470982656 | bytes 6144000 | tf_op jit(solution)/shard_map/dot_general | solution.py:98
  183.1 4.1 %copy.109 = bf16[256,4096]{0,1:T(8,128)(2,1)} copy(bf16[256,4096]{1,0:T(8,128)(2,1)} %convolution_convert_fusion) | data formatting | bytes 4194304 | tf_op jit(solution)/shard_map/convert_element_type | solution.py:99
  187.2 7.9 %all-to-all-start.2 = ((bf16[64,256,64]{1,2,0:T(8,128)(2,1)}), bf16[64,256,64]{1,2,0:T(8,128)(2,1)S(1)}, u32[]{:S(2)}, u32[]{:S(2)}) async-start(bf16[64,256,64]{1,2,0:T(8,128)(2,1)} %bitcast.121), calls=%async_computation.2 | async-start | bytes 4194304 | tf_op jit(solution)/shard_map/all_to_all | solution.py:39
  195.1 102.4 %all-gather.6.cloned.1.call-done = bf16[32,512,64]{1,2,0:T(8,128)(2,1)} async-done(((bf16[2,512,64]{1,2,0:T(8,128)(2,1)}), bf16[32,512,64]{1,2,0:T(8,128)(2,1)}) %all-gather.6.cloned.1.call-update) | async-done | bytes 2097168 | tf_op jit(solution)/shard_map/all_gather | solution.py:46
  297.6 31.2 %all-gather.8.cloned.1.call-done = bf16[64,512,64]{1,2,0:T(8,128)(2,1)} async-done(((bf16[32,512,64]{1,2,0:T(8,128)(2,1)}), bf16[64,512,64]{1,2,0:T(8,128)(2,1)}) %all-gather.8.cloned.1.call-update) | async-done | bytes 4194320 | tf_op jit(solution)/shard_map/all_gather | solution.py:46
  328.8 2.7 copy.117
  331.6 1.9 copy-done.1
  333.5 1.5 fusion.33
  335.4 0.7 reshape.101
  336.1 3.9 %all-to-all-start.3 = ((bf16[8,2,1024]{2,1,0:T(2,128)(2,1)}), bf16[8,2,1024]{2,1,0:T(2,128)(2,1)S(1)}, u32[]{:S(2)}, u32[]{:S(2)}) async-start(bf16[8,2,1024]{2,1,0:T(2,128)(2,1)} %reshape.101), calls=%async_computation.3 | async-start | bytes 65536 | tf_op jit(solution)/shard_map/all_to_all | solution.py:100
  340.0 4.5 %fusion = bf16[1,112,4096]{2,1,0:T(8,128)(2,1)} fusion(bf16[512,4096]{0,1:T(8,128)(2,1)} %bitcast.120, bf16[1,512,112]{1,2,0:T(8,128)(2,1)S(1)} %copy-done.3, bf16[1,512,112]{1,2,0:T(8,128)(2,1)S(1)} %copy-done.4), kind=kOutput, calls=%fused_computation.2 | convolution fusion | flops 470679552 | bytes 5341184 | tf_op jit(solution)/shard_map/dot_general | solution.py:124
  345.2 0.8 convolution_convert_fusion.4
  (58 shorter events, 7.7 us)
Async XLA Ops:
  7.2 171.7 %copy-start = (bf16[1,112,4096]{2,1,0:T(8,128)(2,1)S(1)}, bf16[1,112,4096]{2,1,0:T(8,128)(2,1)}, u32[]{:S(2)}) copy-start(bf16[1,112,4096]{2,1,0:T(8,128)(2,1)} %param.16) | copy-start | bytes 2752516
  7.2 23.5 %copy-start.5 = (bf16[128,64]{0,1:T(8,128)(2,1)S(1)}, bf16[128,64]{0,1:T(8,128)(2,1)}, u32[]{:S(2)}) copy-start(bf16[128,64]{0,1:T(8,128)(2,1)} %param.17) | copy-start | bytes 49156
  7.2 169.2 %all-gather.4.cloned.1.call-start = ((), (), s32[]{:S(2)}) async-start(), calls=%async_computation.6 | async-start | bytes 2129920 | tf_op jit(solution)/shard_map/all_gather | solution.py:94
  26.9 270.7 %all-gather.6.cloned.1.call-start = ((), (), s32[]{:S(2)}) async-start(), calls=%async_computation.7 | async-start | bytes 2228224 | tf_op jit(solution)/shard_map/all_gather | solution.py:46
  176.4 2.5 copy-start.2
  187.2 147.8 %all-to-all-start.2 = ((bf16[64,256,64]{1,2,0:T(8,128)(2,1)}), bf16[64,256,64]{1,2,0:T(8,128)(2,1)S(1)}, u32[]{:S(2)}, u32[]{:S(2)}) async-start(bf16[64,256,64]{1,2,0:T(8,128)(2,1)} %bitcast.121), calls=%async_computation.2 | async-start | bytes 4194304 | tf_op jit(solution)/shard_map/all_to_all | solution.py:39
  195.1 133.7 %all-gather.8.cloned.1.call-start = ((), (), s32[]{:S(2)}) async-start(), calls=%async_computation.8 | async-start | bytes 6291456 | tf_op jit(solution)/shard_map/all_gather | solution.py:46
  328.8 4.7 %copy-start.3 = (bf16[1,512,112]{1,2,0:T(8,128)(2,1)S(1)}, bf16[1,512,112]{1,2,0:T(8,128)(2,1)}, u32[]{:S(2)}) copy-start(bf16[1,512,112]{1,2,0:T(8,128)(2,1)} %param.21) | copy-start | bytes 344068
  328.8 4.7 %copy-start.4 = (bf16[1,512,112]{1,2,0:T(8,128)(2,1)S(1)}, bf16[1,512,112]{1,2,0:T(8,128)(2,1)}, u32[]{:S(2)}) copy-start(bf16[1,512,112]{1,2,0:T(8,128)(2,1)} %param.20) | copy-start | bytes 344068
  331.6 1.9 copy-start.1
  336.1 9.0 %all-to-all-start.3 = ((bf16[8,2,1024]{2,1,0:T(2,128)(2,1)}), bf16[8,2,1024]{2,1,0:T(2,128)(2,1)S(1)}, u32[]{:S(2)}, u32[]{:S(2)}) async-start(bf16[8,2,1024]{2,1,0:T(2,128)(2,1)} %reshape.101), calls=%async_computation.3 | async-start | bytes 65536 | tf_op jit(solution)/shard_map/all_to_all | solution.py:100
Sparse Core Ops, SparseCore 0:
  27.0 149.3 all-gather.3
  178.5 119.0 all-gather.5
  299.7 29.1 all-gather.7
where the time goes:
time: 353 us
  waiting for transfers between devices  261 us (74%)
  blocking collectives  32.2 us (9%)
  local copies, waits for them, and re-layouts  14.9 us (4%)
  matrix products  14.6 us (4%)
  between operations  14 us (4%)
  starting transfers between devices  11.9 us (3%)
  other arithmetic  4.41 us (1%)
    all_gather x2, waiting for transfers between devices, gather_in_order(): parts = lax.all_gather(parts, axes[k], axis=0, tiled=True)  134 us
    all_gather x1, waiting for transfers between devices, per_device(): piece = lax.all_gather(arrived, DP, axis=1, tiled=True)  126 us
    all_to_all x4, blocking collectives, turned_blocks(): lax.all_to_all(parts, axes[k], split_axis=k, concat_axis=k, tiled=True)  26.5 us
    all_to_all x1, starting transfers between devices, sum_at_owner(): lax.all_to_all(parts, axis, split_axis=0, concat_axis=0, tiled=True)  7.87 us
  transfers between devices with their start and end apart: 5, of which 4 were waited for; matrix products, arithmetic and copies ran while one was open for 7% of the time, Pallas kernels for 0%

commit v1 on v0

v1 whole, which is shorter than its diff:
```python
import functools

import jax
import jax.numpy as jnp
from jax import lax
from jax.experimental import pallas as pl
from jax.experimental.pallas import tpu as pltpu
from jax.sharding import Mesh
from jax.sharding import PartitionSpec as P

CAP_B = 32
CAP_A = 64
EXPERT = ("expert_0", "expert_1")
DP = ("dp_0", "dp_1", "dp_2")
Z = "dp_0"
CORE = "dp_2"
PLANE = ("dp_1", "expert_0", "expert_1")
F = 32
BF = jnp.bfloat16
F32 = jnp.float32
LAST = (((1,), (1,)), ((), ()))
MIB = 1 << 20


def iota(shape, dim):
    return lax.broadcasted_iota(jnp.int32, shape, dim)


def dot(a, b):
    return jnp.dot(a, b, preferred_element_type=F32)


def dot_last(a, b):
    return lax.dot_general(a, b, LAST, preferred_element_type=F32)


def call(body, outs, *args, flops=10**7, moved=10**6, scalars=0):
    vmem = pl.BlockSpec(memory_space=pltpu.VMEM)
    smem = pl.BlockSpec(memory_space=pltpu.SMEM)
    many = isinstance(outs, (tuple, list))
    return pl.pallas_call(
        body,
        out_shape=outs,
        in_specs=[smem] * scalars + [vmem] * (len(args) - scalars),
        out_specs=tuple(vmem for _ in outs) if many else vmem,
        cost_estimate=pl.CostEstimate(flops=flops, bytes_accessed=moved, transcendentals=0),
        compiler_params=pltpu.CompilerParams(vmem_limit_bytes=40 * MIB),
        name=body.__name__,
    )(*args)


def shape(*dims, dtype=BF):
    return jax.ShapeDtypeStruct(dims, dtype)


def lane_order(me):
    i, j = iota((512, 512), 0), iota((512, 512), 1)
    core = jnp.bitwise_xor((i // 64) % 2, me)
    hit = (
        (i // 128 == (j // F) % 4)
        & (core == j // 256)
        & ((i // F) % 2 == (j // 128) % 2)
        & (i % F == j % F)
    )
    return jnp.where(hit, 1.0, 0.0).astype(BF)


def weights_kernel(me_ref, gate_ref, up_ref, down_ref, gu_ref, dn_ref):
    order = lane_order(me_ref[0])
    gu_ref[...] = jnp.zeros_like(gu_ref)
    dn_ref[...] = jnp.zeros_like(dn_ref)
    hidden = gate_ref.shape[0]
    for ref, out, base in ((gate_ref, gu_ref, 0), (up_ref, gu_ref, 128), (down_ref, dn_ref, 0)):
        for xh in range(2):
            for zq in range(4):
                tiles = [
                    ref[:, pl.ds((zq * 4 + zi) * 256 + xh * 128, 128)] for zi in range(4)
                ]
                moved = dot(jnp.concatenate(tiles, axis=1), order).astype(BF)
                for o in range(2):
                    for h in range(2):
                        out[o, xh, pl.ds(base, hidden), pl.ds(h * 512 + zq * 128, 128)] = moved[
                            :, (o * 2 + h) * 128 : (o * 2 + h + 1) * 128
                        ]


def pack_kernel(x_ref, g_ref, out_ref):
    x = x_ref[...]
    toks, feats = x.shape
    twice = jnp.concatenate([x, x], axis=0)
    keep = iota(twice.shape, 1) // F == iota(twice.shape, 0) // toks
    twice = jnp.where(keep, twice, jnp.zeros_like(twice))
    pick = jnp.where(iota((F, feats), 1) % F == iota((F, feats), 0), 1.0, 0.0).astype(BF)
    block = jnp.concatenate([dot_last(pick, twice).astype(BF), g_ref[...]], axis=0)
    for z in range(out_ref.shape[0]):
        out_ref[z] = block


def placed(routes, rows, capacity, tokens):
    lanes = routes.shape[1]
    expert = iota((rows, lanes), 0) // capacity
    slot = iota((rows, lanes), 0) % capacity
    first, second = routes[0:1, :] == expert, routes[1:2, :] == expert
    named = first | second
    i, j = iota((lanes, lanes), 0), iota((lanes, lanes), 1)
    earlier = jnp.where((i < tokens) & (i < j % tokens), 1.0, 0.0).astype(BF)
    before = dot(jnp.where(named, 1.0, 0.0).astype(BF), earlier)
    return named & (before == slot.astype(F32)), first, second


def rows_new_kernel(routes_ref, got_ref, out_ref):
    routes = routes_ref[...]
    rows = out_ref.shape[1]
    toks = routes.shape[1] // 2
    hit, _, _ = placed(routes, rows, CAP_B, toks)
    lane = iota(hit.shape, 1) // toks
    x = got_ref[:, 0:F, :].reshape(-1, 2 * toks)
    width = x.shape[0]
    for h in range(2):
        picks = jnp.where(hit & (lane == h), 1.0, 0.0).astype(BF)
        block = dot_last(picks, x).astype(BF)
        for xh in range(2):
            out_ref[xh, :, h * width : (h + 1) * width] = block


def rows_old_kernel(routes_ref, gates_ref, got_ref, out_ref):
    routes, gates = routes_ref[...], gates_ref[...]
    rows, toks = out_ref.shape[1], routes.shape[1]
    hit, first, second = placed(routes, rows, CAP_A, toks)
    weight = jnp.where(first, gates[0:1, :], 0.0) + jnp.where(second, gates[1:2, :], 0.0)
    weight = jnp.sum(jnp.where(hit, weight, 0.0), axis=1, keepdims=True)
    picks = jnp.where(hit, 1.0, 0.0).astype(BF)
    for h in range(2):
        g = got_ref[:, F * (1 + h) : F * (2 + h), :].reshape(-1, toks)
        block = (dot_last(picks, g) * weight).astype(BF)
        width = block.shape[1]
        for xh in range(2):
            out_ref[xh, :, h * width : (h + 1) * width] = block


def up_kernel(own_ref, other_ref, gu_ref, dn_ref, hidden_ref, out_ref):
    total = None
    for o, ref in enumerate((own_ref, other_ref)):
        for xh in range(2):
            term = dot_last(ref[xh], gu_ref[o, xh])
            total = term if total is None else total + term
    gate, up = total[:, :128], total[:, 128:]
    hidden = (gate / (1.0 + jnp.exp(-gate)) * up).astype(BF)
    hidden_ref[...] = hidden
    for xh in range(2):
        out_ref[xh] = dot(hidden, dn_ref[1, xh]).astype(BF)


def down_kernel(hidden_ref, dn_ref, arrived_ref, out_ref):
    hidden = hidden_ref[...]
    for xh in range(2):
        out_ref[xh] = (dot(hidden, dn_ref[0, xh]) + arrived_ref[xh].astype(F32)).astype(BF)


def mix_kernel(routes_ref, gates_ref, got_ref, out_ref):
    routes, gates = routes_ref[...], gates_ref[...]
    rows, width = got_ref.shape[1], got_ref.shape[2] // 2
    toks = routes.shape[1] // 2
    hit, first, second = placed(routes, rows, CAP_B, toks)
    weight = jnp.where(first, gates[0:1, :], 0.0) + jnp.where(second, gates[1:2, :], 0.0)
    weight = jnp.where(hit, weight, 0.0).T[:toks]
    high = weight.astype(BF)
    rest = weight - high.astype(F32)
    middle = rest.astype(BF)
    low = (rest - middle.astype(F32)).astype(BF)
    halves = []
    for h in range(2):
        total = None
        for xh in range(2):
            got = got_ref[xh, :, h * width : (h + 1) * width]
            for part in (high, middle, low):
                term = dot(part, got)
                total = term if total is None else total + term
        halves.append(total)
    mixed = jnp.concatenate(halves, axis=0).T.astype(BF)
    out_ref[...] = mixed.reshape(out_ref.shape)


def total_kernel(got_ref, out_ref):
    total = got_ref[0].astype(F32)
    for z in range(1, got_ref.shape[0]):
        total = total + got_ref[z].astype(F32)
    turned = total.T
    toks = out_ref.shape[0]
    out_ref[...] = jnp.concatenate([turned[:toks], turned[toks:]], axis=1).astype(BF)


def back_kernel(me_ref, own_ref, other_ref, dn_ref, gate_ref, up_ref, down_ref, dg_ref, du_ref, held):
    total = None
    refs = (own_ref, other_ref)
    for o, ref in enumerate(refs):
        for xh in range(2):
            term = dot_last(dn_ref[o, xh], ref[xh])
            total = term if total is None else total + term
    gate, up = gate_ref[...].astype(F32), up_ref[...].astype(F32)
    grad = total[: gate.shape[0]]
    sigma = 1.0 / (1.0 + jnp.exp(-gate))
    active = gate * sigma
    dg_ref[...] = (grad * up * sigma * (1.0 + gate * (1.0 - sigma))).astype(BF)
    du_ref[...] = (grad * active).astype(BF)
    hidden = (active * up).astype(BF)
    for o, ref in enumerate(refs):
        for xh in range(2):
            held[o, xh] = dot(hidden, ref[xh]).astype(BF)
    order = lane_order(me_ref[0])
    for xh in range(2):
        for zq in range(4):
            tiles = [
                held[o, xh, :, pl.ds(h * 512 + zq * 128, 128)] for o in range(2) for h in range(2)
            ]
            moved = dot_last(jnp.concatenate(tiles, axis=1), order).astype(BF)
            for zi in range(4):
                down_ref[:, pl.ds((zq * 4 + zi) * 256 + xh * 128, 128)] = moved[
                    :, zi * 128 : (zi + 1) * 128
                ]


def other_core(array):
    return lax.ppermute(array, CORE, [(0, 1), (1, 0)])


def over_plane(rows):
    peers = rows.reshape(16, -1, rows.shape[2])
    return lax.all_to_all(peers, PLANE, 0, 0, tiled=True).reshape(rows.shape)


def per_device(
    x_new,
    routes_new,
    gates_new,
    w_gate,
    w_up,
    w_down,
    grad_out,
    routes_old,
    gates_old,
    pre_gate,
    pre_up,
):
    me = lax.axis_index(CORE).astype(jnp.int32).reshape(1)
    experts = lax.axis_size(EXPERT)
    rows_new, rows_old = experts * CAP_B, experts * CAP_A
    hidden_units = w_gate.shape[2]
    twice = lambda a: jnp.concatenate([a.T, a.T], axis=1)
    routes_b, gates_b = twice(routes_new), twice(gates_new)
    routes_a, gates_a = routes_old.T, gates_old.T

    packed = call(pack_kernel, shape(16, 3 * F, 128), x_new, grad_out.T)
    got = lax.all_to_all(packed, Z, 0, 0, tiled=True)
    gate_up, down = call(
        weights_kernel,
        (shape(2, 2, 256, 1024), shape(2, 2, 128, 1024)),
        me,
        w_gate[0].T,
        w_up[0].T,
        w_down[0],
        scalars=1,
        flops=14 * 10**8,
        moved=6 * 10**6,
    )

    own = over_plane(call(rows_new_kernel, shape(2, rows_new, 1024), routes_b, got))
    other = other_core(own)
    hidden, partial = call(
        up_kernel,
        (shape(rows_new, 128), shape(2, rows_new, 1024)),
        own,
        other,
        gate_up,
        down,
        flops=8 * 10**8,
        moved=4 * 10**6,
    )
    summed = call(
        down_kernel, shape(2, rows_new, 1024), hidden, down, other_core(partial), flops=2 * 10**8
    )
    mixed = call(
        mix_kernel, shape(16, F, 128), routes_b, gates_b, over_plane(summed), flops=4 * 10**8
    )
    mixed = lax.all_to_all(mixed, Z, 0, 0, tiled=True)
    mixed = call(total_kernel, shape(*x_new.shape), mixed)

    own_a = over_plane(call(rows_old_kernel, shape(2, rows_old, 1024), routes_a, gates_a, got))
    other_a = other_core(own_a)
    vmem = pl.BlockSpec(memory_space=pltpu.VMEM)
    weight_grad, gate_grad, up_grad = pl.pallas_call(
        back_kernel,
        out_shape=(
            shape(hidden_units, 4096),
            shape(hidden_units, rows_old),
            shape(hidden_units, rows_old),
        ),
        in_specs=[pl.BlockSpec(memory_space=pltpu.SMEM)] + [vmem] * 5,
        out_specs=(vmem,) * 3,
        scratch_shapes=[pltpu.VMEM((2, 2, hidden_units, 1024), BF)],
        cost_estimate=pl.CostEstimate(
            flops=15 * 10**8, bytes_accessed=8 * 10**6, transcendentals=0
        ),
        compiler_params=pltpu.CompilerParams(vmem_limit_bytes=40 * MIB),
        name="back_kernel",
    )(me, own_a, other_a, down, pre_gate[0].T, pre_up[0].T)
    return (mixed, weight_grad[None], gate_grad.T[None], up_grad.T[None])


def solution(mesh):
    torus = Mesh(
        mesh.devices.reshape(4, 2, 16, 2, 2), ("expert_0", "expert_1", "dp_0", "dp_1", "dp_2")
    )
    placed_as = (
        P(EXPERT, DP),
        P(EXPERT, None),
        P(EXPERT, None),
        P(EXPERT, None, DP),
        P(EXPERT, None, DP),
        P(EXPERT, DP, None),
        P(EXPERT, DP),
        P(EXPERT, None),
        P(EXPERT, None),
        P(EXPERT, None, DP),
        P(EXPERT, None, DP),
    )
    return jax.shard_map(
        per_device,
        mesh=torus,
        in_specs=placed_as,
        out_specs=(P(EXPERT, DP), P(EXPERT, DP, None), P(EXPERT, None, DP), P(EXPERT, None, DP)),
        check_vma=False,
    )
```

time: 353 us -> 153 us (0.43)
  waiting for transfers between devices: 261 us -> 52 us
  starting transfers between devices: 11.9 us -> 72.5 us
  blocking collectives: 32.2 us -> 0 us
  Pallas kernels: 0 us -> 19.9 us
  matrix products: 14.6 us -> 0 us
  between operations: 14 us -> 0.8 us
  local copies, waits for them, and re-layouts: 14.9 us -> 4.98 us
    all_gather x3 -> x0, waiting for transfers between devices: 260 us -> none  [the longest x2 134 us: gather_in_order(): parts = lax.all_gather(parts, axes[k], axis=0, tiled=True)]
    all_to_all x2 -> x5, waiting for transfers between devices: 0.57 us -> 52 us  [the longest x3 29.7 us: over_plane(): return lax.all_to_all(peers, PLANE, 0, 0, tiled=True).reshape(rows.shape)]
    all_to_all x2 -> x5, starting transfers between devices: 11.8 us -> 49.7 us  [the longest x1 18.1 us: per_device(): mixed = lax.all_to_all(mixed, Z, 0, 0, tiled=True)]
    all_to_all x4 -> x0, blocking collectives: 26.5 us -> none  [turned_blocks(): lax.all_to_all(parts, axes[k], split_axis=k, concat_axis=k, tiled=True)]
    ppermute x0 -> x3, starting transfers between devices: none -> 22.9 us  [other_core(): return lax.ppermute(array, CORE, [(0, 1), (1, 0)])]
    pallas_call x0 -> x9, Pallas kernels: none -> 19.9 us  [the longest x8 13.1 us: call(): pl.pallas_call(body, out_shape=outs, in_specs=[smem] * scalars + [vmem] *...]
    dot_general x7 -> x0, matrix products: 14.6 us -> none  [the longest x1 4.54 us: per_device(): lax.dot_general(hidden_old, piece, (((0,), (0,)), ((), ())), preferred_el...]
    all_gather x1 -> x0, blocking collectives: 5.71 us -> none  [gather_in_order(): parts = lax.all_gather(parts, axes[k], axis=0, tiled=True)]
  transfers between devices with their start and end apart: 5 -> 8, of which waited for: 4 -> 5; matrix products, arithmetic and copies ran while one was open for 7% -> 1% of each run, Pallas kernels for 0% -> 11%
where the time goes in v1:
time: 153 us; the launch traced here: 151 us
  starting transfers between devices  72.5 us (47%)
  waiting for transfers between devices  52 us (34%)
  Pallas kernels  19.9 us (13%)
  local copies, waits for them, and re-layouts  4.98 us (3%)
    all_to_all x3, waiting for transfers between devices, over_plane(): return lax.all_to_all(peers, PLANE, 0, 0, tiled=True).reshape(rows.shape)  29.7 us
    ppermute x3, starting transfers between devices, other_core(): return lax.ppermute(array, CORE, [(0, 1), (1, 0)])  22.9 us
    all_to_all x1, starting transfers between devices, per_device(): mixed = lax.all_to_all(mixed, Z, 0, 0, tiled=True)  18.1 us
    all_to_all x1, waiting for transfers between devices, per_device(): got = lax.all_to_all(packed, Z, 0, 0, tiled=True)  17.2 us
    all_to_all x1, starting transfers between devices, per_device(): got = lax.all_to_all(packed, Z, 0, 0, tiled=True)  15.9 us
    all_to_all x3, starting transfers between devices, over_plane(): return lax.all_to_all(peers, PLANE, 0, 0, tiled=True).reshape(rows.shape)  15.7 us
    pallas_call x8, Pallas kernels, call(): pl.pallas_call(body, out_shape=outs, in_specs=[smem] * scalars + [vmem] *...  13.1 us
    pallas_call x1, Pallas kernels, per_device(): pl.pallas_call(back_kernel, out_shape=(shape(hidden_units, 4096), shape(h...  6.77 us
  transfers between devices with their start and end apart: 8, of which 5 were waited for; matrix products, arithmetic and copies ran while one was open for 1% of the time, Pallas kernels for 11%

profile of v1, /device:TPU:1, one launch (start us, length us, event | category | flops | bytes accessed | tf_op | source)
XLA Modules:
  0.0 151.2 jit_solution(6363077143245937547)
XLA Ops:
  2.1 0.9 pack_kernel.1
  3.0 15.9 %all-to-all-start = ((bf16[16,96,128]{2,1,0:T(8,128)(2,1)}), bf16[16,96,128]{2,1,0:T(8,128)(2,1)S(1)}, u32[]{:S(2)}, u32[]{:S(2)}) async-start(bf16[16,96,128]{2,1,0:T(8,128)(2,1)} %pack_kernel.1), calls=%async_computation | async-start | bytes 786432 | tf_op jit(solution)/shard_map/all_to_all | solution.py:254
  19.7 17.2 %all-to-all-done.got_ref = bf16[16,96,128]{2,1,0:T(8,128)(2,1)S(1)} async-done(((bf16[16,96,128]{2,1,0:T(8,128)(2,1)}), bf16[16,96,128]{2,1,0:T(8,128)(2,1)S(1)}, u32[]{:S(2)}, u32[]{:S(2)}) %all-to-all-start) | async-done | bytes 393248 | tf_op jit(solution)/shard_map/all_to_all | solution.py:254
  36.9 1.4 rows_new_kernel.1
  38.3 6.8 %all-to-all-start.1 = ((bf16[16,32,1024]{2,1,0:T(8,128)(2,1)}), bf16[16,32,1024]{2,1,0:T(8,128)(2,1)S(1)}, u32[]{:S(2)}, u32[]{:S(2)}) async-start(bf16[16,32,1024]{2,1,0:T(8,128)(2,1)} %bitcast.3), calls=%async_computation.1 | async-start | bytes 2097152 | tf_op jit(solution)/shard_map/all_to_all | solution.py:229
  45.1 1.9 %rows_old_kernel.1 = bf16[2,512,1024]{2,1,0:T(8,128)(2,1)} custom-call(s32[2,128]{1,0:T(2,128)S(1)} %bitcast.36, f32[2,128]{1,0:T(2,128)S(1)} %bitcast.37, bf16[16,96,128]{2,1,0:T(8,128)(2,1)S(1)} %all-to-all-done.got_ref), custom_call_target="tpu_custom_call" | custom-call | flops 10000000 | bytes 1000000 | tf_op jit(solution)/shard_map/rows_old_kernel/pallas_call | solution.py:41
  47.0 10.6 %all-to-all-done.1 = bf16[16,32,1024]{2,1,0:T(8,128)(2,1)S(1)} async-done(((bf16[16,32,1024]{2,1,0:T(8,128)(2,1)}), bf16[16,32,1024]{2,1,0:T(8,128)(2,1)S(1)}, u32[]{:S(2)}, u32[]{:S(2)}) %all-to-all-start.1) | async-done | bytes 1048608 | tf_op jit(solution)/shard_map/all_to_all | solution.py:229
  57.6 4.4 %all-to-all-start.4 = ((bf16[16,64,1024]{2,1,0:T(8,128)(2,1)}), bf16[16,64,1024]{2,1,0:T(8,128)(2,1)}, u32[]{:S(2)}, u32[]{:S(2)}) async-start(bf16[16,64,1024]{2,1,0:T(8,128)(2,1)} %bitcast.15), calls=%async_computation.4 | async-start | bytes 4194304 | tf_op jit(solution)/shard_map/all_to_all | solution.py:229
  62.0 9.6 %collective-permute-start = (bf16[2,256,1024]{2,1,0:T(8,128)(2,1)S(1)}, bf16[2,256,1024]{2,1,0:T(8,128)(2,1)S(1)}, u32[]{:S(2)}, u32[]{:S(2)}) collective-permute-start(bf16[2,256,1024]{2,1,0:T(8,128)(2,1)S(1)} %bitcast.32), channel_id=1, source_target_pairs={{0,1},{1,0},{2,3},{3,2},{4,5},{5,4},{6,7},{7,6},{8,9},{9,8},{10,11... | collective-permute-start | bytes 3145736 | tf_op jit(solution)/shard_map/ppermute | solution.py:224
  71.7 1.2 copy-done.4
  72.8 1.2 copy-done.5
  74.0 1.2 copy-done.6
  75.2 2.5 %weights_kernel.1 = (bf16[2,2,256,1024]{3,2,1,0:T(8,128)(2,1)S(1)}, bf16[2,2,128,1024]{3,2,1,0:T(8,128)(2,1)S(1)}) custom-call(s32[1]{0:T(128)} %bitcast.5.me_ref, bf16[112,4096]{1,0:T(8,128)(2,1)S(1)} %bitcast.38, bf16[112,4096]{1,0:T(8,128)(2,1)S(1)} %bitcast.39, bf16[112,4096]{1,0:T(8,128)(2,1)S(1)} %bitcast.40), custom_call_target="tpu_custom_call" | custom-call | flops 1400000000 | bytes 6000000 | tf_op jit(solution)/shard_map/weights_kernel/pallas_call | solution.py:41
  77.7 2.6 %up_kernel.1 = (bf16[256,128]{1,0:T(8,128)(2,1)S(1)}, bf16[2,256,1024]{2,1,0:T(8,128)(2,1)}) custom-call(bf16[2,256,1024]{2,1,0:T(8,128)(2,1)S(1)} %bitcast.33, bf16[2,256,1024]{2,1,0:T(8,128)(2,1)S(1)} %collective-permute-done.other_ref, bf16[2,2,256,1024]{3,2,1,0:T(8,128)(2,1)S(1)} %get-tuple-element.11.gu_ref, ...), custom_call_target="tpu_custom_call" | custom-call | flops 800000000 | bytes 4000000 | tf_op jit(solution)/shard_map/up_kernel/pallas_call | solution.py:41
  80.3 1.9 %collective-permute-start.1 = (bf16[2,256,1024]{2,1,0:T(8,128)(2,1)}, bf16[2,256,1024]{2,1,0:T(8,128)(2,1)S(1)}, u32[]{:S(2)}, u32[]{:S(2)}) collective-permute-start(bf16[2,256,1024]{2,1,0:T(8,128)(2,1)} %get-tuple-element.14), channel_id=1, source_target_pairs={{0,1},{1,0},{2,3},{3,2},{4,5},{5,4},{6,7},{7,6},{8,9},{9,8},{10,11... | collective-permute-start | bytes 3145736 | tf_op jit(solution)/shard_map/ppermute | solution.py:224
  82.2 1.7 %all-to-all-done.4 = bf16[16,64,1024]{2,1,0:T(8,128)(2,1)} async-done(((bf16[16,64,1024]{2,1,0:T(8,128)(2,1)}), bf16[16,64,1024]{2,1,0:T(8,128)(2,1)}, u32[]{:S(2)}, u32[]{:S(2)}) %all-to-all-start.4) | async-done | bytes 2097184 | tf_op jit(solution)/shard_map/all_to_all | solution.py:229
  83.9 11.3 %collective-permute-start.2 = (bf16[2,512,1024]{2,1,0:T(8,128)(2,1)}, bf16[2,512,1024]{2,1,0:T(8,128)(2,1)}, u32[]{:S(2)}, u32[]{:S(2)}) collective-permute-start(bf16[2,512,1024]{2,1,0:T(8,128)(2,1)} %bitcast.16.own_ref), channel_id=1, source_target_pairs={{0,1},{1,0},{2,3},{3,2},{4,5},{5,4},{6,7},{7,6},{8,9},{9,8},{10,11... | collective-permute-start | bytes 6291464 | tf_op jit(solution)/shard_map/ppermute | solution.py:224
  95.3 1.4 down_kernel.1
  96.7 4.5 %all-to-all-start.2 = ((bf16[16,32,1024]{2,1,0:T(8,128)(2,1)}), bf16[16,32,1024]{2,1,0:T(8,128)(2,1)S(1)}, u32[]{:S(2)}, u32[]{:S(2)}) async-start(bf16[16,32,1024]{2,1,0:T(8,128)(2,1)} %bitcast.11), calls=%async_computation.2 | async-start | bytes 2097152 | tf_op jit(solution)/shard_map/all_to_all | solution.py:229
  101.4 17.3 %all-to-all-done.2 = bf16[16,32,1024]{2,1,0:T(8,128)(2,1)S(1)} async-done(((bf16[16,32,1024]{2,1,0:T(8,128)(2,1)}), bf16[16,32,1024]{2,1,0:T(8,128)(2,1)S(1)}, u32[]{:S(2)}, u32[]{:S(2)}) %all-to-all-start.2) | async-done | bytes 1048608 | tf_op jit(solution)/shard_map/all_to_all | solution.py:229
  118.7 1.6 %mix_kernel.1 = bf16[16,32,128]{2,1,0:T(8,128)(2,1)} custom-call(s32[2,128]{1,0:T(2,128)S(1)} %pad_add_fusion.routes_ref, f32[2,128]{1,0:T(2,128)S(1)} %pad_maximum_fusion.gates_ref, bf16[2,256,1024]{2,1,0:T(8,128)(2,1)S(1)} %bitcast.34), custom_call_target="tpu_custom_call" | custom-call | flops 400000000 | bytes 1000000 | tf_op jit(solution)/shard_map/mix_kernel/pallas_call | solution.py:41
  120.3 18.1 %all-to-all-start.3 = ((bf16[16,32,128]{2,1,0:T(8,128)(2,1)}), bf16[16,32,128]{2,1,0:T(8,128)(2,1)S(1)}, u32[]{:S(2)}, u32[]{:S(2)}) async-start(bf16[16,32,128]{2,1,0:T(8,128)(2,1)} %mix_kernel.1), calls=%async_computation.3 | async-start | bytes 262144 | tf_op jit(solution)/shard_map/all_to_all | solution.py:285
  138.4 6.8 %back_kernel.1 = (bf16[112,4096]{1,0:T(8,128)(2,1)}, bf16[112,512]{1,0:T(8,128)(2,1)}, bf16[112,512]{1,0:T(8,128)(2,1)}) custom-call(s32[1]{0:T(128)} %bitcast.5.me_ref, bf16[2,512,1024]{2,1,0:T(8,128)(2,1)} %bitcast.16.own_ref, bf16[2,512,1024]{2,1,0:T(8,128)(2,1)} %collective-permute-done.2.other_ref, ...), custom_call_target="tpu_custom_call" | custom-call | flops 1500000000 | bytes 8000000 | tf_op jit(solution)/shard_map/back_kernel/pallas_call | solution.py:291
  145.2 5.2 %all-to-all-done.3.got_ref = bf16[16,32,128]{2,1,0:T(8,128)(2,1)S(1)} async-done(((bf16[16,32,128]{2,1,0:T(8,128)(2,1)}), bf16[16,32,128]{2,1,0:T(8,128)(2,1)S(1)}, u32[]{:S(2)}, u32[]{:S(2)}) %all-to-all-start.3) | async-done | bytes 131104 | tf_op jit(solution)/shard_map/all_to_all | solution.py:285
  (23 shorter events, 3.2 us)
Async XLA Ops:
  0.6 0.7 copy-start
  1.3 0.7 copy-start.1
  3.0 42.1 %copy-start.2 = (s32[128,2]{0,1:T(2,128)S(1)}, s32[128,2]{0,1:T(2,128)}, u32[]{:S(2)}) copy-start(s32[128,2]{0,1:T(2,128)} %param.18) | copy-start | bytes 3076
  3.0 42.1 %copy-start.3 = (f32[128,2]{0,1:T(2,128)S(1)}, f32[128,2]{0,1:T(2,128)}, u32[]{:S(2)}) copy-start(f32[128,2]{0,1:T(2,128)} %param.19) | copy-start | bytes 3076
  3.0 33.9 %all-to-all-start = ((bf16[16,96,128]{2,1,0:T(8,128)(2,1)}), bf16[16,96,128]{2,1,0:T(8,128)(2,1)S(1)}, u32[]{:S(2)}, u32[]{:S(2)}) async-start(bf16[16,96,128]{2,1,0:T(8,128)(2,1)} %pack_kernel.1), calls=%async_computation | async-start | bytes 786432 | tf_op jit(solution)/shard_map/all_to_all | solution.py:254
  38.3 19.3 %all-to-all-start.1 = ((bf16[16,32,1024]{2,1,0:T(8,128)(2,1)}), bf16[16,32,1024]{2,1,0:T(8,128)(2,1)S(1)}, u32[]{:S(2)}, u32[]{:S(2)}) async-start(bf16[16,32,1024]{2,1,0:T(8,128)(2,1)} %bitcast.3), calls=%async_computation.1 | async-start | bytes 2097152 | tf_op jit(solution)/shard_map/all_to_all | solution.py:229
  57.6 26.3 %all-to-all-start.4 = ((bf16[16,64,1024]{2,1,0:T(8,128)(2,1)}), bf16[16,64,1024]{2,1,0:T(8,128)(2,1)}, u32[]{:S(2)}, u32[]{:S(2)}) async-start(bf16[16,64,1024]{2,1,0:T(8,128)(2,1)} %bitcast.15), calls=%async_computation.4 | async-start | bytes 4194304 | tf_op jit(solution)/shard_map/all_to_all | solution.py:229
  62.0 15.7 %collective-permute-start = (bf16[2,256,1024]{2,1,0:T(8,128)(2,1)S(1)}, bf16[2,256,1024]{2,1,0:T(8,128)(2,1)S(1)}, u32[]{:S(2)}, u32[]{:S(2)}) collective-permute-start(bf16[2,256,1024]{2,1,0:T(8,128)(2,1)S(1)} %bitcast.32), channel_id=1, source_target_pairs={{0,1},{1,0},{2,3},{3,2},{4,5},{5,4},{6,7},{7,6},{8,9},{9,8},{10,11... | collective-permute-start | bytes 3145736 | tf_op jit(solution)/shard_map/ppermute | solution.py:224
  71.7 1.2 copy-start.4
  72.8 1.2 copy-start.5
  74.0 1.2 copy-start.6
  80.3 15.0 %collective-permute-start.1 = (bf16[2,256,1024]{2,1,0:T(8,128)(2,1)}, bf16[2,256,1024]{2,1,0:T(8,128)(2,1)S(1)}, u32[]{:S(2)}, u32[]{:S(2)}) collective-permute-start(bf16[2,256,1024]{2,1,0:T(8,128)(2,1)} %get-tuple-element.14), channel_id=1, source_target_pairs={{0,1},{1,0},{2,3},{3,2},{4,5},{5,4},{6,7},{7,6},{8,9},{9,8},{10,11... | collective-permute-start | bytes 3145736 | tf_op jit(solution)/shard_map/ppermute | solution.py:224
  83.9 54.4 %collective-permute-start.2 = (bf16[2,512,1024]{2,1,0:T(8,128)(2,1)}, bf16[2,512,1024]{2,1,0:T(8,128)(2,1)}, u32[]{:S(2)}, u32[]{:S(2)}) collective-permute-start(bf16[2,512,1024]{2,1,0:T(8,128)(2,1)} %bitcast.16.own_ref), channel_id=1, source_target_pairs={{0,1},{1,0},{2,3},{3,2},{4,5},{5,4},{6,7},{7,6},{8,9},{9,8},{10,11... | collective-permute-start | bytes 6291464 | tf_op jit(solution)/shard_map/ppermute | solution.py:224
  95.3 6.0 %copy-start.9 = (f32[64,2]{0,1:T(2,128)S(1)}, f32[64,2]{0,1:T(2,128)}, u32[]{:S(2)}) copy-start(f32[64,2]{0,1:T(2,128)} %param.13) | copy-start | bytes 1540
  96.7 41.7 %copy-start.7 = (bf16[1,512,112]{1,2,0:T(8,128)(2,1)S(1)}, bf16[1,512,112]{1,2,0:T(8,128)(2,1)}, u32[]{:S(2)}) copy-start(bf16[1,512,112]{1,2,0:T(8,128)(2,1)} %param.20) | copy-start | bytes 344068
  96.7 41.7 %copy-start.8 = (bf16[1,512,112]{1,2,0:T(8,128)(2,1)S(1)}, bf16[1,512,112]{1,2,0:T(8,128)(2,1)}, u32[]{:S(2)}) copy-start(bf16[1,512,112]{1,2,0:T(8,128)(2,1)} %param.21) | copy-start | bytes 344068
  96.7 22.0 %all-to-all-start.2 = ((bf16[16,32,1024]{2,1,0:T(8,128)(2,1)}), bf16[16,32,1024]{2,1,0:T(8,128)(2,1)S(1)}, u32[]{:S(2)}, u32[]{:S(2)}) async-start(bf16[16,32,1024]{2,1,0:T(8,128)(2,1)} %bitcast.11), calls=%async_computation.2 | async-start | bytes 2097152 | tf_op jit(solution)/shard_map/all_to_all | solution.py:229
  120.3 30.1 %all-to-all-start.3 = ((bf16[16,32,128]{2,1,0:T(8,128)(2,1)}), bf16[16,32,128]{2,1,0:T(8,128)(2,1)S(1)}, u32[]{:S(2)}, u32[]{:S(2)}) async-start(bf16[16,32,128]{2,1,0:T(8,128)(2,1)} %mix_kernel.1), calls=%async_computation.3 | async-start | bytes 262144 | tf_op jit(solution)/shard_map/all_to_all | solution.py:285

commit v2 on v1

--- a/solution.py
+++ b/solution.py
@@ -14,6 +14,7 @@
 DP = ("dp_0", "dp_1", "dp_2")
 Z = "dp_0"
 CORE = "dp_2"
+XH = "dp_1"
 PLANE = ("dp_1", "expert_0", "expert_1")
 F = 32
 BF = jnp.bfloat16
@@ -44,7 +45,7 @@
         in_specs=[smem] * scalars + [vmem] * (len(args) - scalars),
         out_specs=tuple(vmem for _ in outs) if many else vmem,
         cost_estimate=pl.CostEstimate(flops=flops, bytes_accessed=moved, transcendentals=0),
-        compiler_params=pltpu.CompilerParams(vmem_limit_bytes=40 * MIB),
+        compiler_params=pltpu.CompilerParams(vmem_limit_bytes=16 * MIB),
         name=body.__name__,
     )(*args)
 
@@ -123,19 +124,20 @@
             out_ref[xh, :, h * width : (h + 1) * width] = block
 
 
-def rows_old_kernel(routes_ref, gates_ref, got_ref, out_ref):
+def rows_old_kernel(me_ref, routes_ref, gates_ref, got_ref, other_ref, out_ref):
     routes, gates = routes_ref[...], gates_ref[...]
-    rows, toks = out_ref.shape[1], routes.shape[1]
-    hit, first, second = placed(routes, rows, CAP_A, toks)
+    experts, _, slots, width = out_ref.shape
+    toks = routes.shape[1]
+    hit, first, second = placed(routes, experts * slots, slots, toks)
     weight = jnp.where(first, gates[0:1, :], 0.0) + jnp.where(second, gates[1:2, :], 0.0)
     weight = jnp.sum(jnp.where(hit, weight, 0.0), axis=1, keepdims=True)
     picks = jnp.where(hit, 1.0, 0.0).astype(BF)
-    for h in range(2):
-        g = got_ref[:, F * (1 + h) : F * (2 + h), :].reshape(-1, toks)
-        block = (dot_last(picks, g) * weight).astype(BF)
-        width = block.shape[1]
-        for xh in range(2):
-            out_ref[xh, :, h * width : (h + 1) * width] = block
+    mine = me_ref[1]
+    for xh, ref, base in ((mine, got_ref, F), (1 - mine, other_ref, 0)):
+        for h in range(2):
+            g = ref[:, base + F * h : base + F * (1 + h), :].reshape(-1, toks)
+            block = (dot_last(picks, g) * weight).astype(BF).reshape(experts, slots, -1)
+            out_ref[:, xh, :, h * (width // 2) : (h + 1) * (width // 2)] = block
 
 
 def up_kernel(own_ref, other_ref, gu_ref, dn_ref, hidden_ref, out_ref):
@@ -190,12 +192,16 @@
     out_ref[...] = jnp.concatenate([turned[:toks], turned[toks:]], axis=1).astype(BF)
 
 
+def rows_of(ref, xh):
+    return ref[:, xh].reshape(-1, ref.shape[3])
+
+
 def back_kernel(me_ref, own_ref, other_ref, dn_ref, gate_ref, up_ref, down_ref, dg_ref, du_ref, held):
     total = None
     refs = (own_ref, other_ref)
     for o, ref in enumerate(refs):
         for xh in range(2):
-            term = dot_last(dn_ref[o, xh], ref[xh])
+            term = dot_last(dn_ref[o, xh], rows_of(ref, xh))
             total = term if total is None else total + term
     gate, up = gate_ref[...].astype(F32), up_ref[...].astype(F32)
     grad = total[: gate.shape[0]]
@@ -206,7 +212,7 @@
     hidden = (active * up).astype(BF)
     for o, ref in enumerate(refs):
         for xh in range(2):
-            held[o, xh] = dot(hidden, ref[xh]).astype(BF)
+            held[o, xh] = dot(hidden, rows_of(ref, xh)).astype(BF)
     order = lane_order(me_ref[0])
     for xh in range(2):
         for zq in range(4):
@@ -242,7 +248,7 @@
     pre_gate,
     pre_up,
 ):
-    me = lax.axis_index(CORE).astype(jnp.int32).reshape(1)
+    me = jnp.stack([lax.axis_index(CORE), lax.axis_index(XH)]).astype(jnp.int32)
     experts = lax.axis_size(EXPERT)
     rows_new, rows_old = experts * CAP_B, experts * CAP_A
     hidden_units = w_gate.shape[2]
@@ -264,6 +270,8 @@
         moved=6 * 10**6,
     )
 
+    got, gate_up, down = lax.optimization_barrier((got, gate_up, down))
+
     own = over_plane(call(rows_new_kernel, shape(2, rows_new, 1024), routes_b, got))
     other = other_core(own)
     hidden, partial = call(
@@ -285,7 +293,18 @@
     mixed = lax.all_to_all(mixed, Z, 0, 0, tiled=True)
     mixed = call(total_kernel, shape(*x_new.shape), mixed)
 
-    own_a = over_plane(call(rows_old_kernel, shape(2, rows_old, 1024), routes_a, gates_a, got))
+    far = lax.ppermute(got[:, F:], XH, [(0, 1), (1, 0)])
+    rows_a = call(
+        rows_old_kernel,
+        shape(experts, 2, CAP_A, 1024),
+        me,
+        routes_a,
+        gates_a,
+        got,
+        far,
+        scalars=1,
+    )
+    own_a = lax.all_to_all(rows_a, EXPERT, 0, 0, tiled=True)
     other_a = other_core(own_a)
     vmem = pl.BlockSpec(memory_space=pltpu.VMEM)
     weight_grad, gate_grad, up_grad = pl.pallas_call(
@@ -301,7 +320,7 @@
         cost_estimate=pl.CostEstimate(
             flops=15 * 10**8, bytes_accessed=8 * 10**6, transcendentals=0
         ),
-        compiler_params=pltpu.CompilerParams(vmem_limit_bytes=40 * MIB),
+        compiler_params=pltpu.CompilerParams(vmem_limit_bytes=16 * MIB),
         name="back_kernel",
     )(me, own_a, other_a, down, pre_gate[0].T, pre_up[0].T)
     return (mixed, weight_grad[None], gate_grad.T[None], up_grad.T[None])

time: 153 us -> 154 us (level)
  waiting for transfers between devices: 52 us -> 47.3 us
  local copies, waits for them, and re-layouts: 4.98 us -> 7.89 us
    all_to_all x3 -> x2, waiting for transfers between devices: 29.7 us -> 18.2 us  [over_plane(): return lax.all_to_all(peers, PLANE, 0, 0, tiled=True).reshape(rows.shape)]
    ppermute x0 -> x1, waiting for transfers between devices: none -> 9.74 us  [per_device(): far = lax.ppermute(got[:, F:], XH, [(0, 1), (1, 0)])]
    all_to_all x1, waiting for transfers between devices: 17.2 us -> 9.48 us  [per_device(): got = lax.all_to_all(packed, Z, 0, 0, tiled=True)]
    all_to_all x3 -> x2, starting transfers between devices: 15.7 us -> 10.5 us  [over_plane(): return lax.all_to_all(peers, PLANE, 0, 0, tiled=True).reshape(rows.shape)]
    ppermute x0 -> x1, starting transfers between devices: none -> 4.78 us  [per_device(): far = lax.ppermute(got[:, F:], XH, [(0, 1), (1, 0)])]
    all_to_all x0 -> x1, starting transfers between devices: none -> 4.36 us  [per_device(): own_a = lax.all_to_all(rows_a, EXPERT, 0, 0, tiled=True)]
    unnamed x20 -> x24, local copies, waits for them, and re-layouts: 4.98 us -> 7.87 us
    all_to_all x0 -> x1, waiting for transfers between devices: none -> 2.36 us  [per_device(): own_a = lax.all_to_all(rows_a, EXPERT, 0, 0, tiled=True)]
  transfers between devices with their start and end apart: 8 -> 9, of which waited for: 5 -> 6; matrix products, arithmetic and copies ran while one was open for 1% -> 1% of each run, Pallas kernels for 11% -> 11%
where the time goes in v2:
time: 154 us; the launch traced here: 151 us
  starting transfers between devices  73.9 us (48%)
  waiting for transfers between devices  47.3 us (31%)
  Pallas kernels  20 us (13%)
  local copies, waits for them, and re-layouts  7.89 us (5%)
    ppermute x3, starting transfers between devices, other_core(): return lax.ppermute(array, CORE, [(0, 1), (1, 0)])  22.1 us
    all_to_all x2, waiting for transfers between devices, over_plane(): return lax.all_to_all(peers, PLANE, 0, 0, tiled=True).reshape(rows.shape)  18.2 us
    all_to_all x1, starting transfers between devices, per_device(): mixed = lax.all_to_all(mixed, Z, 0, 0, tiled=True)  16.4 us
    all_to_all x1, starting transfers between devices, per_device(): got = lax.all_to_all(packed, Z, 0, 0, tiled=True)  15.7 us
    pallas_call x8, Pallas kernels, call(): pl.pallas_call(body, out_shape=outs, in_specs=[smem] * scalars + [vmem] *...  13.2 us
    all_to_all x2, starting transfers between devices, over_plane(): return lax.all_to_all(peers, PLANE, 0, 0, tiled=True).reshape(rows.shape)  10.5 us
    ppermute x1, waiting for transfers between devices, per_device(): far = lax.ppermute(got[:, F:], XH, [(0, 1), (1, 0)])  9.74 us
    all_to_all x1, waiting for transfers between devices, per_device(): got = lax.all_to_all(packed, Z, 0, 0, tiled=True)  9.48 us
  transfers between devices with their start and end apart: 9, of which 6 were waited for; matrix products, arithmetic and copies ran while one was open for 1% of the time, Pallas kernels for 11%

profile of v2, /device:TPU:1, one launch (start us, length us, event | category | flops | bytes accessed | tf_op | source)
XLA Modules:
  0.0 150.8 jit_solution(13315182901026574124)
XLA Ops:
  3.0 15.7 %all-to-all-start = ((bf16[16,96,128]{2,1,0:T(8,128)(2,1)}), bf16[16,96,128]{2,1,0:T(8,128)(2,1)S(1)}, u32[]{:S(2)}, u32[]{:S(2)}) async-start(bf16[16,96,128]{2,1,0:T(8,128)(2,1)} %pack_kernel.1), calls=%async_computation | async-start | bytes 786432 | tf_op jit(solution)/shard_map/all_to_all | solution.py:260
  23.2 2.8 %weights_kernel.1 = (bf16[2,2,256,1024]{3,2,1,0:T(8,128)(2,1)S(1)}, bf16[2,2,128,1024]{3,2,1,0:T(8,128)(2,1)S(1)}) custom-call(s32[2]{0:T(128)S(1)} %pad_add_fusion.1.me_ref, bf16[112,4096]{1,0:T(8,128)(2,1)S(1)} %bitcast.37, bf16[112,4096]{1,0:T(8,128)(2,1)S(1)} %bitcast.38, bf16[112,4096]{1,0:T(8,128)(2,1)S(1)} %bitcast.39), custom_call_target="tpu_custom_call" | custom-call | flops 1400000000 | bytes 6000000 | tf_op jit(solution)/shard_map/weights_kernel/pallas_call | solution.py:42
  25.9 1.3 copy-done
  27.2 9.5 %all-to-all-done.got_ref = bf16[16,96,128]{2,1,0:T(8,128)(2,1)S(1)} async-done(((bf16[16,96,128]{2,1,0:T(8,128)(2,1)}), bf16[16,96,128]{2,1,0:T(8,128)(2,1)S(1)}, u32[]{:S(2)}, u32[]{:S(2)}) %all-to-all-start) | async-done | bytes 393248 | tf_op jit(solution)/shard_map/all_to_all | solution.py:260
  36.7 1.4 rows_new_kernel.1
  38.1 6.8 %all-to-all-start.1 = ((bf16[16,32,1024]{2,1,0:T(8,128)(2,1)}), bf16[16,32,1024]{2,1,0:T(8,128)(2,1)S(1)}, u32[]{:S(2)}, u32[]{:S(2)}) async-start(bf16[16,32,1024]{2,1,0:T(8,128)(2,1)} %bitcast.10), calls=%async_computation.1 | async-start | bytes 2097152 | tf_op jit(solution)/shard_map/all_to_all | solution.py:235
  44.9 4.8 %collective-permute-start.2 = (bf16[16,64,128]{2,1,0:T(8,128)(2,1)S(1)}, bf16[16,64,128]{2,1,0:T(8,128)(2,1)S(1)}, u32[]{:S(2)}, u32[]{:S(2)}) collective-permute-start(bf16[16,64,128]{2,1,0:T(8,128)(2,1)S(1)} %slice.3), channel_id=1, source_target_pairs={{0,2},{2,0},{1,3},{3,1},{4,6},{6,4},{5,7},{7,5},{8,10},{10,8},{9,1... | collective-permute-start | bytes 786440 | tf_op jit(solution)/shard_map/ppermute | solution.py:296
  49.7 9.7 %collective-permute-done.2.other_ref = bf16[16,64,128]{2,1,0:T(8,128)(2,1)S(1)} collective-permute-done((bf16[16,64,128]{2,1,0:T(8,128)(2,1)S(1)}, bf16[16,64,128]{2,1,0:T(8,128)(2,1)S(1)}, u32[]{:S(2)}, u32[]{:S(2)}) %collective-permute-start.2) | collective-permute-done | bytes 262176 | tf_op jit(solution)/shard_map/ppermute | solution.py:296
  59.5 2.8 %rows_old_kernel.1 = bf16[8,2,64,1024]{3,2,1,0:T(8,128)(2,1)} custom-call(s32[2]{0:T(128)S(1)} %pad_add_fusion.1.me_ref, s32[2,128]{1,0:T(2,128)S(1)} %bitcast.35, f32[2,128]{1,0:T(2,128)S(1)} %bitcast.36, bf16[16,96,128]{2,1,0:T(8,128)(2,1)S(1)} %all-to-all-done.got_ref, bf16[16,64,128]{2,1,0:T(8,128)(2,1)S(1)} %collective-permute-done.2.other_ref), custom_call_target="tpu_custom_call" | custom-call | flops 10000000 | bytes 1000000 | tf_op jit(solution)/shard_map/rows_old_kernel/pallas_call | solution.py:42
  62.2 4.4 %all-to-all-start.4 = ((bf16[8,2,64,1024]{3,2,1,0:T(8,128)(2,1)}), bf16[8,2,64,1024]{3,2,1,0:T(8,128)(2,1)}, u32[]{:S(2)}, u32[]{:S(2)}) async-start(bf16[8,2,64,1024]{3,2,1,0:T(8,128)(2,1)} %rows_old_kernel.1), calls=%async_computation.4 | async-start | bytes 4194304 | tf_op jit(solution)/shard_map/all_to_all | solution.py:307
  66.6 9.4 %collective-permute-start = (bf16[2,256,1024]{2,1,0:T(8,128)(2,1)S(1)}, bf16[2,256,1024]{2,1,0:T(8,128)(2,1)S(1)}, u32[]{:S(2)}, u32[]{:S(2)}) collective-permute-start(bf16[2,256,1024]{2,1,0:T(8,128)(2,1)S(1)} %bitcast.31), channel_id=1, source_target_pairs={{0,1},{1,0},{2,3},{3,2},{4,5},{5,4},{6,7},{7,6},{8,9},{9,8},{10,11... | collective-permute-start | bytes 3145736 | tf_op jit(solution)/shard_map/ppermute | solution.py:230
  76.0 2.3 %collective-permute-done.other_ref = bf16[2,256,1024]{2,1,0:T(8,128)(2,1)S(1)} collective-permute-done((bf16[2,256,1024]{2,1,0:T(8,128)(2,1)S(1)}, bf16[2,256,1024]{2,1,0:T(8,128)(2,1)S(1)}, u32[]{:S(2)}, u32[]{:S(2)}) %collective-permute-start) | collective-permute-done | bytes 1048608 | tf_op jit(solution)/shard_map/ppermute | solution.py:230
  78.3 1.6 %copy-done.1 = bf16[2,2,256,1024]{3,2,1,0:T(8,128)(2,1)S(1)} copy-done((bf16[2,2,256,1024]{3,2,1,0:T(8,128)(2,1)S(1)}, bf16[2,2,256,1024]{3,2,1,0:T(8,128)(2,1)}, u32[]{:S(2)}) %copy-start.1) | copy-done | bytes 2097176
  79.9 1.6 %up_kernel.1 = (bf16[256,128]{1,0:T(8,128)(2,1)S(1)}, bf16[2,256,1024]{2,1,0:T(8,128)(2,1)S(1)}) custom-call(bf16[2,256,1024]{2,1,0:T(8,128)(2,1)S(1)} %bitcast.32, bf16[2,256,1024]{2,1,0:T(8,128)(2,1)S(1)} %collective-permute-done.other_ref, bf16[2,2,256,1024]{3,2,1,0:T(8,128)(2,1)S(1)} %copy-done.1, bf16[2,2,128,1024]{3,2,1,0:T(8,128)(2,1)S(1)} %get-tuple-element.18.dn_ref), custom_call_target="tpu_custom_call" | custom-call | flops 800000000 | bytes 4000000 | tf_op jit(solution)/shard_map/up_kernel/pallas_call | solution.py:42
  81.5 2.3 %collective-permute-start.1 = (bf16[2,256,1024]{2,1,0:T(8,128)(2,1)S(1)}, bf16[2,256,1024]{2,1,0:T(8,128)(2,1)S(1)}, u32[]{:S(2)}, u32[]{:S(2)}) collective-permute-start(bf16[2,256,1024]{2,1,0:T(8,128)(2,1)S(1)} %get-tuple-element.20), channel_id=1, source_target_pairs={{0,1},{1,0},{2,3},{3,2},{4,5},{5,4},{6,7},{7,6},{8,9},{9,8},{10,11... | collective-permute-start | bytes 3145736 | tf_op jit(solution)/shard_map/ppermute | solution.py:230
  83.8 2.4 %all-to-all-done.4.own_ref = bf16[8,2,64,1024]{3,2,1,0:T(8,128)(2,1)} async-done(((bf16[8,2,64,1024]{3,2,1,0:T(8,128)(2,1)}), bf16[8,2,64,1024]{3,2,1,0:T(8,128)(2,1)}, u32[]{:S(2)}, u32[]{:S(2)}) %all-to-all-start.4) | async-done | bytes 2097184 | tf_op jit(solution)/shard_map/all_to_all | solution.py:307
  86.1 10.4 %collective-permute-start.3 = (bf16[8,2,64,1024]{3,2,1,0:T(8,128)(2,1)}, bf16[8,2,64,1024]{3,2,1,0:T(8,128)(2,1)}, u32[]{:S(2)}, u32[]{:S(2)}) collective-permute-start(bf16[8,2,64,1024]{3,2,1,0:T(8,128)(2,1)} %all-to-all-done.4.own_ref), channel_id=1, source_target_pairs={{0,1},{1,0},{2,3},{3,2},{4,5},{5,4},{6,7},{7,6},{8,9},{9,8},{10,11... | collective-permute-start | bytes 6291464 | tf_op jit(solution)/shard_map/ppermute | solution.py:230
  96.5 1.4 down_kernel.1
  98.0 3.8 %all-to-all-start.2 = ((bf16[16,32,1024]{2,1,0:T(8,128)(2,1)}), bf16[16,32,1024]{2,1,0:T(8,128)(2,1)S(1)}, u32[]{:S(2)}, u32[]{:S(2)}) async-start(bf16[16,32,1024]{2,1,0:T(8,128)(2,1)} %bitcast.12), calls=%async_computation.2 | async-start | bytes 2097152 | tf_op jit(solution)/shard_map/all_to_all | solution.py:235
  101.8 18.2 %all-to-all-done.2 = bf16[16,32,1024]{2,1,0:T(8,128)(2,1)S(1)} async-done(((bf16[16,32,1024]{2,1,0:T(8,128)(2,1)}), bf16[16,32,1024]{2,1,0:T(8,128)(2,1)S(1)}, u32[]{:S(2)}, u32[]{:S(2)}) %all-to-all-start.2) | async-done | bytes 1048608 | tf_op jit(solution)/shard_map/all_to_all | solution.py:235
  120.1 1.6 %mix_kernel.1 = bf16[16,32,128]{2,1,0:T(8,128)(2,1)} custom-call(s32[2,128]{1,0:T(2,128)S(1)} %pad_add_fusion.routes_ref, f32[2,128]{1,0:T(2,128)S(1)} %pad_maximum_fusion.gates_ref, bf16[2,256,1024]{2,1,0:T(8,128)(2,1)S(1)} %bitcast.33), custom_call_target="tpu_custom_call" | custom-call | flops 400000000 | bytes 1000000 | tf_op jit(solution)/shard_map/mix_kernel/pallas_call | solution.py:42
  121.7 16.4 %all-to-all-start.3 = ((bf16[16,32,128]{2,1,0:T(8,128)(2,1)}), bf16[16,32,128]{2,1,0:T(8,128)(2,1)S(1)}, u32[]{:S(2)}, u32[]{:S(2)}) async-start(bf16[16,32,128]{2,1,0:T(8,128)(2,1)} %mix_kernel.1), calls=%async_computation.3 | async-start | bytes 262144 | tf_op jit(solution)/shard_map/all_to_all | solution.py:293
  138.1 6.8 %back_kernel.1 = (bf16[112,4096]{1,0:T(8,128)(2,1)}, bf16[112,512]{1,0:T(8,128)(2,1)}, bf16[112,512]{1,0:T(8,128)(2,1)}) custom-call(s32[2]{0:T(128)S(1)} %pad_add_fusion.1.me_ref, bf16[8,2,64,1024]{3,2,1,0:T(8,128)(2,1)} %all-to-all-done.4.own_ref, bf16[8,2,64,1024]{3,2,1,0:T(8,128)(2,1)} %collective-permute-done.3.other_ref, ...), custom_call_target="tpu_custom_call" | custom-call | flops 1500000000 | bytes 8000000 | tf_op jit(solution)/shard_map/back_kernel/pallas_call | solution.py:310
  144.9 5.2 %all-to-all-done.3.got_ref = bf16[16,32,128]{2,1,0:T(8,128)(2,1)S(1)} async-done(((bf16[16,32,128]{2,1,0:T(8,128)(2,1)}), bf16[16,32,128]{2,1,0:T(8,128)(2,1)S(1)}, u32[]{:S(2)}, u32[]{:S(2)}) %all-to-all-start.3) | async-done | bytes 131104 | tf_op jit(solution)/shard_map/all_to_all | solution.py:293
  (31 shorter events, 7.7 us)
Async XLA Ops:
  0.6 0.7 copy-start.2
  1.3 0.7 copy-start.3
  3.0 33.8 %all-to-all-start = ((bf16[16,96,128]{2,1,0:T(8,128)(2,1)}), bf16[16,96,128]{2,1,0:T(8,128)(2,1)S(1)}, u32[]{:S(2)}, u32[]{:S(2)}) async-start(bf16[16,96,128]{2,1,0:T(8,128)(2,1)} %pack_kernel.1), calls=%async_computation | async-start | bytes 786432 | tf_op jit(solution)/shard_map/all_to_all | solution.py:260
  19.6 1.2 copy-start.6
  20.8 1.2 copy-start.7
  22.0 1.2 copy-start.8
  25.9 1.3 copy-start
  27.2 32.2 %copy-start.4 = (s32[128,2]{0,1:T(2,128)S(1)}, s32[128,2]{0,1:T(2,128)}, u32[]{:S(2)}) copy-start(s32[128,2]{0,1:T(2,128)} %param.18) | copy-start | bytes 3076
  27.2 32.2 %copy-start.5 = (f32[128,2]{0,1:T(2,128)S(1)}, f32[128,2]{0,1:T(2,128)}, u32[]{:S(2)}) copy-start(f32[128,2]{0,1:T(2,128)} %param.19) | copy-start | bytes 3076
  38.1 24.1 %all-to-all-start.1 = ((bf16[16,32,1024]{2,1,0:T(8,128)(2,1)}), bf16[16,32,1024]{2,1,0:T(8,128)(2,1)S(1)}, u32[]{:S(2)}, u32[]{:S(2)}) async-start(bf16[16,32,1024]{2,1,0:T(8,128)(2,1)} %bitcast.10), calls=%async_computation.1 | async-start | bytes 2097152 | tf_op jit(solution)/shard_map/all_to_all | solution.py:235
  44.9 14.5 %collective-permute-start.2 = (bf16[16,64,128]{2,1,0:T(8,128)(2,1)S(1)}, bf16[16,64,128]{2,1,0:T(8,128)(2,1)S(1)}, u32[]{:S(2)}, u32[]{:S(2)}) collective-permute-start(bf16[16,64,128]{2,1,0:T(8,128)(2,1)S(1)} %slice.3), channel_id=1, source_target_pairs={{0,2},{2,0},{1,3},{3,1},{4,6},{6,4},{5,7},{7,5},{8,10},{10,8},{9,1... | collective-permute-start | bytes 786440 | tf_op jit(solution)/shard_map/ppermute | solution.py:296
  62.2 23.9 %all-to-all-start.4 = ((bf16[8,2,64,1024]{3,2,1,0:T(8,128)(2,1)}), bf16[8,2,64,1024]{3,2,1,0:T(8,128)(2,1)}, u32[]{:S(2)}, u32[]{:S(2)}) async-start(bf16[8,2,64,1024]{3,2,1,0:T(8,128)(2,1)} %rows_old_kernel.1), calls=%async_computation.4 | async-start | bytes 4194304 | tf_op jit(solution)/shard_map/all_to_all | solution.py:307
  66.6 11.7 %collective-permute-start = (bf16[2,256,1024]{2,1,0:T(8,128)(2,1)S(1)}, bf16[2,256,1024]{2,1,0:T(8,128)(2,1)S(1)}, u32[]{:S(2)}, u32[]{:S(2)}) collective-permute-start(bf16[2,256,1024]{2,1,0:T(8,128)(2,1)S(1)} %bitcast.31), channel_id=1, source_target_pairs={{0,1},{1,0},{2,3},{3,2},{4,5},{5,4},{6,7},{7,6},{8,9},{9,8},{10,11... | collective-permute-start | bytes 3145736 | tf_op jit(solution)/shard_map/ppermute | solution.py:230
  78.3 1.6 %copy-start.1 = (bf16[2,2,256,1024]{3,2,1,0:T(8,128)(2,1)S(1)}, bf16[2,2,256,1024]{3,2,1,0:T(8,128)(2,1)}, u32[]{:S(2)}) copy-start(bf16[2,2,256,1024]{3,2,1,0:T(8,128)(2,1)} %copy-done) | copy-start | bytes 6291460
  81.5 15.0 %collective-permute-start.1 = (bf16[2,256,1024]{2,1,0:T(8,128)(2,1)S(1)}, bf16[2,256,1024]{2,1,0:T(8,128)(2,1)S(1)}, u32[]{:S(2)}, u32[]{:S(2)}) collective-permute-start(bf16[2,256,1024]{2,1,0:T(8,128)(2,1)S(1)} %get-tuple-element.20), channel_id=1, source_target_pairs={{0,1},{1,0},{2,3},{3,2},{4,5},{5,4},{6,7},{7,6},{8,9},{9,8},{10,11... | collective-permute-start | bytes 3145736 | tf_op jit(solution)/shard_map/ppermute | solution.py:230
  86.1 51.9 %collective-permute-start.3 = (bf16[8,2,64,1024]{3,2,1,0:T(8,128)(2,1)}, bf16[8,2,64,1024]{3,2,1,0:T(8,128)(2,1)}, u32[]{:S(2)}, u32[]{:S(2)}) collective-permute-start(bf16[8,2,64,1024]{3,2,1,0:T(8,128)(2,1)} %all-to-all-done.4.own_ref), channel_id=1, source_target_pairs={{0,1},{1,0},{2,3},{3,2},{4,5},{5,4},{6,7},{7,6},{8,9},{9,8},{10,11... | collective-permute-start | bytes 6291464 | tf_op jit(solution)/shard_map/ppermute | solution.py:230
  96.5 5.2 %copy-start.11 = (f32[64,2]{0,1:T(2,128)S(1)}, f32[64,2]{0,1:T(2,128)}, u32[]{:S(2)}) copy-start(f32[64,2]{0,1:T(2,128)} %param.13) | copy-start | bytes 1540
  98.0 40.1 %copy-start.9 = (bf16[1,512,112]{1,2,0:T(8,128)(2,1)S(1)}, bf16[1,512,112]{1,2,0:T(8,128)(2,1)}, u32[]{:S(2)}) copy-start(bf16[1,512,112]{1,2,0:T(8,128)(2,1)} %param.20) | copy-start | bytes 344068
  98.0 40.1 %copy-start.10 = (bf16[1,512,112]{1,2,0:T(8,128)(2,1)S(1)}, bf16[1,512,112]{1,2,0:T(8,128)(2,1)}, u32[]{:S(2)}) copy-start(bf16[1,512,112]{1,2,0:T(8,128)(2,1)} %param.21) | copy-start | bytes 344068
  98.0 22.1 %all-to-all-start.2 = ((bf16[16,32,1024]{2,1,0:T(8,128)(2,1)}), bf16[16,32,1024]{2,1,0:T(8,128)(2,1)S(1)}, u32[]{:S(2)}, u32[]{:S(2)}) async-start(bf16[16,32,1024]{2,1,0:T(8,128)(2,1)} %bitcast.12), calls=%async_computation.2 | async-start | bytes 2097152 | tf_op jit(solution)/shard_map/all_to_all | solution.py:235
  121.7 28.4 %all-to-all-start.3 = ((bf16[16,32,128]{2,1,0:T(8,128)(2,1)}), bf16[16,32,128]{2,1,0:T(8,128)(2,1)S(1)}, u32[]{:S(2)}, u32[]{:S(2)}) async-start(bf16[16,32,128]{2,1,0:T(8,128)(2,1)} %mix_kernel.1), calls=%async_computation.3 | async-start | bytes 262144 | tf_op jit(solution)/shard_map/all_to_all | solution.py:293

commit v3 on v1

--- a/solution.py
+++ b/solution.py
@@ -14,6 +14,7 @@
 DP = ("dp_0", "dp_1", "dp_2")
 Z = "dp_0"
 CORE = "dp_2"
+XH = "dp_1"
 PLANE = ("dp_1", "expert_0", "expert_1")
 F = 32
 BF = jnp.bfloat16
@@ -44,7 +45,7 @@
         in_specs=[smem] * scalars + [vmem] * (len(args) - scalars),
         out_specs=tuple(vmem for _ in outs) if many else vmem,
         cost_estimate=pl.CostEstimate(flops=flops, bytes_accessed=moved, transcendentals=0),
-        compiler_params=pltpu.CompilerParams(vmem_limit_bytes=40 * MIB),
+        compiler_params=pltpu.CompilerParams(vmem_limit_bytes=16 * MIB),
         name=body.__name__,
     )(*args)
 
@@ -125,25 +126,26 @@
 
 def rows_old_kernel(routes_ref, gates_ref, got_ref, out_ref):
     routes, gates = routes_ref[...], gates_ref[...]
-    rows, toks = out_ref.shape[1], routes.shape[1]
-    hit, first, second = placed(routes, rows, CAP_A, toks)
+    experts, slots, width = out_ref.shape
+    toks = routes.shape[1]
+    hit, first, second = placed(routes, experts * slots, slots, toks)
     weight = jnp.where(first, gates[0:1, :], 0.0) + jnp.where(second, gates[1:2, :], 0.0)
     weight = jnp.sum(jnp.where(hit, weight, 0.0), axis=1, keepdims=True)
     picks = jnp.where(hit, 1.0, 0.0).astype(BF)
     for h in range(2):
         g = got_ref[:, F * (1 + h) : F * (2 + h), :].reshape(-1, toks)
-        block = (dot_last(picks, g) * weight).astype(BF)
-        width = block.shape[1]
-        for xh in range(2):
-            out_ref[xh, :, h * width : (h + 1) * width] = block
-
-
-def up_kernel(own_ref, other_ref, gu_ref, dn_ref, hidden_ref, out_ref):
-    total = None
-    for o, ref in enumerate((own_ref, other_ref)):
-        for xh in range(2):
-            term = dot_last(ref[xh], gu_ref[o, xh])
-            total = term if total is None else total + term
+        block = (dot_last(picks, g) * weight).astype(BF).reshape(experts, slots, -1)
+        out_ref[:, :, h * (width // 2) : (h + 1) * (width // 2)] = block
+
+
+def own_up_kernel(own_ref, gu_ref, out_ref):
+    out_ref[...] = dot_last(own_ref[0], gu_ref[0, 0]) + dot_last(own_ref[1], gu_ref[0, 1])
+
+
+def up_kernel(begun_ref, other_ref, gu_ref, dn_ref, hidden_ref, out_ref):
+    total = begun_ref[...]
+    for xh in range(2):
+        total = total + dot_last(other_ref[xh], gu_ref[1, xh])
     gate, up = total[:, :128], total[:, 128:]
     hidden = (gate / (1.0 + jnp.exp(-gate)) * up).astype(BF)
     hidden_ref[...] = hidden
@@ -190,13 +192,22 @@
     out_ref[...] = jnp.concatenate([turned[:toks], turned[toks:]], axis=1).astype(BF)
 
 
-def back_kernel(me_ref, own_ref, other_ref, dn_ref, gate_ref, up_ref, down_ref, dg_ref, du_ref, held):
+def back_kernel(
+    me_ref, own_ref, far_ref, own_other_ref, far_other_ref, dn_ref, gate_ref, up_ref,
+    down_ref, dg_ref, du_ref, held,
+):
+    mine = me_ref[1]
+    parts = (
+        (0, mine, own_ref),
+        (1, mine, own_other_ref),
+        (0, 1 - mine, far_ref),
+        (1, 1 - mine, far_other_ref),
+    )
+    rows = lambda ref: ref[...].reshape(-1, ref.shape[2])
     total = None
-    refs = (own_ref, other_ref)
-    for o, ref in enumerate(refs):
-        for xh in range(2):
-            term = dot_last(dn_ref[o, xh], ref[xh])
-            total = term if total is None else total + term
+    for o, xh, ref in parts:
+        term = dot_last(dn_ref[o, xh], rows(ref))
+        total = term if total is None else total + term
     gate, up = gate_ref[...].astype(F32), up_ref[...].astype(F32)
     grad = total[: gate.shape[0]]
     sigma = 1.0 / (1.0 + jnp.exp(-gate))
@@ -204,9 +215,8 @@
     dg_ref[...] = (grad * up * sigma * (1.0 + gate * (1.0 - sigma))).astype(BF)
     du_ref[...] = (grad * active).astype(BF)
     hidden = (active * up).astype(BF)
-    for o, ref in enumerate(refs):
-        for xh in range(2):
-            held[o, xh] = dot(hidden, ref[xh]).astype(BF)
+    for o, xh, ref in parts:
+        held[o, xh] = dot(hidden, rows(ref)).astype(BF)
     order = lane_order(me_ref[0])
     for xh in range(2):
         for zq in range(4):
@@ -242,7 +252,7 @@
     pre_gate,
     pre_up,
 ):
-    me = lax.axis_index(CORE).astype(jnp.int32).reshape(1)
+    me = jnp.stack([lax.axis_index(CORE), lax.axis_index(XH)]).astype(jnp.int32)
     experts = lax.axis_size(EXPERT)
     rows_new, rows_old = experts * CAP_B, experts * CAP_A
     hidden_units = w_gate.shape[2]
@@ -264,12 +274,17 @@
         moved=6 * 10**6,
     )
 
+    got, gate_up, down = lax.optimization_barrier((got, gate_up, down))
+
     own = over_plane(call(rows_new_kernel, shape(2, rows_new, 1024), routes_b, got))
+    rows_a = call(rows_old_kernel, shape(experts, CAP_A, 1024), routes_a, gates_a, got)
+    own, rows_a = lax.optimization_barrier((own, rows_a))
     other = other_core(own)
+    begun = call(own_up_kernel, shape(rows_new, 256, dtype=F32), own, gate_up, flops=3 * 10**8)
     hidden, partial = call(
         up_kernel,
         (shape(rows_new, 128), shape(2, rows_new, 1024)),
-        own,
+        begun,
         other,
         gate_up,
         down,
@@ -285,8 +300,9 @@
     mixed = lax.all_to_all(mixed, Z, 0, 0, tiled=True)
     mixed = call(total_kernel, shape(*x_new.shape), mixed)
 
-    own_a = over_plane(call(rows_old_kernel, shape(2, rows_old, 1024), routes_a, gates_a, got))
-    other_a = other_core(own_a)
+    own_a = lax.all_to_all(rows_a, EXPERT, 0, 0, tiled=True)
+    far_a = lax.ppermute(own_a, XH, [(0, 1), (1, 0)])
+    own_other, far_other = other_core(own_a), other_core(far_a)
     vmem = pl.BlockSpec(memory_space=pltpu.VMEM)
     weight_grad, gate_grad, up_grad = pl.pallas_call(
         back_kernel,
@@ -295,15 +311,15 @@
             shape(hidden_units, rows_old),
             shape(hidden_units, rows_old),
         ),
-        in_specs=[pl.BlockSpec(memory_space=pltpu.SMEM)] + [vmem] * 5,
+        in_specs=[pl.BlockSpec(memory_space=pltpu.SMEM)] + [vmem] * 7,
         out_specs=(vmem,) * 3,
         scratch_shapes=[pltpu.VMEM((2, 2, hidden_units, 1024), BF)],
         cost_estimate=pl.CostEstimate(
             flops=15 * 10**8, bytes_accessed=8 * 10**6, transcendentals=0
         ),
-        compiler_params=pltpu.CompilerParams(vmem_limit_bytes=40 * MIB),
+        compiler_params=pltpu.CompilerParams(vmem_limit_bytes=16 * MIB),
         name="back_kernel",
-    )(me, own_a, other_a, down, pre_gate[0].T, pre_up[0].T)
+    )(me, own_a, far_a, own_other, far_other, down, pre_gate[0].T, pre_up[0].T)
     return (mixed, weight_grad[None], gate_grad.T[None], up_grad.T[None])
 
 

time: 153 us -> 155 us (1.013)
  the two profiles are of different devices: /device:TPU:1 before, /device:TPU:26 now
where the time goes in v3:
time: 155 us; the launch traced here: 154 us
  waiting for transfers between devices  67.2 us (43%)
  starting transfers between devices  57.9 us (37%)
  Pallas kernels  20.2 us (13%)
  local copies, waits for them, and re-layouts  6.92 us (4%)
    all_to_all x2, waiting for transfers between devices, over_plane(): return lax.all_to_all(peers, PLANE, 0, 0, tiled=True).reshape(rows.shape)  20 us
    all_to_all x1, waiting for transfers between devices, per_device(): got = lax.all_to_all(packed, Z, 0, 0, tiled=True)  16.4 us
    ppermute x1, waiting for transfers between devices, per_device(): far_a = lax.ppermute(own_a, XH, [(0, 1), (1, 0)])  16 us
    all_to_all x2, starting transfers between devices, over_plane(): return lax.all_to_all(peers, PLANE, 0, 0, tiled=True).reshape(rows.shape)  15.7 us
    all_to_all x1, starting transfers between devices, per_device(): got = lax.all_to_all(packed, Z, 0, 0, tiled=True)  15.2 us
    pallas_call x9, Pallas kernels, call(): pl.pallas_call(body, out_shape=outs, in_specs=[smem] * scalars + [vmem] *...  13.8 us
    all_to_all x1, starting transfers between devices, per_device(): mixed = lax.all_to_all(mixed, Z, 0, 0, tiled=True)  10.1 us
    all_to_all x1, waiting for transfers between devices, per_device(): mixed = lax.all_to_all(mixed, Z, 0, 0, tiled=True)  8.13 us
  transfers between devices with their start and end apart: 10, of which 6 were waited for; matrix products, arithmetic and copies ran while one was open for 1% of the time, Pallas kernels for 12%

profile of v3, /device:TPU:26, one launch (start us, length us, event | category | flops | bytes accessed | tf_op | source)
XLA Modules:
  0.0 154.1 jit_solution(8309384013339829733)
XLA Ops:
  3.0 15.2 %all-to-all-start = ((bf16[16,96,128]{2,1,0:T(8,128)(2,1)}), bf16[16,96,128]{2,1,0:T(8,128)(2,1)S(1)}, u32[]{:S(2)}, u32[]{:S(2)}) async-start(bf16[16,96,128]{2,1,0:T(8,128)(2,1)} %pack_kernel.1), calls=%async_computation | async-start | bytes 786432 | tf_op jit(solution)/shard_map/all_to_all | solution.py:264
  19.1 1.2 copy-done.6
  20.3 1.2 copy-done.7
  22.6 2.9 %weights_kernel.1 = (bf16[2,2,256,1024]{3,2,1,0:T(8,128)(2,1)S(1)}, bf16[2,2,128,1024]{3,2,1,0:T(8,128)(2,1)S(1)}) custom-call(s32[2]{0:T(128)S(1)} %pad_add_fusion.1.me_ref, bf16[112,4096]{1,0:T(8,128)(2,1)S(1)} %bitcast.36, bf16[112,4096]{1,0:T(8,128)(2,1)S(1)} %bitcast.37, bf16[112,4096]{1,0:T(8,128)(2,1)S(1)} %bitcast.38), custom_call_target="tpu_custom_call" | custom-call | flops 1400000000 | bytes 6000000 | tf_op jit(solution)/shard_map/weights_kernel/pallas_call | solution.py:42
  25.5 16.4 %all-to-all-done.got_ref = bf16[16,96,128]{2,1,0:T(8,128)(2,1)S(1)} async-done(((bf16[16,96,128]{2,1,0:T(8,128)(2,1)}), bf16[16,96,128]{2,1,0:T(8,128)(2,1)S(1)}, u32[]{:S(2)}, u32[]{:S(2)}) %all-to-all-start) | async-done | bytes 393248 | tf_op jit(solution)/shard_map/all_to_all | solution.py:264
  43.3 7.1 %all-to-all-start.1 = ((bf16[16,32,1024]{2,1,0:T(8,128)(2,1)}), bf16[16,32,1024]{2,1,0:T(8,128)(2,1)}, u32[]{:S(2)}, u32[]{:S(2)}) async-start(bf16[16,32,1024]{2,1,0:T(8,128)(2,1)} %bitcast.31), calls=%async_computation.1 | async-start | bytes 2097152 | tf_op jit(solution)/shard_map/all_to_all | solution.py:239
  52.1 9.0 %all-to-all-done.1 = bf16[16,32,1024]{2,1,0:T(8,128)(2,1)} async-done(((bf16[16,32,1024]{2,1,0:T(8,128)(2,1)}), bf16[16,32,1024]{2,1,0:T(8,128)(2,1)}, u32[]{:S(2)}, u32[]{:S(2)}) %all-to-all-start.1) | async-done | bytes 1048608 | tf_op jit(solution)/shard_map/all_to_all | solution.py:239
  61.0 1.9 %collective-permute-start = (bf16[2,256,1024]{2,1,0:T(8,128)(2,1)}, bf16[2,256,1024]{2,1,0:T(8,128)(2,1)}, u32[]{:S(2)}, u32[]{:S(2)}) collective-permute-start(bf16[2,256,1024]{2,1,0:T(8,128)(2,1)} %bitcast.11.own_ref), channel_id=1, source_target_pairs={{0,1},{1,0},{2,3},{3,2},{4,5},{5,4},{6,7},{7,6},{8,9},{9,8},{10,11... | collective-permute-start | bytes 3145736 | tf_op jit(solution)/shard_map/ppermute | solution.py:234
  62.9 7.1 %all-to-all-start.4 = ((bf16[8,64,1024]{2,1,0:T(8,128)(2,1)}), bf16[8,64,1024]{2,1,0:T(8,128)(2,1)}, u32[]{:S(2)}, u32[]{:S(2)}) async-start(bf16[8,64,1024]{2,1,0:T(8,128)(2,1)} %copy-done), calls=%async_computation.4 | async-start | bytes 2097152 | tf_op jit(solution)/shard_map/all_to_all | solution.py:303
  70.0 1.7 %own_up_kernel.1.begun_ref = f32[256,256]{1,0:T(8,128)S(1)} custom-call(bf16[2,256,1024]{2,1,0:T(8,128)(2,1)} %bitcast.11.own_ref, bf16[2,2,256,1024]{3,2,1,0:T(8,128)(2,1)S(1)} %get-tuple-element.20.gu_ref), custom_call_target="tpu_custom_call" | custom-call | flops 300000000 | bytes 1000000 | tf_op jit(solution)/shard_map/own_up_kernel/pallas_call | solution.py:42
  71.7 3.5 %up_kernel.1 = (bf16[256,128]{1,0:T(8,128)(2,1)S(1)}, bf16[2,256,1024]{2,1,0:T(8,128)(2,1)}) custom-call(f32[256,256]{1,0:T(8,128)S(1)} %own_up_kernel.1.begun_ref, bf16[2,256,1024]{2,1,0:T(8,128)(2,1)} %collective-permute-done.other_ref, bf16[2,2,256,1024]{3,2,1,0:T(8,128)(2,1)S(1)} %get-tuple-element.20.gu_ref, ...), custom_call_target="tpu_custom_call" | custom-call | flops 800000000 | bytes 4000000 | tf_op jit(solution)/shard_map/up_kernel/pallas_call | solution.py:42
  75.3 2.1 %collective-permute-start.1 = (bf16[2,256,1024]{2,1,0:T(8,128)(2,1)}, bf16[2,256,1024]{2,1,0:T(8,128)(2,1)S(1)}, u32[]{:S(2)}, u32[]{:S(2)}) collective-permute-start(bf16[2,256,1024]{2,1,0:T(8,128)(2,1)} %get-tuple-element.23), channel_id=1, source_target_pairs={{0,1},{1,0},{2,3},{3,2},{4,5},{5,4},{6,7},{7,6},{8,9},{9,8},{10,11... | collective-permute-start | bytes 3145736 | tf_op jit(solution)/shard_map/ppermute | solution.py:234
  77.4 6.7 %all-to-all-done.4.own_ref = bf16[8,64,1024]{2,1,0:T(8,128)(2,1)} async-done(((bf16[8,64,1024]{2,1,0:T(8,128)(2,1)}), bf16[8,64,1024]{2,1,0:T(8,128)(2,1)}, u32[]{:S(2)}, u32[]{:S(2)}) %all-to-all-start.4) | async-done | bytes 1048608 | tf_op jit(solution)/shard_map/all_to_all | solution.py:303
  84.1 1.9 %collective-permute-start.2 = (bf16[8,64,1024]{2,1,0:T(8,128)(2,1)}, bf16[8,64,1024]{2,1,0:T(8,128)(2,1)}, u32[]{:S(2)}, u32[]{:S(2)}) collective-permute-start(bf16[8,64,1024]{2,1,0:T(8,128)(2,1)} %all-to-all-done.4.own_ref), channel_id=1, source_target_pairs={{0,2},{2,0},{1,3},{3,1},{4,6},{6,4},{5,7},{7,5},{8,10},{10,8},{9,1... | collective-permute-start | bytes 3145736 | tf_op jit(solution)/shard_map/ppermute | solution.py:304
  86.0 1.4 down_kernel.1
  87.4 8.6 %all-to-all-start.2 = ((bf16[16,32,1024]{2,1,0:T(8,128)(2,1)}), bf16[16,32,1024]{2,1,0:T(8,128)(2,1)S(1)}, u32[]{:S(2)}, u32[]{:S(2)}) async-start(bf16[16,32,1024]{2,1,0:T(8,128)(2,1)} %bitcast.14), calls=%async_computation.2 | async-start | bytes 2097152 | tf_op jit(solution)/shard_map/all_to_all | solution.py:239
  96.0 1.9 %collective-permute-start.3 = (bf16[8,64,1024]{2,1,0:T(8,128)(2,1)}, bf16[8,64,1024]{2,1,0:T(8,128)(2,1)S(1)}, u32[]{:S(2)}, u32[]{:S(2)}) collective-permute-start(bf16[8,64,1024]{2,1,0:T(8,128)(2,1)} %all-to-all-done.4.own_ref), channel_id=1, source_target_pairs={{0,1},{1,0},{2,3},{3,2},{4,5},{5,4},{6,7},{7,6},{8,9},{9,8},{10,11... | collective-permute-start | bytes 3145736 | tf_op jit(solution)/shard_map/ppermute | solution.py:234
  97.9 16.0 %collective-permute-done.2.far_ref = bf16[8,64,1024]{2,1,0:T(8,128)(2,1)} collective-permute-done((bf16[8,64,1024]{2,1,0:T(8,128)(2,1)}, bf16[8,64,1024]{2,1,0:T(8,128)(2,1)}, u32[]{:S(2)}, u32[]{:S(2)}) %collective-permute-start.2) | collective-permute-done | bytes 1048608 | tf_op jit(solution)/shard_map/ppermute | solution.py:304
  113.9 1.9 %collective-permute-start.4 = (bf16[8,64,1024]{2,1,0:T(8,128)(2,1)}, bf16[8,64,1024]{2,1,0:T(8,128)(2,1)}, u32[]{:S(2)}, u32[]{:S(2)}) collective-permute-start(bf16[8,64,1024]{2,1,0:T(8,128)(2,1)} %collective-permute-done.2.far_ref), channel_id=1, source_target_pairs={{0,1},{1,0},{2,3},{3,2},{4,5},{5,4},{6,7},{7,6},{8,9},{9,8},{10,11... | collective-permute-start | bytes 3145736 | tf_op jit(solution)/shard_map/ppermute | solution.py:234
  115.9 11.1 %all-to-all-done.2 = bf16[16,32,1024]{2,1,0:T(8,128)(2,1)S(1)} async-done(((bf16[16,32,1024]{2,1,0:T(8,128)(2,1)}), bf16[16,32,1024]{2,1,0:T(8,128)(2,1)S(1)}, u32[]{:S(2)}, u32[]{:S(2)}) %all-to-all-start.2) | async-done | bytes 1048608 | tf_op jit(solution)/shard_map/all_to_all | solution.py:239
  127.0 1.6 %mix_kernel.1 = bf16[16,32,128]{2,1,0:T(8,128)(2,1)} custom-call(s32[2,128]{1,0:T(2,128)S(1)} %pad_add_fusion.routes_ref, f32[2,128]{1,0:T(2,128)S(1)} %pad_maximum_fusion.gates_ref, bf16[2,256,1024]{2,1,0:T(8,128)(2,1)S(1)} %bitcast.32), custom_call_target="tpu_custom_call" | custom-call | flops 400000000 | bytes 1000000 | tf_op jit(solution)/shard_map/mix_kernel/pallas_call | solution.py:42
  128.5 10.1 %all-to-all-start.3 = ((bf16[16,32,128]{2,1,0:T(8,128)(2,1)}), bf16[16,32,128]{2,1,0:T(8,128)(2,1)S(1)}, u32[]{:S(2)}, u32[]{:S(2)}) async-start(bf16[16,32,128]{2,1,0:T(8,128)(2,1)} %mix_kernel.1), calls=%async_computation.3 | async-start | bytes 262144 | tf_op jit(solution)/shard_map/all_to_all | solution.py:300
  138.7 6.5 %back_kernel.1 = (bf16[112,4096]{1,0:T(8,128)(2,1)}, bf16[112,512]{1,0:T(8,128)(2,1)}, bf16[112,512]{1,0:T(8,128)(2,1)}) custom-call(s32[2]{0:T(128)S(1)} %pad_add_fusion.1.me_ref, bf16[8,64,1024]{2,1,0:T(8,128)(2,1)} %all-to-all-done.4.own_ref, bf16[8,64,1024]{2,1,0:T(8,128)(2,1)} %collective-permute-done.2.far_ref, ...), custom_call_target="tpu_custom_call" | custom-call | flops 1500000000 | bytes 8000000 | tf_op jit(solution)/shard_map/back_kernel/pallas_call | solution.py:307
  145.2 8.1 %all-to-all-done.3.got_ref = bf16[16,32,128]{2,1,0:T(8,128)(2,1)S(1)} async-done(((bf16[16,32,128]{2,1,0:T(8,128)(2,1)}), bf16[16,32,128]{2,1,0:T(8,128)(2,1)S(1)}, u32[]{:S(2)}, u32[]{:S(2)}) %all-to-all-start.3) | async-done | bytes 131104 | tf_op jit(solution)/shard_map/all_to_all | solution.py:300
  (33 shorter events, 8.3 us)
Async XLA Ops:
  0.6 0.7 copy-start.2
  1.3 0.7 copy-start.3
  3.0 39.0 %all-to-all-start = ((bf16[16,96,128]{2,1,0:T(8,128)(2,1)}), bf16[16,96,128]{2,1,0:T(8,128)(2,1)S(1)}, u32[]{:S(2)}, u32[]{:S(2)}) async-start(bf16[16,96,128]{2,1,0:T(8,128)(2,1)} %pack_kernel.1), calls=%async_computation | async-start | bytes 786432 | tf_op jit(solution)/shard_map/all_to_all | solution.py:264
  19.1 1.2 copy-start.6
  20.3 1.2 copy-start.7
  21.4 1.2 copy-start.8
  25.5 25.0 %copy-start.4 = (s32[128,2]{0,1:T(2,128)S(1)}, s32[128,2]{0,1:T(2,128)}, u32[]{:S(2)}) copy-start(s32[128,2]{0,1:T(2,128)} %param.18) | copy-start | bytes 3076
  25.5 25.0 %copy-start.5 = (f32[128,2]{0,1:T(2,128)S(1)}, f32[128,2]{0,1:T(2,128)}, u32[]{:S(2)}) copy-start(f32[128,2]{0,1:T(2,128)} %param.19) | copy-start | bytes 3076
  42.4 1.0 copy-start.1
  43.3 17.7 %all-to-all-start.1 = ((bf16[16,32,1024]{2,1,0:T(8,128)(2,1)}), bf16[16,32,1024]{2,1,0:T(8,128)(2,1)}, u32[]{:S(2)}, u32[]{:S(2)}) async-start(bf16[16,32,1024]{2,1,0:T(8,128)(2,1)} %bitcast.31), calls=%async_computation.1 | async-start | bytes 2097152 | tf_op jit(solution)/shard_map/all_to_all | solution.py:239
  51.1 1.0 copy-start
  61.0 10.7 %collective-permute-start = (bf16[2,256,1024]{2,1,0:T(8,128)(2,1)}, bf16[2,256,1024]{2,1,0:T(8,128)(2,1)}, u32[]{:S(2)}, u32[]{:S(2)}) collective-permute-start(bf16[2,256,1024]{2,1,0:T(8,128)(2,1)} %bitcast.11.own_ref), channel_id=1, source_target_pairs={{0,1},{1,0},{2,3},{3,2},{4,5},{5,4},{6,7},{7,6},{8,9},{9,8},{10,11... | collective-permute-start | bytes 3145736 | tf_op jit(solution)/shard_map/ppermute | solution.py:234
  62.9 21.1 %all-to-all-start.4 = ((bf16[8,64,1024]{2,1,0:T(8,128)(2,1)}), bf16[8,64,1024]{2,1,0:T(8,128)(2,1)}, u32[]{:S(2)}, u32[]{:S(2)}) async-start(bf16[8,64,1024]{2,1,0:T(8,128)(2,1)} %copy-done), calls=%async_computation.4 | async-start | bytes 2097152 | tf_op jit(solution)/shard_map/all_to_all | solution.py:303
  75.3 10.7 %collective-permute-start.1 = (bf16[2,256,1024]{2,1,0:T(8,128)(2,1)}, bf16[2,256,1024]{2,1,0:T(8,128)(2,1)S(1)}, u32[]{:S(2)}, u32[]{:S(2)}) collective-permute-start(bf16[2,256,1024]{2,1,0:T(8,128)(2,1)} %get-tuple-element.23), channel_id=1, source_target_pairs={{0,1},{1,0},{2,3},{3,2},{4,5},{5,4},{6,7},{7,6},{8,9},{9,8},{10,11... | collective-permute-start | bytes 3145736 | tf_op jit(solution)/shard_map/ppermute | solution.py:234
  84.1 29.8 %collective-permute-start.2 = (bf16[8,64,1024]{2,1,0:T(8,128)(2,1)}, bf16[8,64,1024]{2,1,0:T(8,128)(2,1)}, u32[]{:S(2)}, u32[]{:S(2)}) collective-permute-start(bf16[8,64,1024]{2,1,0:T(8,128)(2,1)} %all-to-all-done.4.own_ref), channel_id=1, source_target_pairs={{0,2},{2,0},{1,3},{3,1},{4,6},{6,4},{5,7},{7,5},{8,10},{10,8},{9,1... | collective-permute-start | bytes 3145736 | tf_op jit(solution)/shard_map/ppermute | solution.py:304
  86.0 29.8 %copy-start.11 = (f32[64,2]{0,1:T(2,128)S(1)}, f32[64,2]{0,1:T(2,128)}, u32[]{:S(2)}) copy-start(f32[64,2]{0,1:T(2,128)} %param.13) | copy-start | bytes 1540
  87.4 51.3 %copy-start.9 = (bf16[1,512,112]{1,2,0:T(8,128)(2,1)S(1)}, bf16[1,512,112]{1,2,0:T(8,128)(2,1)}, u32[]{:S(2)}) copy-start(bf16[1,512,112]{1,2,0:T(8,128)(2,1)} %param.20) | copy-start | bytes 344068
  87.4 51.3 %copy-start.10 = (bf16[1,512,112]{1,2,0:T(8,128)(2,1)S(1)}, bf16[1,512,112]{1,2,0:T(8,128)(2,1)}, u32[]{:S(2)}) copy-start(bf16[1,512,112]{1,2,0:T(8,128)(2,1)} %param.21) | copy-start | bytes 344068
  87.4 39.6 %all-to-all-start.2 = ((bf16[16,32,1024]{2,1,0:T(8,128)(2,1)}), bf16[16,32,1024]{2,1,0:T(8,128)(2,1)S(1)}, u32[]{:S(2)}, u32[]{:S(2)}) async-start(bf16[16,32,1024]{2,1,0:T(8,128)(2,1)} %bitcast.14), calls=%async_computation.2 | async-start | bytes 2097152 | tf_op jit(solution)/shard_map/all_to_all | solution.py:239
  96.0 42.7 %collective-permute-start.3 = (bf16[8,64,1024]{2,1,0:T(8,128)(2,1)}, bf16[8,64,1024]{2,1,0:T(8,128)(2,1)S(1)}, u32[]{:S(2)}, u32[]{:S(2)}) collective-permute-start(bf16[8,64,1024]{2,1,0:T(8,128)(2,1)} %all-to-all-done.4.own_ref), channel_id=1, source_target_pairs={{0,1},{1,0},{2,3},{3,2},{4,5},{5,4},{6,7},{7,6},{8,9},{9,8},{10,11... | collective-permute-start | bytes 3145736 | tf_op jit(solution)/shard_map/ppermute | solution.py:234
  113.9 24.8 %collective-permute-start.4 = (bf16[8,64,1024]{2,1,0:T(8,128)(2,1)}, bf16[8,64,1024]{2,1,0:T(8,128)(2,1)}, u32[]{:S(2)}, u32[]{:S(2)}) collective-permute-start(bf16[8,64,1024]{2,1,0:T(8,128)(2,1)} %collective-permute-done.2.far_ref), channel_id=1, source_target_pairs={{0,1},{1,0},{2,3},{3,2},{4,5},{5,4},{6,7},{7,6},{8,9},{9,8},{10,11... | collective-permute-start | bytes 3145736 | tf_op jit(solution)/shard_map/ppermute | solution.py:234
  128.5 24.8 %all-to-all-start.3 = ((bf16[16,32,128]{2,1,0:T(8,128)(2,1)}), bf16[16,32,128]{2,1,0:T(8,128)(2,1)S(1)}, u32[]{:S(2)}, u32[]{:S(2)}) async-start(bf16[16,32,128]{2,1,0:T(8,128)(2,1)} %mix_kernel.1), calls=%async_computation.3 | async-start | bytes 262144 | tf_op jit(solution)/shard_map/all_to_all | solution.py:300

commit v4 on v2

--- a/solution.py
+++ b/solution.py
@@ -15,7 +15,8 @@
 Z = "dp_0"
 CORE = "dp_2"
 XH = "dp_1"
-PLANE = ("dp_1", "expert_0", "expert_1")
+PLANE = ("expert_0", "expert_1", "dp_1")
+Z_XH = ("dp_0", "dp_1")
 F = 32
 BF = jnp.bfloat16
 F32 = jnp.float32
@@ -109,78 +110,96 @@
     return named & (before == slot.astype(F32)), first, second
 
 
-def rows_new_kernel(routes_ref, got_ref, out_ref):
-    routes = routes_ref[...]
-    rows = out_ref.shape[1]
+def tables_kernel(
+    routes_b_ref, gates_b_ref, routes_a_ref, gates_a_ref, picks_b_ref, mix_ref, picks_a_ref, weight_a_ref
+):
+    def weights(hit, first, second, gates):
+        named = jnp.where(first, gates[0:1, :], 0.0) + jnp.where(second, gates[1:2, :], 0.0)
+        return jnp.where(hit, named, 0.0)
+
+    routes, gates = routes_b_ref[...], gates_b_ref[...]
     toks = routes.shape[1] // 2
-    hit, _, _ = placed(routes, rows, CAP_B, toks)
+    hit, first, second = placed(routes, picks_b_ref.shape[1], CAP_B, toks)
     lane = iota(hit.shape, 1) // toks
-    x = got_ref[:, 0:F, :].reshape(-1, 2 * toks)
-    width = x.shape[0]
     for h in range(2):
-        picks = jnp.where(hit & (lane == h), 1.0, 0.0).astype(BF)
-        block = dot_last(picks, x).astype(BF)
-        for xh in range(2):
-            out_ref[xh, :, h * width : (h + 1) * width] = block
-
-
-def rows_old_kernel(me_ref, routes_ref, gates_ref, got_ref, other_ref, out_ref):
-    routes, gates = routes_ref[...], gates_ref[...]
+        picks_b_ref[h] = jnp.where(hit & (lane == h), 1.0, 0.0).astype(BF)
+    weight = weights(hit, first, second, gates).T[:toks]
+    high = weight.astype(BF)
+    rest = weight - high.astype(F32)
+    middle = rest.astype(BF)
+    mix_ref[0] = high
+    mix_ref[1] = middle
+    mix_ref[2] = (rest - middle.astype(F32)).astype(BF)
+
+    routes, gates = routes_a_ref[...], gates_a_ref[...]
+    hit, first, second = placed(routes, picks_a_ref.shape[0], CAP_A, routes.shape[1])
+    picks_a_ref[...] = jnp.where(hit, 1.0, 0.0).astype(BF)
+    weight = jnp.sum(weights(hit, first, second, gates), axis=1, keepdims=True)
+    weight_a_ref[...] = jnp.broadcast_to(weight, weight_a_ref.shape)
+
+
+def rows_new_kernel(picks_ref, got_ref, out_ref):
     experts, _, slots, width = out_ref.shape
-    toks = routes.shape[1]
-    hit, first, second = placed(routes, experts * slots, slots, toks)
-    weight = jnp.where(first, gates[0:1, :], 0.0) + jnp.where(second, gates[1:2, :], 0.0)
-    weight = jnp.sum(jnp.where(hit, weight, 0.0), axis=1, keepdims=True)
-    picks = jnp.where(hit, 1.0, 0.0).astype(BF)
+    x = got_ref[:, 0:F, :].reshape(-1, picks_ref.shape[2])
+    for h in range(2):
+        block = dot_last(picks_ref[h], x).astype(BF).reshape(experts, slots, -1)
+        for xh in range(2):
+            out_ref[:, xh, :, h * (width // 2) : (h + 1) * (width // 2)] = block
+
+
+def pick_old(picks_ref, weight_ref, ref, base, h):
+    g = ref[:, base + F * h : base + F * (1 + h), :].reshape(-1, picks_ref.shape[1])
+    return (dot_last(picks_ref[...], g) * weight_ref[:, 0:1]).astype(BF)
+
+
+def near_rows_kernel(picks_ref, weight_ref, got_ref, out_ref):
+    experts, slots, width = out_ref.shape
+    for h in range(2):
+        block = pick_old(picks_ref, weight_ref, got_ref, F, h).reshape(experts, slots, -1)
+        out_ref[:, :, h * (width // 2) : (h + 1) * (width // 2)] = block
+
+
+def far_rows_kernel(me_ref, picks_ref, weight_ref, far_ref, near_ref, out_ref):
+    experts, _, slots, width = out_ref.shape
     mine = me_ref[1]
-    for xh, ref, base in ((mine, got_ref, F), (1 - mine, other_ref, 0)):
-        for h in range(2):
-            g = ref[:, base + F * h : base + F * (1 + h), :].reshape(-1, toks)
-            block = (dot_last(picks, g) * weight).astype(BF).reshape(experts, slots, -1)
-            out_ref[:, xh, :, h * (width // 2) : (h + 1) * (width // 2)] = block
+    out_ref[:, mine] = near_ref[...]
+    for h in range(2):
+        block = pick_old(picks_ref, weight_ref, far_ref, 0, h).reshape(experts, slots, -1)
+        out_ref[:, 1 - mine, :, h * (width // 2) : (h + 1) * (width // 2)] = block
 
 
 def up_kernel(own_ref, other_ref, gu_ref, dn_ref, hidden_ref, out_ref):
     total = None
     for o, ref in enumerate((own_ref, other_ref)):
         for xh in range(2):
-            term = dot_last(ref[xh], gu_ref[o, xh])
+            term = dot_last(rows_of(ref, xh), gu_ref[o, xh])
             total = term if total is None else total + term
     gate, up = total[:, :128], total[:, 128:]
     hidden = (gate / (1.0 + jnp.exp(-gate)) * up).astype(BF)
     hidden_ref[...] = hidden
+    groups, _, slots, width = out_ref.shape
     for xh in range(2):
-        out_ref[xh] = dot(hidden, dn_ref[1, xh]).astype(BF)
+        out_ref[:, xh] = dot(hidden, dn_ref[1, xh]).astype(BF).reshape(groups, slots, width)
 
 
 def down_kernel(hidden_ref, dn_ref, arrived_ref, out_ref):
     hidden = hidden_ref[...]
+    groups, _, slots, width = out_ref.shape
     for xh in range(2):
-        out_ref[xh] = (dot(hidden, dn_ref[0, xh]) + arrived_ref[xh].astype(F32)).astype(BF)
-
-
-def mix_kernel(routes_ref, gates_ref, got_ref, out_ref):
-    routes, gates = routes_ref[...], gates_ref[...]
-    rows, width = got_ref.shape[1], got_ref.shape[2] // 2
-    toks = routes.shape[1] // 2
-    hit, first, second = placed(routes, rows, CAP_B, toks)
-    weight = jnp.where(first, gates[0:1, :], 0.0) + jnp.where(second, gates[1:2, :], 0.0)
-    weight = jnp.where(hit, weight, 0.0).T[:toks]
-    high = weight.astype(BF)
-    rest = weight - high.astype(F32)
-    middle = rest.astype(BF)
-    low = (rest - middle.astype(F32)).astype(BF)
-    halves = []
-    for h in range(2):
-        total = None
-        for xh in range(2):
-            got = got_ref[xh, :, h * width : (h + 1) * width]
-            for part in (high, middle, low):
-                term = dot(part, got)
-                total = term if total is None else total + term
-        halves.append(total)
-    mixed = jnp.concatenate(halves, axis=0).T.astype(BF)
-    out_ref[...] = mixed.reshape(out_ref.shape)
+        total = dot(hidden, dn_ref[0, xh]) + rows_of(arrived_ref, xh).astype(F32)
+        out_ref[:, xh] = total.astype(BF).reshape(groups, slots, width)
+
+
+def mix_kernel(mix_ref, got_ref, out_ref):
+    width = got_ref.shape[3] // 2
+    for xh in range(2):
+        rows = rows_of(got_ref, xh)
+        halves = []
+        for h in range(2):
+            got = rows[:, h * width : (h + 1) * width]
+            halves.append(dot(mix_ref[0], got) + dot(mix_ref[1], got) + dot(mix_ref[2], got))
+        mixed = jnp.concatenate(halves, axis=0).T.astype(BF)
+        out_ref[:, xh] = mixed.reshape(out_ref.shape[0], F, -1)
 
 
 def total_kernel(got_ref, out_ref):
@@ -230,9 +249,9 @@
     return lax.ppermute(array, CORE, [(0, 1), (1, 0)])
 
 
-def over_plane(rows):
-    peers = rows.reshape(16, -1, rows.shape[2])
-    return lax.all_to_all(peers, PLANE, 0, 0, tiled=True).reshape(rows.shape)
+def exchange(array, axes):
+    peers = array.reshape(lax.axis_size(axes), -1, array.shape[-1])
+    return lax.all_to_all(peers, axes, 0, 0, tiled=True).reshape(array.shape)
 
 
 def per_device(
@@ -270,41 +289,46 @@
         moved=6 * 10**6,
     )
 
-    got, gate_up, down = lax.optimization_barrier((got, gate_up, down))
-
-    own = over_plane(call(rows_new_kernel, shape(2, rows_new, 1024), routes_b, got))
-    other = other_core(own)
+    picks_b, mix, picks_a, weight_a = call(
+        tables_kernel,
+        (
+            shape(2, rows_new, 128),
+            shape(3, x_new.shape[0], rows_new),
+            shape(rows_old, 128),
+            shape(rows_old, 128, dtype=F32),
+        ),
+        routes_b,
+        gates_b,
+        routes_a,
+        gates_a,
+    )
+    got, gate_up, down, picks_b, mix, picks_a, weight_a = lax.optimization_barrier(
+        (got, gate_up, down, picks_b, mix, picks_a, weight_a)
+    )
+
+    rows_b = shape(experts, 2, CAP_B, 1024)
+    own = exchange(call(rows_new_kernel, rows_b, picks_b, got), PLANE)
+    far = lax.ppermute(got[:, F:], XH, [(0, 1), (1, 0)])
+    rows_a = shape(experts, 2, CAP_A, 1024)
+    near = call(near_rows_kernel, shape(experts, CAP_A, 1024), picks_a, weight_a, got)
+    begun = call(far_rows_kernel, rows_a, me, picks_a, weight_a, far, near, scalars=1)
+    own, begun = lax.optimization_barrier((own, begun))
+    own_a = lax.all_to_all(begun, EXPERT, 0, 0, tiled=True)
+
     hidden, partial = call(
         up_kernel,
-        (shape(rows_new, 128), shape(2, rows_new, 1024)),
+        (shape(rows_new, 128), rows_b),
         own,
-        other,
+        other_core(own),
         gate_up,
         down,
         flops=8 * 10**8,
         moved=4 * 10**6,
     )
-    summed = call(
-        down_kernel, shape(2, rows_new, 1024), hidden, down, other_core(partial), flops=2 * 10**8
-    )
-    mixed = call(
-        mix_kernel, shape(16, F, 128), routes_b, gates_b, over_plane(summed), flops=4 * 10**8
-    )
-    mixed = lax.all_to_all(mixed, Z, 0, 0, tiled=True)
-    mixed = call(total_kernel, shape(*x_new.shape), mixed)
-
-    far = lax.ppermute(got[:, F:], XH, [(0, 1), (1, 0)])
-    rows_a = call(
-        rows_old_kernel,
-        shape(experts, 2, CAP_A, 1024),
-        me,
-        routes_a,
-        gates_a,
-        got,
-        far,
-        scalars=1,
-    )
-    own_a = lax.all_to_all(rows_a, EXPERT, 0, 0, tiled=True)
+    summed = call(down_kernel, rows_b, hidden, down, other_core(partial), flops=2 * 10**8)
+    own_a, summed = lax.optimization_barrier((own_a, summed))
+    returned = exchange(summed, EXPERT)
+
     other_a = other_core(own_a)
     vmem = pl.BlockSpec(memory_space=pltpu.VMEM)
     weight_grad, gate_grad, up_grad = pl.pallas_call(
@@ -323,6 +347,13 @@
         compiler_params=pltpu.CompilerParams(vmem_limit_bytes=16 * MIB),
         name="back_kernel",
     )(me, own_a, other_a, down, pre_gate[0].T, pre_up[0].T)
+    returned, weight_grad, gate_grad, up_grad = lax.optimization_barrier(
+        (returned, weight_grad, gate_grad, up_grad)
+    )
+
+    mixed = call(mix_kernel, shape(16, 2, F, 128), mix, returned, flops=4 * 10**8)
+    mixed = exchange(mixed.reshape(32, F, 128), Z_XH)
+    mixed = call(total_kernel, shape(*x_new.shape), mixed)
     return (mixed, weight_grad[None], gate_grad.T[None], up_grad.T[None])
 
 

time: 154 us -> 161 us (1.045)
  blocking collectives: 0 us -> 32.5 us
  starting transfers between devices: 73.9 us -> 49.3 us
  waiting for transfers between devices: 47.3 us -> 44.9 us
  local copies, waits for them, and re-layouts: 7.89 us -> 9.91 us
    all_to_all x0 -> x1, blocking collectives: none -> 32.5 us  [exchange(): return lax.all_to_all(peers, axes, 0, 0, tiled=True).reshape(array.shape)]
    all_to_all x4 -> x3, starting transfers between devices: 31.3 us -> 14.7 us  [the longest x2 10.3 us: exchange(): return lax.all_to_all(peers, axes, 0, 0, tiled=True).reshape(array.shape)]
    ppermute x3, starting transfers between devices: 22.1 us -> 14.1 us  [other_core(): return lax.ppermute(array, CORE, [(0, 1), (1, 0)])]
    all_to_all x1, waiting for transfers between devices: 9.48 us -> 6.21 us  [per_device(): got = lax.all_to_all(packed, Z, 0, 0, tiled=True)]
    unnamed x24 -> x26, local copies, waits for them, and re-layouts: 7.87 us -> 9.89 us
    all_to_all x4 -> x3, waiting for transfers between devices: 25.8 us -> 26.5 us  [the longest x1 18 us: per_device(): own_a = lax.all_to_all(begun, EXPERT, 0, 0, tiled=True)]
    pallas_call x8 -> x10, Pallas kernels: 13.2 us -> 12.7 us  [call(): pl.pallas_call(body, out_shape=outs, in_specs=[smem] * scalars + [vmem] *...]
  transfers between devices with their start and end apart: 9 -> 8, of which waited for: 6 -> 6; matrix products, arithmetic and copies ran while one was open for 1% -> 1% of each run, Pallas kernels for 11% -> 10%
where the time goes in v4:
time: 161 us; the launch traced here: 159 us
  starting transfers between devices  49.3 us (31%)
  waiting for transfers between devices  44.9 us (28%)
  blocking collectives  32.5 us (20%)
  Pallas kernels  19.5 us (12%)
  local copies, waits for them, and re-layouts  9.91 us (6%)
  other arithmetic  1.73 us (1%)
    all_to_all x1, blocking collectives, exchange(): return lax.all_to_all(peers, axes, 0, 0, tiled=True).reshape(array.shape)  32.5 us
    all_to_all x1, waiting for transfers between devices, per_device(): own_a = lax.all_to_all(begun, EXPERT, 0, 0, tiled=True)  18 us
    all_to_all x1, starting transfers between devices, per_device(): got = lax.all_to_all(packed, Z, 0, 0, tiled=True)  15.7 us
    ppermute x3, starting transfers between devices, other_core(): return lax.ppermute(array, CORE, [(0, 1), (1, 0)])  14.1 us
    pallas_call x10, Pallas kernels, call(): pl.pallas_call(body, out_shape=outs, in_specs=[smem] * scalars + [vmem] *...  12.7 us
    all_to_all x2, starting transfers between devices, exchange(): return lax.all_to_all(peers, axes, 0, 0, tiled=True).reshape(array.shape)  10.3 us
    unnamed x26, local copies, waits for them, and re-layouts  9.89 us
    ppermute x1, waiting for transfers between devices, per_device(): far = lax.ppermute(got[:, F:], XH, [(0, 1), (1, 0)])  9.09 us
  transfers between devices with their start and end apart: 8, of which 6 were waited for; matrix products, arithmetic and copies ran while one was open for 1% of the time, Pallas kernels for 10%

profile of v4, /device:TPU:1, one launch (start us, length us, event | category | flops | bytes accessed | tf_op | source)
XLA Modules:
  0.0 158.7 jit_solution(2577582336201825770)
XLA Ops:
  3.0 15.7 %all-to-all-start = ((bf16[16,96,128]{2,1,0:T(8,128)(2,1)}), bf16[16,96,128]{2,1,0:T(8,128)(2,1)S(1)}, u32[]{:S(2)}, u32[]{:S(2)}) async-start(bf16[16,96,128]{2,1,0:T(8,128)(2,1)} %pack_kernel.1), calls=%async_computation | async-start | bytes 786432 | tf_op jit(solution)/shard_map/all_to_all | solution.py:279
  22.9 1.2 copy-done.4
  24.1 1.2 copy-done.5
  26.4 2.8 %weights_kernel.1 = (bf16[2,2,256,1024]{3,2,1,0:T(8,128)(2,1)S(1)}, bf16[2,2,128,1024]{3,2,1,0:T(8,128)(2,1)S(1)}) custom-call(s32[2]{0:T(128)S(1)} %pad_add_fusion.1.me_ref, bf16[112,4096]{1,0:T(8,128)(2,1)S(1)} %bitcast.37, bf16[112,4096]{1,0:T(8,128)(2,1)S(1)} %bitcast.38, bf16[112,4096]{1,0:T(8,128)(2,1)S(1)} %bitcast.39), custom_call_target="tpu_custom_call" | custom-call | flops 1400000000 | bytes 6000000 | tf_op jit(solution)/shard_map/weights_kernel/pallas_call | solution.py:43
  29.2 1.3 copy-done
  30.5 6.2 %all-to-all-done.got_ref = bf16[16,96,128]{2,1,0:T(8,128)(2,1)S(1)} async-done(((bf16[16,96,128]{2,1,0:T(8,128)(2,1)}), bf16[16,96,128]{2,1,0:T(8,128)(2,1)S(1)}, u32[]{:S(2)}, u32[]{:S(2)}) %all-to-all-start) | async-done | bytes 393248 | tf_op jit(solution)/shard_map/all_to_all | solution.py:279
  36.7 1.3 rows_new_kernel.1
  38.0 6.8 %all-to-all-start.1 = ((bf16[16,32,1024]{2,1,0:T(8,128)(2,1)}), bf16[16,32,1024]{2,1,0:T(8,128)(2,1)S(1)}, u32[]{:S(2)}, u32[]{:S(2)}) async-start(bf16[16,32,1024]{2,1,0:T(8,128)(2,1)} %bitcast.12), calls=%async_computation.1 | async-start | bytes 2097152 | tf_op jit(solution)/shard_map/all_to_all | solution.py:254
  44.8 4.8 %collective-permute-start = (bf16[16,64,128]{2,1,0:T(8,128)(2,1)S(1)}, bf16[16,64,128]{2,1,0:T(8,128)(2,1)S(1)}, u32[]{:S(2)}, u32[]{:S(2)}) collective-permute-start(bf16[16,64,128]{2,1,0:T(8,128)(2,1)S(1)} %slice.3), channel_id=1, source_target_pairs={{0,2},{2,0},{1,3},{3,1},{4,6},{6,4},{5,7},{7,5},{8,10},{10,8},{9,1... | collective-permute-start | bytes 786440 | tf_op jit(solution)/shard_map/ppermute | solution.py:311
  50.0 9.1 %collective-permute-done.far_ref = bf16[16,64,128]{2,1,0:T(8,128)(2,1)S(1)} collective-permute-done((bf16[16,64,128]{2,1,0:T(8,128)(2,1)S(1)}, bf16[16,64,128]{2,1,0:T(8,128)(2,1)S(1)}, u32[]{:S(2)}, u32[]{:S(2)}) %collective-permute-start) | collective-permute-done | bytes 262176 | tf_op jit(solution)/shard_map/ppermute | solution.py:311
  59.1 2.4 %far_rows_kernel.1 = bf16[8,2,64,1024]{3,2,1,0:T(8,128)(2,1)} custom-call(s32[2]{0:T(128)S(1)} %pad_add_fusion.1.me_ref, bf16[512,128]{1,0:T(8,128)(2,1)S(1)} %get-tuple-element.39.picks_ref, f32[512,128]{1,0:T(8,128)S(1)} %get-tuple-element.40.weight_ref, bf16[16,64,128]{2,1,0:T(8,128)(2,1)S(1)} %collective-permute-done.far_ref, ...), custom_call_target="tpu_custom_call" | custom-call | flops 10000000 | bytes 1000000 | tf_op jit(solution)/shard_map/far_rows_kernel/pallas_call | solution.py:43
  61.5 9.5 %collective-permute-start.1 = (bf16[8,2,32,1024]{3,2,1,0:T(8,128)(2,1)S(1)}, bf16[8,2,32,1024]{3,2,1,0:T(8,128)(2,1)S(1)}, u32[]{:S(2)}, u32[]{:S(2)}) collective-permute-start(bf16[8,2,32,1024]{3,2,1,0:T(8,128)(2,1)S(1)} %bitcast.32), channel_id=1, source_target_pairs={{0,1},{1,0},{2,3},{3,2},{4,5},{5,4},{6,7},{7,6},{8,9},{9,8},{10,11... | collective-permute-start | bytes 3145736 | tf_op jit(solution)/shard_map/ppermute | solution.py:249
  71.0 4.4 %all-to-all-start.2 = ((bf16[8,2,64,1024]{3,2,1,0:T(8,128)(2,1)}), bf16[8,2,64,1024]{3,2,1,0:T(8,128)(2,1)}, u32[]{:S(2)}, u32[]{:S(2)}) async-start(bf16[8,2,64,1024]{3,2,1,0:T(8,128)(2,1)} %far_rows_kernel.1), calls=%async_computation.2 | async-start | bytes 4194304 | tf_op jit(solution)/shard_map/all_to_all | solution.py:316
  75.4 1.6 copy-done.1
  76.9 1.6 %up_kernel.1 = (bf16[256,128]{1,0:T(8,128)(2,1)S(1)}, bf16[8,2,32,1024]{3,2,1,0:T(8,128)(2,1)S(1)}) custom-call(bf16[8,2,32,1024]{3,2,1,0:T(8,128)(2,1)S(1)} %bitcast.33, bf16[8,2,32,1024]{3,2,1,0:T(8,128)(2,1)S(1)} %collective-permute-done.1.other_ref, bf16[2,2,256,1024]{3,2,1,0:T(8,128)(2,1)S(1)} %copy-done.1, ...), custom_call_target="tpu_custom_call" | custom-call | flops 800000000 | bytes 4000000 | tf_op jit(solution)/shard_map/up_kernel/pallas_call | solution.py:43
  78.6 1.9 %collective-permute-start.2 = (bf16[8,2,32,1024]{3,2,1,0:T(8,128)(2,1)S(1)}, bf16[8,2,32,1024]{3,2,1,0:T(8,128)(2,1)S(1)}, u32[]{:S(2)}, u32[]{:S(2)}) collective-permute-start(bf16[8,2,32,1024]{3,2,1,0:T(8,128)(2,1)S(1)} %get-tuple-element.46), channel_id=1, source_target_pairs={{0,1},{1,0},{2,3},{3,2},{4,5},{5,4},{6,7},{7,6},{8,9},{9,8},{10,11... | collective-permute-start | bytes 3145736 | tf_op jit(solution)/shard_map/ppermute | solution.py:249
  80.5 2.6 %collective-permute-done.2.arrived_ref = bf16[8,2,32,1024]{3,2,1,0:T(8,128)(2,1)S(1)} collective-permute-done((bf16[8,2,32,1024]{3,2,1,0:T(8,128)(2,1)S(1)}, bf16[8,2,32,1024]{3,2,1,0:T(8,128)(2,1)S(1)}, u32[]{:S(2)}, u32[]{:S(2)}) %collective-permute-start.2) | collective-permute-done | bytes 1048608 | tf_op jit(solution)/shard_map/ppermute | solution.py:249
  83.1 1.4 down_kernel.1
  84.5 18.0 %all-to-all-done.2.own_ref = bf16[8,2,64,1024]{3,2,1,0:T(8,128)(2,1)} async-done(((bf16[8,2,64,1024]{3,2,1,0:T(8,128)(2,1)}), bf16[8,2,64,1024]{3,2,1,0:T(8,128)(2,1)}, u32[]{:S(2)}, u32[]{:S(2)}) %all-to-all-start.2) | async-done | bytes 2097184 | tf_op jit(solution)/shard_map/all_to_all | solution.py:316
  102.5 2.7 %collective-permute-start.3 = (bf16[8,2,64,1024]{3,2,1,0:T(8,128)(2,1)}, bf16[8,2,64,1024]{3,2,1,0:T(8,128)(2,1)}, u32[]{:S(2)}, u32[]{:S(2)}) collective-permute-start(bf16[8,2,64,1024]{3,2,1,0:T(8,128)(2,1)} %all-to-all-done.2.own_ref), channel_id=1, source_target_pairs={{0,1},{1,0},{2,3},{3,2},{4,5},{5,4},{6,7},{7,6},{8,9},{9,8},{10,11... | collective-permute-start | bytes 6291464 | tf_op jit(solution)/shard_map/ppermute | solution.py:249
  105.2 3.6 %all-to-all-start.3 = ((bf16[8,64,1024]{2,1,0:T(8,128)(2,1)}), bf16[8,64,1024]{2,1,0:T(8,128)(2,1)S(1)}, u32[]{:S(2)}, u32[]{:S(2)}) async-start(bf16[8,64,1024]{2,1,0:T(8,128)(2,1)} %bitcast.14), calls=%async_computation.3 | async-start | bytes 2097152 | tf_op jit(solution)/shard_map/all_to_all | solution.py:254
  109.3 6.8 %back_kernel.1 = (bf16[112,4096]{1,0:T(8,128)(2,1)}, bf16[112,512]{1,0:T(8,128)(2,1)}, bf16[112,512]{1,0:T(8,128)(2,1)}) custom-call(s32[2]{0:T(128)S(1)} %pad_add_fusion.1.me_ref, bf16[8,2,64,1024]{3,2,1,0:T(8,128)(2,1)} %all-to-all-done.2.own_ref, bf16[8,2,64,1024]{3,2,1,0:T(8,128)(2,1)} %collective-permute-done.3.other_ref, ...), custom_call_target="tpu_custom_call" | custom-call | flops 1500000000 | bytes 8000000 | tf_op jit(solution)/shard_map/back_kernel/pallas_call | solution.py:334
  116.1 8.5 %all-to-all-done.3 = bf16[8,64,1024]{2,1,0:T(8,128)(2,1)S(1)} async-done(((bf16[8,64,1024]{2,1,0:T(8,128)(2,1)}), bf16[8,64,1024]{2,1,0:T(8,128)(2,1)S(1)}, u32[]{:S(2)}, u32[]{:S(2)}) %all-to-all-start.3) | async-done | bytes 1048608 | tf_op jit(solution)/shard_map/all_to_all | solution.py:254
  125.3 32.5 %all_to_all.25.got_ref = bf16[32,32,128]{2,1,0:T(8,128)(2,1)S(1)} all-to-all(bf16[32,32,128]{2,1,0:T(8,128)(2,1)S(1)} %bitcast.35), channel_id=1, replica_groups=mesh['expert_0'=4,'expert_1'=2,'dp_0'=16,'dp_1'=2,'dp_2'=2] {'dp_0','dp_1'}, dimensions={0} | all-to-all | bytes 524288 | tf_op jit(solution)/shard_map/all_to_all | solution.py:254
  (34 shorter events, 10.2 us)
Async XLA Ops:
  0.6 0.7 copy-start.2
  1.3 0.7 copy-start.3
  3.0 33.8 %all-to-all-start = ((bf16[16,96,128]{2,1,0:T(8,128)(2,1)}), bf16[16,96,128]{2,1,0:T(8,128)(2,1)S(1)}, u32[]{:S(2)}, u32[]{:S(2)}) async-start(bf16[16,96,128]{2,1,0:T(8,128)(2,1)} %pack_kernel.1), calls=%async_computation | async-start | bytes 786432 | tf_op jit(solution)/shard_map/all_to_all | solution.py:279
  20.4 0.7 copy-start.9
  21.1 0.7 copy-start.10
  22.2 0.7 copy-start.11
  22.9 1.2 copy-start.4
  24.1 1.2 copy-start.5
  25.2 1.2 copy-start.6
  29.2 1.3 copy-start
  38.0 23.5 %all-to-all-start.1 = ((bf16[16,32,1024]{2,1,0:T(8,128)(2,1)}), bf16[16,32,1024]{2,1,0:T(8,128)(2,1)S(1)}, u32[]{:S(2)}, u32[]{:S(2)}) async-start(bf16[16,32,1024]{2,1,0:T(8,128)(2,1)} %bitcast.12), calls=%async_computation.1 | async-start | bytes 2097152 | tf_op jit(solution)/shard_map/all_to_all | solution.py:254
  44.8 14.3 %collective-permute-start = (bf16[16,64,128]{2,1,0:T(8,128)(2,1)S(1)}, bf16[16,64,128]{2,1,0:T(8,128)(2,1)S(1)}, u32[]{:S(2)}, u32[]{:S(2)}) collective-permute-start(bf16[16,64,128]{2,1,0:T(8,128)(2,1)S(1)} %slice.3), channel_id=1, source_target_pairs={{0,2},{2,0},{1,3},{3,1},{4,6},{6,4},{5,7},{7,5},{8,10},{10,8},{9,1... | collective-permute-start | bytes 786440 | tf_op jit(solution)/shard_map/ppermute | solution.py:311
  61.5 13.8 %collective-permute-start.1 = (bf16[8,2,32,1024]{3,2,1,0:T(8,128)(2,1)S(1)}, bf16[8,2,32,1024]{3,2,1,0:T(8,128)(2,1)S(1)}, u32[]{:S(2)}, u32[]{:S(2)}) collective-permute-start(bf16[8,2,32,1024]{3,2,1,0:T(8,128)(2,1)S(1)} %bitcast.32), channel_id=1, source_target_pairs={{0,1},{1,0},{2,3},{3,2},{4,5},{5,4},{6,7},{7,6},{8,9},{9,8},{10,11... | collective-permute-start | bytes 3145736 | tf_op jit(solution)/shard_map/ppermute | solution.py:249
  71.0 31.5 %all-to-all-start.2 = ((bf16[8,2,64,1024]{3,2,1,0:T(8,128)(2,1)}), bf16[8,2,64,1024]{3,2,1,0:T(8,128)(2,1)}, u32[]{:S(2)}, u32[]{:S(2)}) async-start(bf16[8,2,64,1024]{3,2,1,0:T(8,128)(2,1)} %far_rows_kernel.1), calls=%async_computation.2 | async-start | bytes 4194304 | tf_op jit(solution)/shard_map/all_to_all | solution.py:316
  75.3 1.6 %copy-start.1 = (bf16[2,2,256,1024]{3,2,1,0:T(8,128)(2,1)S(1)}, bf16[2,2,256,1024]{3,2,1,0:T(8,128)(2,1)}, u32[]{:S(2)}) copy-start(bf16[2,2,256,1024]{3,2,1,0:T(8,128)(2,1)} %copy-done) | copy-start | bytes 6291460
  78.6 4.6 %collective-permute-start.2 = (bf16[8,2,32,1024]{3,2,1,0:T(8,128)(2,1)S(1)}, bf16[8,2,32,1024]{3,2,1,0:T(8,128)(2,1)S(1)}, u32[]{:S(2)}, u32[]{:S(2)}) collective-permute-start(bf16[8,2,32,1024]{3,2,1,0:T(8,128)(2,1)S(1)} %get-tuple-element.46), channel_id=1, source_target_pairs={{0,1},{1,0},{2,3},{3,2},{4,5},{5,4},{6,7},{7,6},{8,9},{9,8},{10,11... | collective-permute-start | bytes 3145736 | tf_op jit(solution)/shard_map/ppermute | solution.py:249
  83.1 26.2 %copy-start.7 = (bf16[1,512,112]{1,2,0:T(8,128)(2,1)S(1)}, bf16[1,512,112]{1,2,0:T(8,128)(2,1)}, u32[]{:S(2)}) copy-start(bf16[1,512,112]{1,2,0:T(8,128)(2,1)} %param.20) | copy-start | bytes 344068
  83.1 26.2 %copy-start.8 = (bf16[1,512,112]{1,2,0:T(8,128)(2,1)S(1)}, bf16[1,512,112]{1,2,0:T(8,128)(2,1)}, u32[]{:S(2)}) copy-start(bf16[1,512,112]{1,2,0:T(8,128)(2,1)} %param.21) | copy-start | bytes 344068
  102.5 6.8 %collective-permute-start.3 = (bf16[8,2,64,1024]{3,2,1,0:T(8,128)(2,1)}, bf16[8,2,64,1024]{3,2,1,0:T(8,128)(2,1)}, u32[]{:S(2)}, u32[]{:S(2)}) collective-permute-start(bf16[8,2,64,1024]{3,2,1,0:T(8,128)(2,1)} %all-to-all-done.2.own_ref), channel_id=1, source_target_pairs={{0,1},{1,0},{2,3},{3,2},{4,5},{5,4},{6,7},{7,6},{8,9},{9,8},{10,11... | collective-permute-start | bytes 6291464 | tf_op jit(solution)/shard_map/ppermute | solution.py:249
  105.2 19.4 %all-to-all-start.3 = ((bf16[8,64,1024]{2,1,0:T(8,128)(2,1)}), bf16[8,64,1024]{2,1,0:T(8,128)(2,1)S(1)}, u32[]{:S(2)}, u32[]{:S(2)}) async-start(bf16[8,64,1024]{2,1,0:T(8,128)(2,1)} %bitcast.14), calls=%async_computation.3 | async-start | bytes 2097152 | tf_op jit(solution)/shard_map/all_to_all | solution.py:254
  109.3 15.3 %copy-start.12 = (bf16[3,64,256]{2,1,0:T(8,128)(2,1)S(1)}, bf16[3,64,256]{2,1,0:T(8,128)(2,1)}, u32[]{:S(2)}) copy-start(bf16[3,64,256]{2,1,0:T(8,128)(2,1)} %copy-done.11) | copy-start | bytes 294916

commit v5 on v4

--- a/solution.py
+++ b/solution.py
@@ -14,9 +14,7 @@
 DP = ("dp_0", "dp_1", "dp_2")
 Z = "dp_0"
 CORE = "dp_2"
-XH = "dp_1"
 PLANE = ("expert_0", "expert_1", "dp_1")
-Z_XH = ("dp_0", "dp_1")
 F = 32
 BF = jnp.bfloat16
 F32 = jnp.float32
@@ -86,7 +84,15 @@
                         ]
 
 
-def pack_kernel(x_ref, g_ref, out_ref):
+def pack_kernel(x_hbm, g_hbm, out_ref, x_ref, g_ref, sems):
+    copies = [
+        pltpu.make_async_copy(x_hbm, x_ref, sems.at[0]),
+        pltpu.make_async_copy(g_hbm, g_ref, sems.at[1]),
+    ]
+    for copy in copies:
+        copy.start()
+    for copy in copies:
+        copy.wait()
     x = x_ref[...]
     toks, feats = x.shape
     twice = jnp.concatenate([x, x], axis=0)
@@ -147,25 +153,14 @@
             out_ref[:, xh, :, h * (width // 2) : (h + 1) * (width // 2)] = block
 
 
-def pick_old(picks_ref, weight_ref, ref, base, h):
-    g = ref[:, base + F * h : base + F * (1 + h), :].reshape(-1, picks_ref.shape[1])
-    return (dot_last(picks_ref[...], g) * weight_ref[:, 0:1]).astype(BF)
-
-
-def near_rows_kernel(picks_ref, weight_ref, got_ref, out_ref):
-    experts, slots, width = out_ref.shape
+def rows_old_kernel(picks_ref, weight_ref, got_ref, out_ref):
+    experts, _, slots, width = out_ref.shape
     for h in range(2):
-        block = pick_old(picks_ref, weight_ref, got_ref, F, h).reshape(experts, slots, -1)
-        out_ref[:, :, h * (width // 2) : (h + 1) * (width // 2)] = block
-
-
-def far_rows_kernel(me_ref, picks_ref, weight_ref, far_ref, near_ref, out_ref):
-    experts, _, slots, width = out_ref.shape
-    mine = me_ref[1]
-    out_ref[:, mine] = near_ref[...]
-    for h in range(2):
-        block = pick_old(picks_ref, weight_ref, far_ref, 0, h).reshape(experts, slots, -1)
-        out_ref[:, 1 - mine, :, h * (width // 2) : (h + 1) * (width // 2)] = block
+        g = got_ref[:, F * (1 + h) : F * (2 + h), :].reshape(-1, picks_ref.shape[1])
+        block = (dot_last(picks_ref[...], g) * weight_ref[:, 0:1]).astype(BF)
+        block = block.reshape(experts, slots, -1)
+        for xh in range(2):
+            out_ref[:, xh, :, h * (width // 2) : (h + 1) * (width // 2)] = block
 
 
 def up_kernel(own_ref, other_ref, gu_ref, dn_ref, hidden_ref, out_ref):
@@ -192,14 +187,17 @@
 
 def mix_kernel(mix_ref, got_ref, out_ref):
     width = got_ref.shape[3] // 2
-    for xh in range(2):
-        rows = rows_of(got_ref, xh)
-        halves = []
-        for h in range(2):
-            got = rows[:, h * width : (h + 1) * width]
-            halves.append(dot(mix_ref[0], got) + dot(mix_ref[1], got) + dot(mix_ref[2], got))
-        mixed = jnp.concatenate(halves, axis=0).T.astype(BF)
-        out_ref[:, xh] = mixed.reshape(out_ref.shape[0], F, -1)
+    rows = [rows_of(got_ref, xh) for xh in range(2)]
+    halves = []
+    for h in range(2):
+        total = None
+        for xh in range(2):
+            for part in range(3):
+                term = dot(mix_ref[part], rows[xh][:, h * width : (h + 1) * width])
+                total = term if total is None else total + term
+        halves.append(total)
+    mixed = jnp.concatenate(halves, axis=0).T.astype(BF)
+    out_ref[...] = mixed.reshape(out_ref.shape)
 
 
 def total_kernel(got_ref, out_ref):
@@ -215,9 +213,11 @@
     return ref[:, xh].reshape(-1, ref.shape[3])
 
 
-def back_kernel(me_ref, own_ref, other_ref, dn_ref, gate_ref, up_ref, down_ref, dg_ref, du_ref, held):
+def back_kernel(
+    me_ref, own_ref, other_ref, dn_ref, gate_ref, up_ref, down_ref, dg_ref, du_ref, held
+):
+    refs = (own_ref, other_ref)
     total = None
-    refs = (own_ref, other_ref)
     for o, ref in enumerate(refs):
         for xh in range(2):
             term = dot_last(dn_ref[o, xh], rows_of(ref, xh))
@@ -267,7 +267,7 @@
     pre_gate,
     pre_up,
 ):
-    me = jnp.stack([lax.axis_index(CORE), lax.axis_index(XH)]).astype(jnp.int32)
+    me = lax.axis_index(CORE).astype(jnp.int32).reshape(1)
     experts = lax.axis_size(EXPERT)
     rows_new, rows_old = experts * CAP_B, experts * CAP_A
     hidden_units = w_gate.shape[2]
@@ -275,7 +275,19 @@
     routes_b, gates_b = twice(routes_new), twice(gates_new)
     routes_a, gates_a = routes_old.T, gates_old.T
 
-    packed = call(pack_kernel, shape(16, 3 * F, 128), x_new, grad_out.T)
+    packed = pl.pallas_call(
+        pack_kernel,
+        out_shape=shape(16, 3 * F, 128),
+        in_specs=[pl.BlockSpec(memory_space=pltpu.HBM)] * 2,
+        out_specs=pl.BlockSpec(memory_space=pltpu.VMEM),
+        scratch_shapes=[
+            pltpu.VMEM(x_new.shape, BF),
+            pltpu.VMEM(grad_out.shape[::-1], BF),
+            pltpu.SemaphoreType.DMA((2,)),
+        ],
+        compiler_params=pltpu.CompilerParams(vmem_limit_bytes=16 * MIB),
+        name="pack_kernel",
+    )(x_new, grad_out.T)
     got = lax.all_to_all(packed, Z, 0, 0, tiled=True)
     gate_up, down = call(
         weights_kernel,
@@ -308,12 +320,9 @@
 
     rows_b = shape(experts, 2, CAP_B, 1024)
     own = exchange(call(rows_new_kernel, rows_b, picks_b, got), PLANE)
-    far = lax.ppermute(got[:, F:], XH, [(0, 1), (1, 0)])
     rows_a = shape(experts, 2, CAP_A, 1024)
-    near = call(near_rows_kernel, shape(experts, CAP_A, 1024), picks_a, weight_a, got)
-    begun = call(far_rows_kernel, rows_a, me, picks_a, weight_a, far, near, scalars=1)
-    own, begun = lax.optimization_barrier((own, begun))
-    own_a = lax.all_to_all(begun, EXPERT, 0, 0, tiled=True)
+    sent_a = call(rows_old_kernel, rows_a, picks_a, weight_a, got)
+    own_a = exchange(sent_a, PLANE)
 
     hidden, partial = call(
         up_kernel,
@@ -326,8 +335,7 @@
         moved=4 * 10**6,
     )
     summed = call(down_kernel, rows_b, hidden, down, other_core(partial), flops=2 * 10**8)
-    own_a, summed = lax.optimization_barrier((own_a, summed))
-    returned = exchange(summed, EXPERT)
+    returned = exchange(summed, PLANE)
 
     other_a = other_core(own_a)
     vmem = pl.BlockSpec(memory_space=pltpu.VMEM)
@@ -347,12 +355,11 @@
         compiler_params=pltpu.CompilerParams(vmem_limit_bytes=16 * MIB),
         name="back_kernel",
     )(me, own_a, other_a, down, pre_gate[0].T, pre_up[0].T)
-    returned, weight_grad, gate_grad, up_grad = lax.optimization_barrier(
-        (returned, weight_grad, gate_grad, up_grad)
-    )
-
-    mixed = call(mix_kernel, shape(16, 2, F, 128), mix, returned, flops=4 * 10**8)
-    mixed = exchange(mixed.reshape(32, F, 128), Z_XH)
+    mixed = call(mix_kernel, shape(16, F, 128), mix, returned, flops=4 * 10**8)
+    mixed = exchange(mixed, Z)
+    mixed, weight_grad, gate_grad, up_grad = lax.optimization_barrier(
+        (mixed, weight_grad, gate_grad, up_grad)
+    )
     mixed = call(total_kernel, shape(*x_new.shape), mixed)
     return (mixed, weight_grad[None], gate_grad.T[None], up_grad.T[None])
 

time: 161 us -> 145 us (0.901)
  waiting for transfers between devices: 44.9 us -> 25.4 us
  starting transfers between devices: 49.3 us -> 66.3 us
  blocking collectives: 32.5 us -> 20.8 us
    all_to_all x1 -> x0, waiting for transfers between devices: 18 us -> none  [per_device(): own_a = lax.all_to_all(begun, EXPERT, 0, 0, tiled=True)]
    all_to_all x2 -> x3, starting transfers between devices: 10.3 us -> 27.6 us  [exchange(): return lax.all_to_all(peers, axes, 0, 0, tiled=True).reshape(array.shape)]
    all_to_all x1, blocking collectives: 32.5 us -> 20.8 us  [exchange(): return lax.all_to_all(peers, axes, 0, 0, tiled=True).reshape(array.shape)]
    ppermute x1 -> x0, waiting for transfers between devices: 9.09 us -> none  [per_device(): far = lax.ppermute(got[:, F:], XH, [(0, 1), (1, 0)])]
    ppermute x3, starting transfers between devices: 14.1 us -> 22.9 us  [other_core(): return lax.ppermute(array, CORE, [(0, 1), (1, 0)])]
    all_to_all x2 -> x3, waiting for transfers between devices: 8.51 us -> 15.9 us  [exchange(): return lax.all_to_all(peers, axes, 0, 0, tiled=True).reshape(array.shape)]
    ppermute x1 -> x0, starting transfers between devices: 4.78 us -> none  [per_device(): far = lax.ppermute(got[:, F:], XH, [(0, 1), (1, 0)])]
    all_to_all x1 -> x0, starting transfers between devices: 4.35 us -> none  [per_device(): own_a = lax.all_to_all(begun, EXPERT, 0, 0, tiled=True)]
  transfers between devices with their start and end apart: 8 -> 7, of which waited for: 6 -> 5; matrix products, arithmetic and copies ran while one was open for 1% -> 1% of each run, Pallas kernels for 10% -> 10%
where the time goes in v5:
time: 145 us; the launch traced here: 142 us
  starting transfers between devices  66.3 us (46%)
  waiting for transfers between devices  25.4 us (18%)
  blocking collectives  20.8 us (14%)
  Pallas kernels  17.9 us (12%)
  local copies, waits for them, and re-layouts  9.22 us (6%)
  other arithmetic  1.66 us (1%)
    all_to_all x3, starting transfers between devices, exchange(): return lax.all_to_all(peers, axes, 0, 0, tiled=True).reshape(array.shape)  27.6 us
    ppermute x3, starting transfers between devices, other_core(): return lax.ppermute(array, CORE, [(0, 1), (1, 0)])  22.9 us
    all_to_all x1, blocking collectives, exchange(): return lax.all_to_all(peers, axes, 0, 0, tiled=True).reshape(array.shape)  20.8 us
    all_to_all x3, waiting for transfers between devices, exchange(): return lax.all_to_all(peers, axes, 0, 0, tiled=True).reshape(array.shape)  15.9 us
    all_to_all x1, starting transfers between devices, per_device(): got = lax.all_to_all(packed, Z, 0, 0, tiled=True)  15.8 us
    pallas_call x8, Pallas kernels, call(): pl.pallas_call(body, out_shape=outs, in_specs=[smem] * scalars + [vmem] *...  10.2 us
    unnamed x22, local copies, waits for them, and re-layouts  9.22 us
    all_to_all x1, waiting for transfers between devices, per_device(): got = lax.all_to_all(packed, Z, 0, 0, tiled=True)  7.22 us
  transfers between devices with their start and end apart: 7, of which 5 were waited for; matrix products, arithmetic and copies ran while one was open for 1% of the time, Pallas kernels for 10%

profile of v5, /device:TPU:1, one launch (start us, length us, event | category | flops | bytes accessed | tf_op | source)
XLA Modules:
  0.0 142.1 jit_solution(17594187501103995624)
XLA Ops:
  3.0 15.8 %all-to-all-start = ((bf16[16,96,128]{2,1,0:T(8,128)(2,1)}), bf16[16,96,128]{2,1,0:T(8,128)(2,1)S(1)}, u32[]{:S(2)}, u32[]{:S(2)}) async-start(bf16[16,96,128]{2,1,0:T(8,128)(2,1)} %pack_kernel.1), calls=%async_computation | async-start | bytes 786432 | tf_op jit(solution)/shard_map/all_to_all | solution.py:291
  22.2 1.2 copy-done.4
  23.4 1.2 copy-done.5
  24.6 1.2 copy-done.6
  25.8 2.5 %weights_kernel.1 = (bf16[2,2,256,1024]{3,2,1,0:T(8,128)(2,1)S(1)}, bf16[2,2,128,1024]{3,2,1,0:T(8,128)(2,1)S(1)}) custom-call(s32[1]{0:T(128)} %bitcast.1.me_ref, bf16[112,4096]{1,0:T(8,128)(2,1)S(1)} %bitcast.37, bf16[112,4096]{1,0:T(8,128)(2,1)S(1)} %bitcast.38, bf16[112,4096]{1,0:T(8,128)(2,1)S(1)} %bitcast.39), custom_call_target="tpu_custom_call" | custom-call | flops 1400000000 | bytes 6000000 | tf_op jit(solution)/shard_map/weights_kernel/pallas_call | solution.py:41
  28.3 1.3 copy-done
  29.6 7.2 %all-to-all-done.got_ref = bf16[16,96,128]{2,1,0:T(8,128)(2,1)S(1)} async-done(((bf16[16,96,128]{2,1,0:T(8,128)(2,1)}), bf16[16,96,128]{2,1,0:T(8,128)(2,1)S(1)}, u32[]{:S(2)}, u32[]{:S(2)}) %all-to-all-start) | async-done | bytes 393248 | tf_op jit(solution)/shard_map/all_to_all | solution.py:291
  36.8 1.3 rows_new_kernel.1
  38.1 6.8 %all-to-all-start.1 = ((bf16[16,32,1024]{2,1,0:T(8,128)(2,1)}), bf16[16,32,1024]{2,1,0:T(8,128)(2,1)S(1)}, u32[]{:S(2)}, u32[]{:S(2)}) async-start(bf16[16,32,1024]{2,1,0:T(8,128)(2,1)} %bitcast.11), calls=%async_computation.1 | async-start | bytes 2097152 | tf_op jit(solution)/shard_map/all_to_all | solution.py:254
  44.9 1.8 %rows_old_kernel.1 = bf16[8,2,64,1024]{3,2,1,0:T(8,128)(2,1)} custom-call(bf16[512,128]{1,0:T(8,128)(2,1)S(1)} %get-tuple-element.39.picks_ref, f32[512,128]{1,0:T(8,128)S(1)} %get-tuple-element.40.weight_ref, bf16[16,96,128]{2,1,0:T(8,128)(2,1)S(1)} %all-to-all-done.got_ref), custom_call_target="tpu_custom_call" | custom-call | flops 10000000 | bytes 1000000 | tf_op jit(solution)/shard_map/rows_old_kernel/pallas_call | solution.py:41
  46.6 9.0 %all-to-all-done.1 = bf16[16,32,1024]{2,1,0:T(8,128)(2,1)S(1)} async-done(((bf16[16,32,1024]{2,1,0:T(8,128)(2,1)}), bf16[16,32,1024]{2,1,0:T(8,128)(2,1)S(1)}, u32[]{:S(2)}, u32[]{:S(2)}) %all-to-all-start.1) | async-done | bytes 1048608 | tf_op jit(solution)/shard_map/all_to_all | solution.py:254
  55.7 4.4 %all-to-all-start.4 = ((bf16[16,64,1024]{2,1,0:T(8,128)(2,1)}), bf16[16,64,1024]{2,1,0:T(8,128)(2,1)}, u32[]{:S(2)}, u32[]{:S(2)}) async-start(bf16[16,64,1024]{2,1,0:T(8,128)(2,1)} %bitcast.15), calls=%async_computation.4 | async-start | bytes 4194304 | tf_op jit(solution)/shard_map/all_to_all | solution.py:254
  60.1 10.1 %collective-permute-start = (bf16[8,2,32,1024]{3,2,1,0:T(8,128)(2,1)S(1)}, bf16[8,2,32,1024]{3,2,1,0:T(8,128)(2,1)S(1)}, u32[]{:S(2)}, u32[]{:S(2)}) collective-permute-start(bf16[8,2,32,1024]{3,2,1,0:T(8,128)(2,1)S(1)} %bitcast.32), channel_id=1, source_target_pairs={{0,1},{1,0},{2,3},{3,2},{4,5},{5,4},{6,7},{7,6},{8,9},{9,8},{10,11... | collective-permute-start | bytes 3145736 | tf_op jit(solution)/shard_map/ppermute | solution.py:249
  70.2 2.3 %collective-permute-done.other_ref = bf16[8,2,32,1024]{3,2,1,0:T(8,128)(2,1)S(1)} collective-permute-done((bf16[8,2,32,1024]{3,2,1,0:T(8,128)(2,1)S(1)}, bf16[8,2,32,1024]{3,2,1,0:T(8,128)(2,1)S(1)}, u32[]{:S(2)}, u32[]{:S(2)}) %collective-permute-start) | collective-permute-done | bytes 1048608 | tf_op jit(solution)/shard_map/ppermute | solution.py:249
  72.5 1.6 %copy-done.1 = bf16[2,2,256,1024]{3,2,1,0:T(8,128)(2,1)S(1)} copy-done((bf16[2,2,256,1024]{3,2,1,0:T(8,128)(2,1)S(1)}, bf16[2,2,256,1024]{3,2,1,0:T(8,128)(2,1)}, u32[]{:S(2)}) %copy-start.1) | copy-done | bytes 2097176
  74.0 1.6 %up_kernel.1 = (bf16[256,128]{1,0:T(8,128)(2,1)S(1)}, bf16[8,2,32,1024]{3,2,1,0:T(8,128)(2,1)S(1)}) custom-call(bf16[8,2,32,1024]{3,2,1,0:T(8,128)(2,1)S(1)} %bitcast.33, bf16[8,2,32,1024]{3,2,1,0:T(8,128)(2,1)S(1)} %collective-permute-done.other_ref, bf16[2,2,256,1024]{3,2,1,0:T(8,128)(2,1)S(1)} %copy-done.1, ...), custom_call_target="tpu_custom_call" | custom-call | flops 800000000 | bytes 4000000 | tf_op jit(solution)/shard_map/up_kernel/pallas_call | solution.py:41
  75.7 2.3 %collective-permute-start.1 = (bf16[8,2,32,1024]{3,2,1,0:T(8,128)(2,1)S(1)}, bf16[8,2,32,1024]{3,2,1,0:T(8,128)(2,1)S(1)}, u32[]{:S(2)}, u32[]{:S(2)}) collective-permute-start(bf16[8,2,32,1024]{3,2,1,0:T(8,128)(2,1)S(1)} %get-tuple-element.38), channel_id=1, source_target_pairs={{0,1},{1,0},{2,3},{3,2},{4,5},{5,4},{6,7},{7,6},{8,9},{9,8},{10,11... | collective-permute-start | bytes 3145736 | tf_op jit(solution)/shard_map/ppermute | solution.py:249
  77.9 1.7 %all-to-all-done.4 = bf16[16,64,1024]{2,1,0:T(8,128)(2,1)} async-done(((bf16[16,64,1024]{2,1,0:T(8,128)(2,1)}), bf16[16,64,1024]{2,1,0:T(8,128)(2,1)}, u32[]{:S(2)}, u32[]{:S(2)}) %all-to-all-start.4) | async-done | bytes 2097184 | tf_op jit(solution)/shard_map/all_to_all | solution.py:254
  79.6 10.5 %collective-permute-start.2 = (bf16[8,2,64,1024]{3,2,1,0:T(8,128)(2,1)}, bf16[8,2,64,1024]{3,2,1,0:T(8,128)(2,1)}, u32[]{:S(2)}, u32[]{:S(2)}) collective-permute-start(bf16[8,2,64,1024]{3,2,1,0:T(8,128)(2,1)} %bitcast.16.own_ref), channel_id=1, source_target_pairs={{0,1},{1,0},{2,3},{3,2},{4,5},{5,4},{6,7},{7,6},{8,9},{9,8},{10,11... | collective-permute-start | bytes 6291464 | tf_op jit(solution)/shard_map/ppermute | solution.py:249
  90.6 20.8 %all_to_all.25 = bf16[16,32,1024]{2,1,0:T(8,128)(2,1)S(1)} all-to-all(bf16[16,32,1024]{2,1,0:T(8,128)(2,1)S(1)} %bitcast.34), channel_id=1, replica_groups=mesh['expert_0'=4,'expert_1'=2,'dp_0'=16,'dp_1'=2,'dp_2'=2] {'expert_0',..., dimensions={0} | all-to-all | bytes 2097152 | tf_op jit(solution)/shard_map/all_to_all | solution.py:254
  111.4 1.4 mix_kernel.1
  112.8 16.5 %all-to-all-start.3 = ((bf16[16,32,128]{2,1,0:T(8,128)(2,1)}), bf16[16,32,128]{2,1,0:T(8,128)(2,1)S(1)}, u32[]{:S(2)}, u32[]{:S(2)}) async-start(bf16[16,32,128]{2,1,0:T(8,128)(2,1)} %mix_kernel.1), calls=%async_computation.3 | async-start | bytes 262144 | tf_op jit(solution)/shard_map/all_to_all | solution.py:254
  129.3 6.8 %back_kernel.1 = (bf16[112,4096]{1,0:T(8,128)(2,1)}, bf16[112,512]{1,0:T(8,128)(2,1)}, bf16[112,512]{1,0:T(8,128)(2,1)}) custom-call(s32[1]{0:T(128)} %bitcast.1.me_ref, bf16[8,2,64,1024]{3,2,1,0:T(8,128)(2,1)} %bitcast.16.own_ref, bf16[8,2,64,1024]{3,2,1,0:T(8,128)(2,1)} %collective-permute-done.2.other_ref, ...), custom_call_target="tpu_custom_call" | custom-call | flops 1500000000 | bytes 8000000 | tf_op jit(solution)/shard_map/back_kernel/pallas_call | solution.py:342
  136.1 5.2 %all-to-all-done.3.got_ref = bf16[16,32,128]{2,1,0:T(8,128)(2,1)S(1)} async-done(((bf16[16,32,128]{2,1,0:T(8,128)(2,1)}), bf16[16,32,128]{2,1,0:T(8,128)(2,1)S(1)}, u32[]{:S(2)}, u32[]{:S(2)}) %all-to-all-start.3) | async-done | bytes 131104 | tf_op jit(solution)/shard_map/all_to_all | solution.py:254
  (25 shorter events, 7.0 us)
Async XLA Ops:
  0.6 0.7 copy-start.2
  1.3 0.7 copy-start.3
  3.0 33.8 %all-to-all-start = ((bf16[16,96,128]{2,1,0:T(8,128)(2,1)}), bf16[16,96,128]{2,1,0:T(8,128)(2,1)S(1)}, u32[]{:S(2)}, u32[]{:S(2)}) async-start(bf16[16,96,128]{2,1,0:T(8,128)(2,1)} %pack_kernel.1), calls=%async_computation | async-start | bytes 786432 | tf_op jit(solution)/shard_map/all_to_all | solution.py:291
  20.4 0.7 copy-start.9
  21.1 0.7 copy-start.10
  22.2 1.2 copy-start.4
  23.4 1.2 copy-start.5
  24.6 1.2 copy-start.6
  28.3 1.3 copy-start
  38.1 17.6 %all-to-all-start.1 = ((bf16[16,32,1024]{2,1,0:T(8,128)(2,1)}), bf16[16,32,1024]{2,1,0:T(8,128)(2,1)S(1)}, u32[]{:S(2)}, u32[]{:S(2)}) async-start(bf16[16,32,1024]{2,1,0:T(8,128)(2,1)} %bitcast.11), calls=%async_computation.1 | async-start | bytes 2097152 | tf_op jit(solution)/shard_map/all_to_all | solution.py:254
  55.7 24.0 %all-to-all-start.4 = ((bf16[16,64,1024]{2,1,0:T(8,128)(2,1)}), bf16[16,64,1024]{2,1,0:T(8,128)(2,1)}, u32[]{:S(2)}, u32[]{:S(2)}) async-start(bf16[16,64,1024]{2,1,0:T(8,128)(2,1)} %bitcast.15), calls=%async_computation.4 | async-start | bytes 4194304 | tf_op jit(solution)/shard_map/all_to_all | solution.py:254
  60.1 12.3 %collective-permute-start = (bf16[8,2,32,1024]{3,2,1,0:T(8,128)(2,1)S(1)}, bf16[8,2,32,1024]{3,2,1,0:T(8,128)(2,1)S(1)}, u32[]{:S(2)}, u32[]{:S(2)}) collective-permute-start(bf16[8,2,32,1024]{3,2,1,0:T(8,128)(2,1)S(1)} %bitcast.32), channel_id=1, source_target_pairs={{0,1},{1,0},{2,3},{3,2},{4,5},{5,4},{6,7},{7,6},{8,9},{9,8},{10,11... | collective-permute-start | bytes 3145736 | tf_op jit(solution)/shard_map/ppermute | solution.py:249
  72.4 1.6 %copy-start.1 = (bf16[2,2,256,1024]{3,2,1,0:T(8,128)(2,1)S(1)}, bf16[2,2,256,1024]{3,2,1,0:T(8,128)(2,1)}, u32[]{:S(2)}) copy-start(bf16[2,2,256,1024]{3,2,1,0:T(8,128)(2,1)} %copy-done) | copy-start | bytes 6291460
  75.7 14.5 %collective-permute-start.1 = (bf16[8,2,32,1024]{3,2,1,0:T(8,128)(2,1)S(1)}, bf16[8,2,32,1024]{3,2,1,0:T(8,128)(2,1)S(1)}, u32[]{:S(2)}, u32[]{:S(2)}) collective-permute-start(bf16[8,2,32,1024]{3,2,1,0:T(8,128)(2,1)S(1)} %get-tuple-element.38), channel_id=1, source_target_pairs={{0,1},{1,0},{2,3},{3,2},{4,5},{5,4},{6,7},{7,6},{8,9},{9,8},{10,11... | collective-permute-start | bytes 3145736 | tf_op jit(solution)/shard_map/ppermute | solution.py:249
  79.6 49.6 %collective-permute-start.2 = (bf16[8,2,64,1024]{3,2,1,0:T(8,128)(2,1)}, bf16[8,2,64,1024]{3,2,1,0:T(8,128)(2,1)}, u32[]{:S(2)}, u32[]{:S(2)}) collective-permute-start(bf16[8,2,64,1024]{3,2,1,0:T(8,128)(2,1)} %bitcast.16.own_ref), channel_id=1, source_target_pairs={{0,1},{1,0},{2,3},{3,2},{4,5},{5,4},{6,7},{7,6},{8,9},{9,8},{10,11... | collective-permute-start | bytes 6291464 | tf_op jit(solution)/shard_map/ppermute | solution.py:249
  90.6 38.7 %copy-start.7 = (bf16[1,512,112]{1,2,0:T(8,128)(2,1)S(1)}, bf16[1,512,112]{1,2,0:T(8,128)(2,1)}, u32[]{:S(2)}) copy-start(bf16[1,512,112]{1,2,0:T(8,128)(2,1)} %param.20) | copy-start | bytes 344068
  90.6 38.7 %copy-start.8 = (bf16[1,512,112]{1,2,0:T(8,128)(2,1)S(1)}, bf16[1,512,112]{1,2,0:T(8,128)(2,1)}, u32[]{:S(2)}) copy-start(bf16[1,512,112]{1,2,0:T(8,128)(2,1)} %param.21) | copy-start | bytes 344068
  112.8 28.4 %all-to-all-start.3 = ((bf16[16,32,128]{2,1,0:T(8,128)(2,1)}), bf16[16,32,128]{2,1,0:T(8,128)(2,1)S(1)}, u32[]{:S(2)}, u32[]{:S(2)}) async-start(bf16[16,32,128]{2,1,0:T(8,128)(2,1)} %mix_kernel.1), calls=%async_computation.3 | async-start | bytes 262144 | tf_op jit(solution)/shard_map/all_to_all | solution.py:254

commit v6 on v5

--- a/solution.py
+++ b/solution.py
@@ -99,9 +99,10 @@
     keep = iota(twice.shape, 1) // F == iota(twice.shape, 0) // toks
     twice = jnp.where(keep, twice, jnp.zeros_like(twice))
     pick = jnp.where(iota((F, feats), 1) % F == iota((F, feats), 0), 1.0, 0.0).astype(BF)
-    block = jnp.concatenate([dot_last(pick, twice).astype(BF), g_ref[...]], axis=0)
+    x = dot_last(pick, twice).astype(BF)
+    blocks = [jnp.concatenate([x, g_ref[F * h : F * (h + 1)]], axis=0) for h in range(2)]
     for z in range(out_ref.shape[0]):
-        out_ref[z] = block
+        out_ref[z] = blocks[z % 2]
 
 
 def placed(routes, rows, capacity, tokens):
@@ -153,10 +154,13 @@
             out_ref[:, xh, :, h * (width // 2) : (h + 1) * (width // 2)] = block
 
 
-def rows_old_kernel(picks_ref, weight_ref, got_ref, out_ref):
+def rows_old_kernel(me_ref, picks_ref, weight_ref, got_ref, other_ref, out_ref):
     experts, _, slots, width = out_ref.shape
+    even = me_ref[1] == 0
+    mine = got_ref[:, F : 2 * F, :].reshape(-1, picks_ref.shape[1])
+    other = other_ref[...].reshape(mine.shape)
     for h in range(2):
-        g = got_ref[:, F * (1 + h) : F * (2 + h), :].reshape(-1, picks_ref.shape[1])
+        g = jnp.where(even, mine, other) if h == 0 else jnp.where(even, other, mine)
         block = (dot_last(picks_ref[...], g) * weight_ref[:, 0:1]).astype(BF)
         block = block.reshape(experts, slots, -1)
         for xh in range(2):
@@ -267,7 +271,7 @@
     pre_gate,
     pre_up,
 ):
-    me = lax.axis_index(CORE).astype(jnp.int32).reshape(1)
+    me = jnp.stack([lax.axis_index(CORE), lax.axis_index(Z) % 2]).astype(jnp.int32)
     experts = lax.axis_size(EXPERT)
     rows_new, rows_old = experts * CAP_B, experts * CAP_A
     hidden_units = w_gate.shape[2]
@@ -277,7 +281,7 @@
 
     packed = pl.pallas_call(
         pack_kernel,
-        out_shape=shape(16, 3 * F, 128),
+        out_shape=shape(16, 2 * F, 128),
         in_specs=[pl.BlockSpec(memory_space=pltpu.HBM)] * 2,
         out_specs=pl.BlockSpec(memory_space=pltpu.VMEM),
         scratch_shapes=[
@@ -321,7 +325,8 @@
     rows_b = shape(experts, 2, CAP_B, 1024)
     own = exchange(call(rows_new_kernel, rows_b, picks_b, got), PLANE)
     rows_a = shape(experts, 2, CAP_A, 1024)
-    sent_a = call(rows_old_kernel, rows_a, picks_a, weight_a, got)
+    half = lax.ppermute(got[:, F:], Z, [(z, z ^ 1) for z in range(lax.axis_size(Z))])
+    sent_a = call(rows_old_kernel, rows_a, me, picks_a, weight_a, got, half, scalars=1)
     own_a = exchange(sent_a, PLANE)
 
     hidden, partial = call(

time: 145 us -> 139 us (0.959)
  waiting for transfers between devices: 25.4 us -> 21.5 us
  starting transfers between devices: 66.3 us -> 62.8 us
  Pallas kernels: 17.9 us -> 19.8 us
    ppermute x3, starting transfers between devices: 22.9 us -> 13.6 us  [other_core(): return lax.ppermute(array, CORE, [(0, 1), (1, 0)])]
    ppermute x0 -> x1, starting transfers between devices: none -> 7.77 us  [per_device(): lax.ppermute(got[:, F:], Z, [(z, z ^ 1) for z in range(lax.axis_size(Z))])]
    all_to_all x1, waiting for transfers between devices: 7.22 us -> 1.88 us  [per_device(): got = lax.all_to_all(packed, Z, 0, 0, tiled=True)]
    ppermute x0 -> x1, waiting for transfers between devices: none -> 2.34 us  [per_device(): lax.ppermute(got[:, F:], Z, [(z, z ^ 1) for z in range(lax.axis_size(Z))])]
    pallas_call x8, Pallas kernels: 10.2 us -> 12.1 us  [call(): pl.pallas_call(body, out_shape=outs, in_specs=[smem] * scalars + [vmem] *...]
    all_to_all x3, starting transfers between devices: 27.6 us -> 25.7 us  [exchange(): return lax.all_to_all(peers, axes, 0, 0, tiled=True).reshape(array.shape)]
  transfers between devices with their start and end apart: 7 -> 8, of which waited for: 5 -> 5; matrix products, arithmetic and copies ran while one was open for 1% -> 1% of each run, Pallas kernels for 10% -> 12%
where the time goes in v6:
time: 139 us; the launch traced here: 137 us
  starting transfers between devices  62.8 us (45%)
  waiting for transfers between devices  21.5 us (15%)
  blocking collectives  20.8 us (15%)
  Pallas kernels  19.8 us (14%)
  local copies, waits for them, and re-layouts  9.23 us (7%)
  other arithmetic  1.73 us (1%)
    all_to_all x3, starting transfers between devices, exchange(): return lax.all_to_all(peers, axes, 0, 0, tiled=True).reshape(array.shape)  25.7 us
    all_to_all x1, blocking collectives, exchange(): return lax.all_to_all(peers, axes, 0, 0, tiled=True).reshape(array.shape)  20.8 us
    all_to_all x1, starting transfers between devices, per_device(): got = lax.all_to_all(packed, Z, 0, 0, tiled=True)  15.8 us
    all_to_all x3, waiting for transfers between devices, exchange(): return lax.all_to_all(peers, axes, 0, 0, tiled=True).reshape(array.shape)  15 us
    ppermute x3, starting transfers between devices, other_core(): return lax.ppermute(array, CORE, [(0, 1), (1, 0)])  13.6 us
    pallas_call x8, Pallas kernels, call(): pl.pallas_call(body, out_shape=outs, in_specs=[smem] * scalars + [vmem] *...  12.1 us
    unnamed x22, local copies, waits for them, and re-layouts  9.22 us
    ppermute x1, starting transfers between devices, per_device(): lax.ppermute(got[:, F:], Z, [(z, z ^ 1) for z in range(lax.axis_size(Z))])  7.77 us
  transfers between devices with their start and end apart: 8, of which 5 were waited for; matrix products, arithmetic and copies ran while one was open for 1% of the time, Pallas kernels for 12%

profile of v6, /device:TPU:1, one launch (start us, length us, event | category | flops | bytes accessed | tf_op | source)
XLA Modules:
  0.0 136.7 jit_solution(1096413882707288193)
XLA Ops:
  3.0 15.8 %all-to-all-start = ((bf16[16,64,128]{2,1,0:T(8,128)(2,1)}), bf16[16,64,128]{2,1,0:T(8,128)(2,1)S(1)}, u32[]{:S(2)}, u32[]{:S(2)}) async-start(bf16[16,64,128]{2,1,0:T(8,128)(2,1)} %pack_kernel.1), calls=%async_computation | async-start | bytes 524288 | tf_op jit(solution)/shard_map/all_to_all | solution.py:295
  22.3 1.2 copy-done.4
  23.4 1.2 copy-done.5
  25.8 2.9 %weights_kernel.1 = (bf16[2,2,256,1024]{3,2,1,0:T(8,128)(2,1)S(1)}, bf16[2,2,128,1024]{3,2,1,0:T(8,128)(2,1)S(1)}) custom-call(s32[2]{0:T(128)S(1)} %pad_add_fusion.1.me_ref, bf16[112,4096]{1,0:T(8,128)(2,1)S(1)} %bitcast.38, bf16[112,4096]{1,0:T(8,128)(2,1)S(1)} %bitcast.39, bf16[112,4096]{1,0:T(8,128)(2,1)S(1)} %bitcast.40), custom_call_target="tpu_custom_call" | custom-call | flops 1400000000 | bytes 6000000 | tf_op jit(solution)/shard_map/weights_kernel/pallas_call | solution.py:41
  28.7 1.3 copy-done
  30.0 1.9 %all-to-all-done.got_ref = bf16[16,64,128]{2,1,0:T(8,128)(2,1)S(1)} async-done(((bf16[16,64,128]{2,1,0:T(8,128)(2,1)}), bf16[16,64,128]{2,1,0:T(8,128)(2,1)S(1)}, u32[]{:S(2)}, u32[]{:S(2)}) %all-to-all-start) | async-done | bytes 262176 | tf_op jit(solution)/shard_map/all_to_all | solution.py:295
  31.9 1.3 rows_new_kernel.1
  33.2 6.8 %all-to-all-start.1 = ((bf16[16,32,1024]{2,1,0:T(8,128)(2,1)}), bf16[16,32,1024]{2,1,0:T(8,128)(2,1)S(1)}, u32[]{:S(2)}, u32[]{:S(2)}) async-start(bf16[16,32,1024]{2,1,0:T(8,128)(2,1)} %bitcast.12), calls=%async_computation.1 | async-start | bytes 2097152 | tf_op jit(solution)/shard_map/all_to_all | solution.py:258
  40.0 7.8 %collective-permute-start.2 = (bf16[16,32,128]{2,1,0:T(8,128)(2,1)S(1)}, bf16[16,32,128]{2,1,0:T(8,128)(2,1)S(1)}, u32[]{:S(2)}, u32[]{:S(2)}) collective-permute-start(bf16[16,32,128]{2,1,0:T(8,128)(2,1)S(1)} %slice.3), channel_id=1, source_target_pairs={{0,4},{4,0},{8,12},{12,8},{16,20},{20,16},{24,28},{28,24},{32,36},... | collective-permute-start | bytes 393224 | tf_op jit(solution)/shard_map/ppermute | solution.py:328
  47.8 2.3 %collective-permute-done.2.other_ref = bf16[16,32,128]{2,1,0:T(8,128)(2,1)S(1)} collective-permute-done((bf16[16,32,128]{2,1,0:T(8,128)(2,1)S(1)}, bf16[16,32,128]{2,1,0:T(8,128)(2,1)S(1)}, u32[]{:S(2)}, u32[]{:S(2)}) %collective-permute-start.2) | collective-permute-done | bytes 131104 | tf_op jit(solution)/shard_map/ppermute | solution.py:328
  50.1 2.3 %rows_old_kernel.1 = bf16[8,2,64,1024]{3,2,1,0:T(8,128)(2,1)} custom-call(s32[2]{0:T(128)S(1)} %pad_add_fusion.1.me_ref, bf16[512,128]{1,0:T(8,128)(2,1)S(1)} %get-tuple-element.39.picks_ref, f32[512,128]{1,0:T(8,128)S(1)} %get-tuple-element.40.weight_ref, bf16[16,64,128]{2,1,0:T(8,128)(2,1)S(1)} %all-to-all-done.got_ref, ...), custom_call_target="tpu_custom_call" | custom-call | flops 10000000 | bytes 1000000 | tf_op jit(solution)/shard_map/rows_old_kernel/pallas_call | solution.py:41
  52.4 7.0 %all-to-all-start.4 = ((bf16[16,64,1024]{2,1,0:T(8,128)(2,1)}), bf16[16,64,1024]{2,1,0:T(8,128)(2,1)}, u32[]{:S(2)}, u32[]{:S(2)}) async-start(bf16[16,64,1024]{2,1,0:T(8,128)(2,1)} %bitcast.16), calls=%async_computation.4 | async-start | bytes 4194304 | tf_op jit(solution)/shard_map/all_to_all | solution.py:258
  59.5 5.4 %collective-permute-start = (bf16[8,2,32,1024]{3,2,1,0:T(8,128)(2,1)S(1)}, bf16[8,2,32,1024]{3,2,1,0:T(8,128)(2,1)S(1)}, u32[]{:S(2)}, u32[]{:S(2)}) collective-permute-start(bf16[8,2,32,1024]{3,2,1,0:T(8,128)(2,1)S(1)} %bitcast.33), channel_id=1, source_target_pairs={{0,1},{1,0},{2,3},{3,2},{4,5},{5,4},{6,7},{7,6},{8,9},{9,8},{10,11... | collective-permute-start | bytes 3145736 | tf_op jit(solution)/shard_map/ppermute | solution.py:253
  64.8 2.3 %collective-permute-done.other_ref = bf16[8,2,32,1024]{3,2,1,0:T(8,128)(2,1)S(1)} collective-permute-done((bf16[8,2,32,1024]{3,2,1,0:T(8,128)(2,1)S(1)}, bf16[8,2,32,1024]{3,2,1,0:T(8,128)(2,1)S(1)}, u32[]{:S(2)}, u32[]{:S(2)}) %collective-permute-start) | collective-permute-done | bytes 1048608 | tf_op jit(solution)/shard_map/ppermute | solution.py:253
  67.1 1.6 %copy-done.1 = bf16[2,2,256,1024]{3,2,1,0:T(8,128)(2,1)S(1)} copy-done((bf16[2,2,256,1024]{3,2,1,0:T(8,128)(2,1)S(1)}, bf16[2,2,256,1024]{3,2,1,0:T(8,128)(2,1)}, u32[]{:S(2)}) %copy-start.1) | copy-done | bytes 2097176
  68.7 2.6 %up_kernel.1 = (bf16[256,128]{1,0:T(8,128)(2,1)S(1)}, bf16[8,2,32,1024]{3,2,1,0:T(8,128)(2,1)}) custom-call(bf16[8,2,32,1024]{3,2,1,0:T(8,128)(2,1)S(1)} %bitcast.34, bf16[8,2,32,1024]{3,2,1,0:T(8,128)(2,1)S(1)} %collective-permute-done.other_ref, bf16[2,2,256,1024]{3,2,1,0:T(8,128)(2,1)S(1)} %copy-done.1, bf16[2,2,128,1024]{3,2,1,0:T(8,128)(2,1)S(1)} %get-tuple-element.36.dn_ref), custom_call_target="tpu_custom_call" | custom-call | flops 800000000 | bytes 4000000 | tf_op jit(solution)/shard_map/up_kernel/pallas_call | solution.py:41
  71.3 2.3 %collective-permute-start.1 = (bf16[8,2,32,1024]{3,2,1,0:T(8,128)(2,1)}, bf16[8,2,32,1024]{3,2,1,0:T(8,128)(2,1)S(1)}, u32[]{:S(2)}, u32[]{:S(2)}) collective-permute-start(bf16[8,2,32,1024]{3,2,1,0:T(8,128)(2,1)} %get-tuple-element.38), channel_id=1, source_target_pairs={{0,1},{1,0},{2,3},{3,2},{4,5},{5,4},{6,7},{7,6},{8,9},{9,8},{10,11... | collective-permute-start | bytes 3145736 | tf_op jit(solution)/shard_map/ppermute | solution.py:253
  73.5 9.8 %all-to-all-done.4 = bf16[16,64,1024]{2,1,0:T(8,128)(2,1)} async-done(((bf16[16,64,1024]{2,1,0:T(8,128)(2,1)}), bf16[16,64,1024]{2,1,0:T(8,128)(2,1)}, u32[]{:S(2)}, u32[]{:S(2)}) %all-to-all-start.4) | async-done | bytes 2097184 | tf_op jit(solution)/shard_map/all_to_all | solution.py:258
  83.4 5.9 %collective-permute-start.3 = (bf16[8,2,64,1024]{3,2,1,0:T(8,128)(2,1)}, bf16[8,2,64,1024]{3,2,1,0:T(8,128)(2,1)}, u32[]{:S(2)}, u32[]{:S(2)}) collective-permute-start(bf16[8,2,64,1024]{3,2,1,0:T(8,128)(2,1)} %bitcast.17.own_ref), channel_id=1, source_target_pairs={{0,1},{1,0},{2,3},{3,2},{4,5},{5,4},{6,7},{7,6},{8,9},{9,8},{10,11... | collective-permute-start | bytes 6291464 | tf_op jit(solution)/shard_map/ppermute | solution.py:253
  89.8 20.8 %all_to_all.25 = bf16[16,32,1024]{2,1,0:T(8,128)(2,1)S(1)} all-to-all(bf16[16,32,1024]{2,1,0:T(8,128)(2,1)S(1)} %bitcast.35), channel_id=1, replica_groups=mesh['expert_0'=4,'expert_1'=2,'dp_0'=16,'dp_1'=2,'dp_2'=2] {'expert_0',..., dimensions={0} | all-to-all | bytes 2097152 | tf_op jit(solution)/shard_map/all_to_all | solution.py:258
  110.6 1.4 %mix_kernel.1 = bf16[16,32,128]{2,1,0:T(8,128)(2,1)} custom-call(bf16[3,64,256]{2,1,0:T(8,128)(2,1)S(1)} %get-tuple-element.32.mix_ref, bf16[8,2,32,1024]{3,2,1,0:T(8,128)(2,1)S(1)} %bitcast.36), custom_call_target="tpu_custom_call" | custom-call | flops 400000000 | bytes 1000000 | tf_op jit(solution)/shard_map/mix_kernel/pallas_call | solution.py:41
  112.0 12.0 %all-to-all-start.3 = ((bf16[16,32,128]{2,1,0:T(8,128)(2,1)}), bf16[16,32,128]{2,1,0:T(8,128)(2,1)S(1)}, u32[]{:S(2)}, u32[]{:S(2)}) async-start(bf16[16,32,128]{2,1,0:T(8,128)(2,1)} %mix_kernel.1), calls=%async_computation.3 | async-start | bytes 262144 | tf_op jit(solution)/shard_map/all_to_all | solution.py:258
  124.0 6.8 %back_kernel.1 = (bf16[112,4096]{1,0:T(8,128)(2,1)}, bf16[112,512]{1,0:T(8,128)(2,1)}, bf16[112,512]{1,0:T(8,128)(2,1)}) custom-call(s32[2]{0:T(128)S(1)} %pad_add_fusion.1.me_ref, bf16[8,2,64,1024]{3,2,1,0:T(8,128)(2,1)} %bitcast.17.own_ref, bf16[8,2,64,1024]{3,2,1,0:T(8,128)(2,1)} %collective-permute-done.3.other_ref, ...), custom_call_target="tpu_custom_call" | custom-call | flops 1500000000 | bytes 8000000 | tf_op jit(solution)/shard_map/back_kernel/pallas_call | solution.py:347
  130.8 5.2 %all-to-all-done.3.got_ref = bf16[16,32,128]{2,1,0:T(8,128)(2,1)S(1)} async-done(((bf16[16,32,128]{2,1,0:T(8,128)(2,1)}), bf16[16,32,128]{2,1,0:T(8,128)(2,1)S(1)}, u32[]{:S(2)}, u32[]{:S(2)}) %all-to-all-start.3) | async-done | bytes 131104 | tf_op jit(solution)/shard_map/all_to_all | solution.py:258
  (29 shorter events, 8.3 us)
Async XLA Ops:
  0.6 0.7 copy-start.2
  1.3 0.7 copy-start.3
  3.0 28.9 %all-to-all-start = ((bf16[16,64,128]{2,1,0:T(8,128)(2,1)}), bf16[16,64,128]{2,1,0:T(8,128)(2,1)S(1)}, u32[]{:S(2)}, u32[]{:S(2)}) async-start(bf16[16,64,128]{2,1,0:T(8,128)(2,1)} %pack_kernel.1), calls=%async_computation | async-start | bytes 524288 | tf_op jit(solution)/shard_map/all_to_all | solution.py:295
  20.4 0.7 copy-start.9
  21.1 0.7 copy-start.10
  22.3 1.2 copy-start.4
  23.4 1.2 copy-start.5
  24.6 1.2 copy-start.6
  28.7 1.3 copy-start
  33.2 19.3 %all-to-all-start.1 = ((bf16[16,32,1024]{2,1,0:T(8,128)(2,1)}), bf16[16,32,1024]{2,1,0:T(8,128)(2,1)S(1)}, u32[]{:S(2)}, u32[]{:S(2)}) async-start(bf16[16,32,1024]{2,1,0:T(8,128)(2,1)} %bitcast.12), calls=%async_computation.1 | async-start | bytes 2097152 | tf_op jit(solution)/shard_map/all_to_all | solution.py:258
  40.0 10.1 %collective-permute-start.2 = (bf16[16,32,128]{2,1,0:T(8,128)(2,1)S(1)}, bf16[16,32,128]{2,1,0:T(8,128)(2,1)S(1)}, u32[]{:S(2)}, u32[]{:S(2)}) collective-permute-start(bf16[16,32,128]{2,1,0:T(8,128)(2,1)S(1)} %slice.3), channel_id=1, source_target_pairs={{0,4},{4,0},{8,12},{12,8},{16,20},{20,16},{24,28},{28,24},{32,36},... | collective-permute-start | bytes 393224 | tf_op jit(solution)/shard_map/ppermute | solution.py:328
  52.4 30.9 %all-to-all-start.4 = ((bf16[16,64,1024]{2,1,0:T(8,128)(2,1)}), bf16[16,64,1024]{2,1,0:T(8,128)(2,1)}, u32[]{:S(2)}, u32[]{:S(2)}) async-start(bf16[16,64,1024]{2,1,0:T(8,128)(2,1)} %bitcast.16), calls=%async_computation.4 | async-start | bytes 4194304 | tf_op jit(solution)/shard_map/all_to_all | solution.py:258
  59.5 7.6 %collective-permute-start = (bf16[8,2,32,1024]{3,2,1,0:T(8,128)(2,1)S(1)}, bf16[8,2,32,1024]{3,2,1,0:T(8,128)(2,1)S(1)}, u32[]{:S(2)}, u32[]{:S(2)}) collective-permute-start(bf16[8,2,32,1024]{3,2,1,0:T(8,128)(2,1)S(1)} %bitcast.33), channel_id=1, source_target_pairs={{0,1},{1,0},{2,3},{3,2},{4,5},{5,4},{6,7},{7,6},{8,9},{9,8},{10,11... | collective-permute-start | bytes 3145736 | tf_op jit(solution)/shard_map/ppermute | solution.py:253
  67.1 1.6 %copy-start.1 = (bf16[2,2,256,1024]{3,2,1,0:T(8,128)(2,1)S(1)}, bf16[2,2,256,1024]{3,2,1,0:T(8,128)(2,1)}, u32[]{:S(2)}) copy-start(bf16[2,2,256,1024]{3,2,1,0:T(8,128)(2,1)} %copy-done) | copy-start | bytes 6291460
  71.3 18.0 %collective-permute-start.1 = (bf16[8,2,32,1024]{3,2,1,0:T(8,128)(2,1)}, bf16[8,2,32,1024]{3,2,1,0:T(8,128)(2,1)S(1)}, u32[]{:S(2)}, u32[]{:S(2)}) collective-permute-start(bf16[8,2,32,1024]{3,2,1,0:T(8,128)(2,1)} %get-tuple-element.38), channel_id=1, source_target_pairs={{0,1},{1,0},{2,3},{3,2},{4,5},{5,4},{6,7},{7,6},{8,9},{9,8},{10,11... | collective-permute-start | bytes 3145736 | tf_op jit(solution)/shard_map/ppermute | solution.py:253
  83.4 40.6 %collective-permute-start.3 = (bf16[8,2,64,1024]{3,2,1,0:T(8,128)(2,1)}, bf16[8,2,64,1024]{3,2,1,0:T(8,128)(2,1)}, u32[]{:S(2)}, u32[]{:S(2)}) collective-permute-start(bf16[8,2,64,1024]{3,2,1,0:T(8,128)(2,1)} %bitcast.17.own_ref), channel_id=1, source_target_pairs={{0,1},{1,0},{2,3},{3,2},{4,5},{5,4},{6,7},{7,6},{8,9},{9,8},{10,11... | collective-permute-start | bytes 6291464 | tf_op jit(solution)/shard_map/ppermute | solution.py:253
  89.7 34.2 %copy-start.7 = (bf16[1,512,112]{1,2,0:T(8,128)(2,1)S(1)}, bf16[1,512,112]{1,2,0:T(8,128)(2,1)}, u32[]{:S(2)}) copy-start(bf16[1,512,112]{1,2,0:T(8,128)(2,1)} %param.20) | copy-start | bytes 344068
  89.7 34.2 %copy-start.8 = (bf16[1,512,112]{1,2,0:T(8,128)(2,1)S(1)}, bf16[1,512,112]{1,2,0:T(8,128)(2,1)}, u32[]{:S(2)}) copy-start(bf16[1,512,112]{1,2,0:T(8,128)(2,1)} %param.21) | copy-start | bytes 344068
  112.0 24.0 %all-to-all-start.3 = ((bf16[16,32,128]{2,1,0:T(8,128)(2,1)}), bf16[16,32,128]{2,1,0:T(8,128)(2,1)S(1)}, u32[]{:S(2)}, u32[]{:S(2)}) async-start(bf16[16,32,128]{2,1,0:T(8,128)(2,1)} %mix_kernel.1), calls=%async_computation.3 | async-start | bytes 262144 | tf_op jit(solution)/shard_map/all_to_all | solution.py:258

commit v7 on v6

--- a/solution.py
+++ b/solution.py
@@ -154,17 +154,12 @@
             out_ref[:, xh, :, h * (width // 2) : (h + 1) * (width // 2)] = block
 
 
-def rows_old_kernel(me_ref, picks_ref, weight_ref, got_ref, other_ref, out_ref):
+def rows_old_kernel(picks_ref, weight_ref, got_ref, out_ref):
+    g = got_ref[:, F : 2 * F, :].reshape(-1, picks_ref.shape[1])
+    block = (dot_last(picks_ref[...], g) * weight_ref[:, 0:1]).astype(BF)
     experts, _, slots, width = out_ref.shape
-    even = me_ref[1] == 0
-    mine = got_ref[:, F : 2 * F, :].reshape(-1, picks_ref.shape[1])
-    other = other_ref[...].reshape(mine.shape)
-    for h in range(2):
-        g = jnp.where(even, mine, other) if h == 0 else jnp.where(even, other, mine)
-        block = (dot_last(picks_ref[...], g) * weight_ref[:, 0:1]).astype(BF)
-        block = block.reshape(experts, slots, -1)
-        for xh in range(2):
-            out_ref[:, xh, :, h * (width // 2) : (h + 1) * (width // 2)] = block
+    for xh in range(2):
+        out_ref[:, xh] = block.reshape(experts, slots, width)
 
 
 def up_kernel(own_ref, other_ref, gu_ref, dn_ref, hidden_ref, out_ref):
@@ -218,13 +213,17 @@
 
 
 def back_kernel(
-    me_ref, own_ref, other_ref, dn_ref, gate_ref, up_ref, down_ref, dg_ref, du_ref, held
+    me_ref, own_ref, near_ref, other_ref, other_near_ref, dn_ref, gate_ref, up_ref,
+    down_ref, dg_ref, du_ref, held,
 ):
-    refs = (own_ref, other_ref)
+    width = own_ref.shape[3]
+    mine = pl.ds(pl.multiple_of(me_ref[1] * width, width), width)
+    rest = pl.ds(pl.multiple_of((1 - me_ref[1]) * width, width), width)
+    parts = ((0, mine, own_ref), (1, mine, other_ref), (0, rest, near_ref), (1, rest, other_near_ref))
     total = None
-    for o, ref in enumerate(refs):
-        for xh in range(2):
-            term = dot_last(dn_ref[o, xh], rows_of(ref, xh))
+    for o, lanes, ref in parts:
+        for xh in range(2):
+            term = dot_last(dn_ref[o, xh, :, lanes], rows_of(ref, xh))
             total = term if total is None else total + term
     gate, up = gate_ref[...].astype(F32), up_ref[...].astype(F32)
     grad = total[: gate.shape[0]]
@@ -233,9 +232,9 @@
     dg_ref[...] = (grad * up * sigma * (1.0 + gate * (1.0 - sigma))).astype(BF)
     du_ref[...] = (grad * active).astype(BF)
     hidden = (active * up).astype(BF)
-    for o, ref in enumerate(refs):
-        for xh in range(2):
-            held[o, xh] = dot(hidden, rows_of(ref, xh)).astype(BF)
+    for o, lanes, ref in parts:
+        for xh in range(2):
+            held[o, xh, :, lanes] = dot(hidden, rows_of(ref, xh)).astype(BF)
     order = lane_order(me_ref[0])
     for xh in range(2):
         for zq in range(4):
@@ -324,9 +323,9 @@
 
     rows_b = shape(experts, 2, CAP_B, 1024)
     own = exchange(call(rows_new_kernel, rows_b, picks_b, got), PLANE)
-    rows_a = shape(experts, 2, CAP_A, 1024)
-    half = lax.ppermute(got[:, F:], Z, [(z, z ^ 1) for z in range(lax.axis_size(Z))])
-    sent_a = call(rows_old_kernel, rows_a, me, picks_a, weight_a, got, half, scalars=1)
+    rows_a = shape(experts, 2, CAP_A, 512)
+    sent_a = call(rows_old_kernel, rows_a, picks_a, weight_a, got)
+    own, sent_a = lax.optimization_barrier((own, sent_a))
     own_a = exchange(sent_a, PLANE)
 
     hidden, partial = call(
@@ -342,7 +341,8 @@
     summed = call(down_kernel, rows_b, hidden, down, other_core(partial), flops=2 * 10**8)
     returned = exchange(summed, PLANE)
 
-    other_a = other_core(own_a)
+    near_a = lax.ppermute(own_a, Z, [(z, z ^ 1) for z in range(lax.axis_size(Z))])
+    other_a, other_near = other_core(own_a), other_core(near_a)
     vmem = pl.BlockSpec(memory_space=pltpu.VMEM)
     weight_grad, gate_grad, up_grad = pl.pallas_call(
         back_kernel,
@@ -351,7 +351,7 @@
             shape(hidden_units, rows_old),
             shape(hidden_units, rows_old),
         ),
-        in_specs=[pl.BlockSpec(memory_space=pltpu.SMEM)] + [vmem] * 5,
+        in_specs=[pl.BlockSpec(memory_space=pltpu.SMEM)] + [vmem] * 7,
         out_specs=(vmem,) * 3,
         scratch_shapes=[pltpu.VMEM((2, 2, hidden_units, 1024), BF)],
         cost_estimate=pl.CostEstimate(
@@ -359,7 +359,7 @@
         ),
         compiler_params=pltpu.CompilerParams(vmem_limit_bytes=16 * MIB),
         name="back_kernel",
-    )(me, own_a, other_a, down, pre_gate[0].T, pre_up[0].T)
+    )(me, own_a, near_a, other_a, other_near, down, pre_gate[0].T, pre_up[0].T)
     mixed = call(mix_kernel, shape(16, F, 128), mix, returned, flops=4 * 10**8)
     mixed = exchange(mixed, Z)
     mixed, weight_grad, gate_grad, up_grad = lax.optimization_barrier(

time: 139 us -> 137 us (0.986)
  blocking collectives: 20.8 us -> 0 us
  waiting for transfers between devices: 21.5 us -> 39.2 us
    all_to_all x1 -> x0, blocking collectives: 20.8 us -> none  [exchange(): return lax.all_to_all(peers, axes, 0, 0, tiled=True).reshape(array.shape)]
    all_to_all x3 -> x4, waiting for transfers between devices: 15 us -> 25.4 us  [exchange(): return lax.all_to_all(peers, axes, 0, 0, tiled=True).reshape(array.shape)]
    ppermute x1, waiting for transfers between devices: 2.34 us -> 12.2 us  [per_device(): lax.ppermute(own_a, Z, [(z, z ^ 1) for z in range(lax.axis_size(Z))])]
    ppermute x3 -> x4, starting transfers between devices: 13.6 us -> 19 us  [other_core(): return lax.ppermute(array, CORE, [(0, 1), (1, 0)])]
    all_to_all x3 -> x4, starting transfers between devices: 25.7 us -> 23 us  [exchange(): return lax.all_to_all(peers, axes, 0, 0, tiled=True).reshape(array.shape)]
    ppermute x3 -> x4, waiting for transfers between devices: 2.27 us -> 0.01 us  [other_core(): return lax.ppermute(array, CORE, [(0, 1), (1, 0)])]
    ppermute x1, starting transfers between devices: 7.77 us -> 6.17 us  [per_device(): lax.ppermute(own_a, Z, [(z, z ^ 1) for z in range(lax.axis_size(Z))])]
  transfers between devices with their start and end apart: 8 -> 10, of which waited for: 5 -> 5; matrix products, arithmetic and copies ran while one was open for 1% -> 1% of each run, Pallas kernels for 12% -> 12%
where the time goes in v7:
time: 137 us; the launch traced here: 134 us
  starting transfers between devices  64 us (47%)
  waiting for transfers between devices  39.2 us (29%)
  Pallas kernels  19.5 us (14%)
  local copies, waits for them, and re-layouts  9.25 us (7%)
  other arithmetic  1.73 us (1%)
    all_to_all x4, waiting for transfers between devices, exchange(): return lax.all_to_all(peers, axes, 0, 0, tiled=True).reshape(array.shape)  25.4 us
    all_to_all x4, starting transfers between devices, exchange(): return lax.all_to_all(peers, axes, 0, 0, tiled=True).reshape(array.shape)  23 us
    ppermute x4, starting transfers between devices, other_core(): return lax.ppermute(array, CORE, [(0, 1), (1, 0)])  19 us
    all_to_all x1, starting transfers between devices, per_device(): got = lax.all_to_all(packed, Z, 0, 0, tiled=True)  15.8 us
    pallas_call x8, Pallas kernels, call(): pl.pallas_call(body, out_shape=outs, in_specs=[smem] * scalars + [vmem] *...  12.2 us
    ppermute x1, waiting for transfers between devices, per_device(): lax.ppermute(own_a, Z, [(z, z ^ 1) for z in range(lax.axis_size(Z))])  12.2 us
    unnamed x22, local copies, waits for them, and re-layouts  9.25 us
    pallas_call x1, Pallas kernels, per_device(): pl.pallas_call(back_kernel, out_shape=(shape(hidden_units, 4096), shape(h...  6.37 us
  transfers between devices with their start and end apart: 10, of which 5 were waited for; matrix products, arithmetic and copies ran while one was open for 1% of the time, Pallas kernels for 12%

profile of v7, /device:TPU:1, one launch (start us, length us, event | category | flops | bytes accessed | tf_op | source)
XLA Modules:
  0.0 134.5 jit_solution(14496816273634583279)
XLA Ops:
  3.0 15.8 %all-to-all-start = ((bf16[16,64,128]{2,1,0:T(8,128)(2,1)}), bf16[16,64,128]{2,1,0:T(8,128)(2,1)S(1)}, u32[]{:S(2)}, u32[]{:S(2)}) async-start(bf16[16,64,128]{2,1,0:T(8,128)(2,1)} %pack_kernel.1), calls=%async_computation | async-start | bytes 524288 | tf_op jit(solution)/shard_map/all_to_all | solution.py:294
  25.8 3.1 %weights_kernel.1 = (bf16[2,2,256,1024]{3,2,1,0:T(8,128)(2,1)S(1)}, bf16[2,2,128,1024]{3,2,1,0:T(8,128)(2,1)S(1)}) custom-call(s32[2]{0:T(128)S(1)} %pad_add_fusion.1.me_ref, bf16[112,4096]{1,0:T(8,128)(2,1)S(1)} %bitcast.37, bf16[112,4096]{1,0:T(8,128)(2,1)S(1)} %bitcast.38, bf16[112,4096]{1,0:T(8,128)(2,1)S(1)} %bitcast.39), custom_call_target="tpu_custom_call" | custom-call | flops 1400000000 | bytes 6000000 | tf_op jit(solution)/shard_map/weights_kernel/pallas_call | solution.py:41
  28.9 1.3 copy-done
  30.2 1.7 %all-to-all-done.got_ref = bf16[16,64,128]{2,1,0:T(8,128)(2,1)S(1)} async-done(((bf16[16,64,128]{2,1,0:T(8,128)(2,1)}), bf16[16,64,128]{2,1,0:T(8,128)(2,1)S(1)}, u32[]{:S(2)}, u32[]{:S(2)}) %all-to-all-start) | async-done | bytes 262176 | tf_op jit(solution)/shard_map/all_to_all | solution.py:294
  31.9 1.3 rows_new_kernel.1
  33.2 6.8 %all-to-all-start.1 = ((bf16[16,32,1024]{2,1,0:T(8,128)(2,1)}), bf16[16,32,1024]{2,1,0:T(8,128)(2,1)S(1)}, u32[]{:S(2)}, u32[]{:S(2)}) async-start(bf16[16,32,1024]{2,1,0:T(8,128)(2,1)} %bitcast.12), calls=%async_computation.1 | async-start | bytes 2097152 | tf_op jit(solution)/shard_map/all_to_all | solution.py:257
  39.9 1.3 rows_old_kernel.1
  41.2 9.6 %all-to-all-done.1 = bf16[16,32,1024]{2,1,0:T(8,128)(2,1)S(1)} async-done(((bf16[16,32,1024]{2,1,0:T(8,128)(2,1)}), bf16[16,32,1024]{2,1,0:T(8,128)(2,1)S(1)}, u32[]{:S(2)}, u32[]{:S(2)}) %all-to-all-start.1) | async-done | bytes 1048608 | tf_op jit(solution)/shard_map/all_to_all | solution.py:257
  50.8 9.5 %collective-permute-start = (bf16[8,2,32,1024]{3,2,1,0:T(8,128)(2,1)S(1)}, bf16[8,2,32,1024]{3,2,1,0:T(8,128)(2,1)S(1)}, u32[]{:S(2)}, u32[]{:S(2)}) collective-permute-start(bf16[8,2,32,1024]{3,2,1,0:T(8,128)(2,1)S(1)} %bitcast.33), channel_id=1, source_target_pairs={{0,1},{1,0},{2,3},{3,2},{4,5},{5,4},{6,7},{7,6},{8,9},{9,8},{10,11... | collective-permute-start | bytes 3145736 | tf_op jit(solution)/shard_map/ppermute | solution.py:252
  60.3 4.4 %all-to-all-start.4 = ((bf16[16,64,512]{2,1,0:T(8,128)(2,1)}), bf16[16,64,512]{2,1,0:T(8,128)(2,1)}, u32[]{:S(2)}, u32[]{:S(2)}) async-start(bf16[16,64,512]{2,1,0:T(8,128)(2,1)} %bitcast.16), calls=%async_computation.4 | async-start | bytes 2097152 | tf_op jit(solution)/shard_map/all_to_all | solution.py:257
  64.7 1.6 %copy-done.1 = bf16[2,2,256,1024]{3,2,1,0:T(8,128)(2,1)S(1)} copy-done((bf16[2,2,256,1024]{3,2,1,0:T(8,128)(2,1)S(1)}, bf16[2,2,256,1024]{3,2,1,0:T(8,128)(2,1)}, u32[]{:S(2)}) %copy-start.1) | copy-done | bytes 2097176
  66.2 2.6 %up_kernel.1 = (bf16[256,128]{1,0:T(8,128)(2,1)S(1)}, bf16[8,2,32,1024]{3,2,1,0:T(8,128)(2,1)}) custom-call(bf16[8,2,32,1024]{3,2,1,0:T(8,128)(2,1)S(1)} %bitcast.34, bf16[8,2,32,1024]{3,2,1,0:T(8,128)(2,1)S(1)} %collective-permute-done.other_ref, bf16[2,2,256,1024]{3,2,1,0:T(8,128)(2,1)S(1)} %copy-done.1, bf16[2,2,128,1024]{3,2,1,0:T(8,128)(2,1)S(1)} %get-tuple-element.41.dn_ref), custom_call_target="tpu_custom_call" | custom-call | flops 800000000 | bytes 4000000 | tf_op jit(solution)/shard_map/up_kernel/pallas_call | solution.py:41
  68.8 1.9 %collective-permute-start.1 = (bf16[8,2,32,1024]{3,2,1,0:T(8,128)(2,1)}, bf16[8,2,32,1024]{3,2,1,0:T(8,128)(2,1)S(1)}, u32[]{:S(2)}, u32[]{:S(2)}) collective-permute-start(bf16[8,2,32,1024]{3,2,1,0:T(8,128)(2,1)} %get-tuple-element.43), channel_id=1, source_target_pairs={{0,1},{1,0},{2,3},{3,2},{4,5},{5,4},{6,7},{7,6},{8,9},{9,8},{10,11... | collective-permute-start | bytes 3145736 | tf_op jit(solution)/shard_map/ppermute | solution.py:252
  70.7 9.8 %all-to-all-done.4 = bf16[16,64,512]{2,1,0:T(8,128)(2,1)} async-done(((bf16[16,64,512]{2,1,0:T(8,128)(2,1)}), bf16[16,64,512]{2,1,0:T(8,128)(2,1)}, u32[]{:S(2)}, u32[]{:S(2)}) %all-to-all-start.4) | async-done | bytes 1048608 | tf_op jit(solution)/shard_map/all_to_all | solution.py:257
  80.5 6.2 %collective-permute-start.2 = (bf16[8,2,64,512]{3,2,1,0:T(8,128)(2,1)}, bf16[8,2,64,512]{3,2,1,0:T(8,128)(2,1)S(1)}, u32[]{:S(2)}, u32[]{:S(2)}) collective-permute-start(bf16[8,2,64,512]{3,2,1,0:T(8,128)(2,1)} %bitcast.17.own_ref), channel_id=1, source_target_pairs={{0,4},{4,0},{8,12},{12,8},{16,20},{20,16},{24,28},{28,24},{32,36},... | collective-permute-start | bytes 3145736 | tf_op jit(solution)/shard_map/ppermute | solution.py:344
  86.7 1.4 %down_kernel.1 = bf16[8,2,32,1024]{3,2,1,0:T(8,128)(2,1)} custom-call(bf16[256,128]{1,0:T(8,128)(2,1)S(1)} %get-tuple-element.42.hidden_ref, bf16[2,2,128,1024]{3,2,1,0:T(8,128)(2,1)S(1)} %get-tuple-element.41.dn_ref, bf16[8,2,32,1024]{3,2,1,0:T(8,128)(2,1)S(1)} %collective-permute-done.1.arrived_ref), custom_call_target="tpu_custom_call" | custom-call | flops 200000000 | bytes 1000000 | tf_op jit(solution)/shard_map/down_kernel/pallas_call | solution.py:41
  88.1 5.0 %all-to-all-start.2 = ((bf16[16,32,1024]{2,1,0:T(8,128)(2,1)}), bf16[16,32,1024]{2,1,0:T(8,128)(2,1)S(1)}, u32[]{:S(2)}, u32[]{:S(2)}) async-start(bf16[16,32,1024]{2,1,0:T(8,128)(2,1)} %bitcast.14), calls=%async_computation.2 | async-start | bytes 2097152 | tf_op jit(solution)/shard_map/all_to_all | solution.py:257
  93.1 3.9 %collective-permute-start.3 = (bf16[8,2,64,512]{3,2,1,0:T(8,128)(2,1)}, bf16[8,2,64,512]{3,2,1,0:T(8,128)(2,1)}, u32[]{:S(2)}, u32[]{:S(2)}) collective-permute-start(bf16[8,2,64,512]{3,2,1,0:T(8,128)(2,1)} %bitcast.17.own_ref), channel_id=1, source_target_pairs={{0,1},{1,0},{2,3},{3,2},{4,5},{5,4},{6,7},{7,6},{8,9},{9,8},{10,11... | collective-permute-start | bytes 3145736 | tf_op jit(solution)/shard_map/ppermute | solution.py:252
  97.0 12.2 %collective-permute-done.2.near_ref = bf16[8,2,64,512]{3,2,1,0:T(8,128)(2,1)S(1)} collective-permute-done((bf16[8,2,64,512]{3,2,1,0:T(8,128)(2,1)}, bf16[8,2,64,512]{3,2,1,0:T(8,128)(2,1)S(1)}, u32[]{:S(2)}, u32[]{:S(2)}) %collective-permute-start.2) | collective-permute-done | bytes 1048608 | tf_op jit(solution)/shard_map/ppermute | solution.py:344
  109.2 3.7 %collective-permute-start.4 = (bf16[8,2,64,512]{3,2,1,0:T(8,128)(2,1)S(1)}, bf16[8,2,64,512]{3,2,1,0:T(8,128)(2,1)}, u32[]{:S(2)}, u32[]{:S(2)}) collective-permute-start(bf16[8,2,64,512]{3,2,1,0:T(8,128)(2,1)S(1)} %collective-permute-done.2.near_ref), channel_id=1, source_target_pairs={{0,1},{1,0},{2,3},{3,2},{4,5},{5,4},{6,7},{7,6},{8,9},{9,8},{10,11... | collective-permute-start | bytes 3145736 | tf_op jit(solution)/shard_map/ppermute | solution.py:252
  113.0 1.4 %mix_kernel.1 = bf16[16,32,128]{2,1,0:T(8,128)(2,1)} custom-call(bf16[3,64,256]{2,1,0:T(8,128)(2,1)S(1)} %get-tuple-element.34.mix_ref, bf16[8,2,32,1024]{3,2,1,0:T(8,128)(2,1)S(1)} %bitcast.35), custom_call_target="tpu_custom_call" | custom-call | flops 400000000 | bytes 1000000 | tf_op jit(solution)/shard_map/mix_kernel/pallas_call | solution.py:41
  114.3 6.9 %all-to-all-start.3 = ((bf16[16,32,128]{2,1,0:T(8,128)(2,1)}), bf16[16,32,128]{2,1,0:T(8,128)(2,1)S(1)}, u32[]{:S(2)}, u32[]{:S(2)}) async-start(bf16[16,32,128]{2,1,0:T(8,128)(2,1)} %mix_kernel.1), calls=%async_computation.3 | async-start | bytes 262144 | tf_op jit(solution)/shard_map/all_to_all | solution.py:257
  121.3 6.4 %back_kernel.1 = (bf16[112,4096]{1,0:T(8,128)(2,1)}, bf16[112,512]{1,0:T(8,128)(2,1)}, bf16[112,512]{1,0:T(8,128)(2,1)}) custom-call(s32[2]{0:T(128)S(1)} %pad_add_fusion.1.me_ref, bf16[8,2,64,512]{3,2,1,0:T(8,128)(2,1)} %bitcast.17.own_ref, bf16[8,2,64,512]{3,2,1,0:T(8,128)(2,1)S(1)} %collective-permute-done.2.near_ref, ...), custom_call_target="tpu_custom_call" | custom-call | flops 1500000000 | bytes 8000000 | tf_op jit(solution)/shard_map/back_kernel/pallas_call | solution.py:347
  127.7 6.0 %all-to-all-done.3.got_ref = bf16[16,32,128]{2,1,0:T(8,128)(2,1)S(1)} async-done(((bf16[16,32,128]{2,1,0:T(8,128)(2,1)}), bf16[16,32,128]{2,1,0:T(8,128)(2,1)S(1)}, u32[]{:S(2)}, u32[]{:S(2)}) %all-to-all-start.3) | async-done | bytes 131104 | tf_op jit(solution)/shard_map/all_to_all | solution.py:257
  (31 shorter events, 10.2 us)
Async XLA Ops:
  0.6 0.7 copy-start.2
  1.3 0.7 copy-start.3
  3.0 28.9 %all-to-all-start = ((bf16[16,64,128]{2,1,0:T(8,128)(2,1)}), bf16[16,64,128]{2,1,0:T(8,128)(2,1)S(1)}, u32[]{:S(2)}, u32[]{:S(2)}) async-start(bf16[16,64,128]{2,1,0:T(8,128)(2,1)} %pack_kernel.1), calls=%async_computation | async-start | bytes 524288 | tf_op jit(solution)/shard_map/all_to_all | solution.py:294
  20.4 0.7 copy-start.9
  21.1 0.7 copy-start.10
  22.3 1.2 copy-start.4
  23.4 1.2 copy-start.5
  24.6 1.2 copy-start.6
  28.9 1.3 copy-start
  33.2 17.6 %all-to-all-start.1 = ((bf16[16,32,1024]{2,1,0:T(8,128)(2,1)}), bf16[16,32,1024]{2,1,0:T(8,128)(2,1)S(1)}, u32[]{:S(2)}, u32[]{:S(2)}) async-start(bf16[16,32,1024]{2,1,0:T(8,128)(2,1)} %bitcast.12), calls=%async_computation.1 | async-start | bytes 2097152 | tf_op jit(solution)/shard_map/all_to_all | solution.py:257
  50.8 13.9 %collective-permute-start = (bf16[8,2,32,1024]{3,2,1,0:T(8,128)(2,1)S(1)}, bf16[8,2,32,1024]{3,2,1,0:T(8,128)(2,1)S(1)}, u32[]{:S(2)}, u32[]{:S(2)}) collective-permute-start(bf16[8,2,32,1024]{3,2,1,0:T(8,128)(2,1)S(1)} %bitcast.33), channel_id=1, source_target_pairs={{0,1},{1,0},{2,3},{3,2},{4,5},{5,4},{6,7},{7,6},{8,9},{9,8},{10,11... | collective-permute-start | bytes 3145736 | tf_op jit(solution)/shard_map/ppermute | solution.py:252
  60.3 20.3 %all-to-all-start.4 = ((bf16[16,64,512]{2,1,0:T(8,128)(2,1)}), bf16[16,64,512]{2,1,0:T(8,128)(2,1)}, u32[]{:S(2)}, u32[]{:S(2)}) async-start(bf16[16,64,512]{2,1,0:T(8,128)(2,1)} %bitcast.16), calls=%async_computation.4 | async-start | bytes 2097152 | tf_op jit(solution)/shard_map/all_to_all | solution.py:257
  64.6 1.6 %copy-start.1 = (bf16[2,2,256,1024]{3,2,1,0:T(8,128)(2,1)S(1)}, bf16[2,2,256,1024]{3,2,1,0:T(8,128)(2,1)}, u32[]{:S(2)}) copy-start(bf16[2,2,256,1024]{3,2,1,0:T(8,128)(2,1)} %copy-done) | copy-start | bytes 6291460
  68.8 17.9 %collective-permute-start.1 = (bf16[8,2,32,1024]{3,2,1,0:T(8,128)(2,1)}, bf16[8,2,32,1024]{3,2,1,0:T(8,128)(2,1)S(1)}, u32[]{:S(2)}, u32[]{:S(2)}) collective-permute-start(bf16[8,2,32,1024]{3,2,1,0:T(8,128)(2,1)} %get-tuple-element.43), channel_id=1, source_target_pairs={{0,1},{1,0},{2,3},{3,2},{4,5},{5,4},{6,7},{7,6},{8,9},{9,8},{10,11... | collective-permute-start | bytes 3145736 | tf_op jit(solution)/shard_map/ppermute | solution.py:252
  80.5 28.6 %collective-permute-start.2 = (bf16[8,2,64,512]{3,2,1,0:T(8,128)(2,1)}, bf16[8,2,64,512]{3,2,1,0:T(8,128)(2,1)S(1)}, u32[]{:S(2)}, u32[]{:S(2)}) collective-permute-start(bf16[8,2,64,512]{3,2,1,0:T(8,128)(2,1)} %bitcast.17.own_ref), channel_id=1, source_target_pairs={{0,4},{4,0},{8,12},{12,8},{16,20},{20,16},{24,28},{28,24},{32,36},... | collective-permute-start | bytes 3145736 | tf_op jit(solution)/shard_map/ppermute | solution.py:344
  88.1 33.2 %copy-start.7 = (bf16[1,512,112]{1,2,0:T(8,128)(2,1)S(1)}, bf16[1,512,112]{1,2,0:T(8,128)(2,1)}, u32[]{:S(2)}) copy-start(bf16[1,512,112]{1,2,0:T(8,128)(2,1)} %param.20) | copy-start | bytes 344068
  88.1 33.2 %copy-start.8 = (bf16[1,512,112]{1,2,0:T(8,128)(2,1)S(1)}, bf16[1,512,112]{1,2,0:T(8,128)(2,1)}, u32[]{:S(2)}) copy-start(bf16[1,512,112]{1,2,0:T(8,128)(2,1)} %param.21) | copy-start | bytes 344068
  88.1 24.8 %all-to-all-start.2 = ((bf16[16,32,1024]{2,1,0:T(8,128)(2,1)}), bf16[16,32,1024]{2,1,0:T(8,128)(2,1)S(1)}, u32[]{:S(2)}, u32[]{:S(2)}) async-start(bf16[16,32,1024]{2,1,0:T(8,128)(2,1)} %bitcast.14), calls=%async_computation.2 | async-start | bytes 2097152 | tf_op jit(solution)/shard_map/all_to_all | solution.py:257
  93.1 28.1 %collective-permute-start.3 = (bf16[8,2,64,512]{3,2,1,0:T(8,128)(2,1)}, bf16[8,2,64,512]{3,2,1,0:T(8,128)(2,1)}, u32[]{:S(2)}, u32[]{:S(2)}) collective-permute-start(bf16[8,2,64,512]{3,2,1,0:T(8,128)(2,1)} %bitcast.17.own_ref), channel_id=1, source_target_pairs={{0,1},{1,0},{2,3},{3,2},{4,5},{5,4},{6,7},{7,6},{8,9},{9,8},{10,11... | collective-permute-start | bytes 3145736 | tf_op jit(solution)/shard_map/ppermute | solution.py:252
  109.2 12.1 %collective-permute-start.4 = (bf16[8,2,64,512]{3,2,1,0:T(8,128)(2,1)S(1)}, bf16[8,2,64,512]{3,2,1,0:T(8,128)(2,1)}, u32[]{:S(2)}, u32[]{:S(2)}) collective-permute-start(bf16[8,2,64,512]{3,2,1,0:T(8,128)(2,1)S(1)} %collective-permute-done.2.near_ref), channel_id=1, source_target_pairs={{0,1},{1,0},{2,3},{3,2},{4,5},{5,4},{6,7},{7,6},{8,9},{9,8},{10,11... | collective-permute-start | bytes 3145736 | tf_op jit(solution)/shard_map/ppermute | solution.py:252
  114.3 19.3 %all-to-all-start.3 = ((bf16[16,32,128]{2,1,0:T(8,128)(2,1)}), bf16[16,32,128]{2,1,0:T(8,128)(2,1)S(1)}, u32[]{:S(2)}, u32[]{:S(2)}) async-start(bf16[16,32,128]{2,1,0:T(8,128)(2,1)} %mix_kernel.1), calls=%async_computation.3 | async-start | bytes 262144 | tf_op jit(solution)/shard_map/all_to_all | solution.py:257

commit v8 on v7

--- a/solution.py
+++ b/solution.py
@@ -145,21 +145,20 @@
     weight_a_ref[...] = jnp.broadcast_to(weight, weight_a_ref.shape)
 
 
-def rows_new_kernel(picks_ref, got_ref, out_ref):
-    experts, _, slots, width = out_ref.shape
-    x = got_ref[:, 0:F, :].reshape(-1, picks_ref.shape[2])
+def rows_kernel(picks_b_ref, picks_a_ref, weight_ref, got_ref, out_ref):
+    experts, _, both, width = out_ref.shape
+    slots, half = both // 2, width // 2
+    x = got_ref[:, 0:F, :].reshape(-1, picks_b_ref.shape[2])
     for h in range(2):
-        block = dot_last(picks_ref[h], x).astype(BF).reshape(experts, slots, -1)
-        for xh in range(2):
-            out_ref[:, xh, :, h * (width // 2) : (h + 1) * (width // 2)] = block
-
-
-def rows_old_kernel(picks_ref, weight_ref, got_ref, out_ref):
-    g = got_ref[:, F : 2 * F, :].reshape(-1, picks_ref.shape[1])
-    block = (dot_last(picks_ref[...], g) * weight_ref[:, 0:1]).astype(BF)
-    experts, _, slots, width = out_ref.shape
+        block = dot_last(picks_b_ref[h], x).astype(BF).reshape(experts, slots, half)
+        for xh in range(2):
+            out_ref[:, xh, :slots, h * half : (h + 1) * half] = block
+    g = got_ref[:, F : 2 * F, :].reshape(-1, picks_a_ref.shape[1])
+    block = (dot_last(picks_a_ref[...], g) * weight_ref[:, 0:1]).astype(BF)
+    block = block.reshape(experts, 2 * slots, half)
     for xh in range(2):
-        out_ref[:, xh] = block.reshape(experts, slots, width)
+        out_ref[:, xh, slots:, :half] = block[:, :slots]
+        out_ref[:, xh, slots:, half:] = block[:, slots:]
 
 
 def up_kernel(own_ref, other_ref, gu_ref, dn_ref, hidden_ref, out_ref):
@@ -212,18 +211,24 @@
     return ref[:, xh].reshape(-1, ref.shape[3])
 
 
+def half_rows_of(ref, xh):
+    half = ref.shape[3] // 2
+    both = jnp.concatenate([ref[:, xh, :, :half], ref[:, xh, :, half:]], axis=1)
+    return both.reshape(-1, half)
+
+
 def back_kernel(
     me_ref, own_ref, near_ref, other_ref, other_near_ref, dn_ref, gate_ref, up_ref,
     down_ref, dg_ref, du_ref, held,
 ):
-    width = own_ref.shape[3]
+    width = own_ref.shape[3] // 2
     mine = pl.ds(pl.multiple_of(me_ref[1] * width, width), width)
     rest = pl.ds(pl.multiple_of((1 - me_ref[1]) * width, width), width)
     parts = ((0, mine, own_ref), (1, mine, other_ref), (0, rest, near_ref), (1, rest, other_near_ref))
     total = None
     for o, lanes, ref in parts:
         for xh in range(2):
-            term = dot_last(dn_ref[o, xh, :, lanes], rows_of(ref, xh))
+            term = dot_last(dn_ref[o, xh, :, lanes], half_rows_of(ref, xh))
             total = term if total is None else total + term
     gate, up = gate_ref[...].astype(F32), up_ref[...].astype(F32)
     grad = total[: gate.shape[0]]
@@ -234,7 +239,7 @@
     hidden = (active * up).astype(BF)
     for o, lanes, ref in parts:
         for xh in range(2):
-            held[o, xh, :, lanes] = dot(hidden, rows_of(ref, xh)).astype(BF)
+            held[o, xh, :, lanes] = dot(hidden, half_rows_of(ref, xh)).astype(BF)
     order = lane_order(me_ref[0])
     for xh in range(2):
         for zq in range(4):
@@ -322,11 +327,9 @@
     )
 
     rows_b = shape(experts, 2, CAP_B, 1024)
-    own = exchange(call(rows_new_kernel, rows_b, picks_b, got), PLANE)
-    rows_a = shape(experts, 2, CAP_A, 512)
-    sent_a = call(rows_old_kernel, rows_a, picks_a, weight_a, got)
-    own, sent_a = lax.optimization_barrier((own, sent_a))
-    own_a = exchange(sent_a, PLANE)
+    sent = call(rows_kernel, shape(experts, 2, 2 * CAP_B, 1024), picks_b, picks_a, weight_a, got)
+    arrived = exchange(sent, PLANE)
+    own, own_a = arrived[:, :, :CAP_B], arrived[:, :, CAP_B:]
 
     hidden, partial = call(
         up_kernel,

time: 137 us -> 136 us (level)
  blocking collectives: 0 us -> 27.2 us
  waiting for transfers between devices: 39.2 us -> 25.3 us
  starting transfers between devices: 64 us -> 51.1 us
  Pallas kernels: 19.5 us -> 16.4 us
  local copies, waits for them, and re-layouts: 9.25 us -> 11.3 us
    all_to_all x0 -> x1, blocking collectives: none -> 27.2 us  [exchange(): return lax.all_to_all(peers, axes, 0, 0, tiled=True).reshape(array.shape)]
    all_to_all x4 -> x2, waiting for transfers between devices: 25.4 us -> 6 us  [exchange(): return lax.all_to_all(peers, axes, 0, 0, tiled=True).reshape(array.shape)]
    all_to_all x4 -> x2, starting transfers between devices: 23 us -> 10.1 us  [exchange(): return lax.all_to_all(peers, axes, 0, 0, tiled=True).reshape(array.shape)]
    ppermute x1, waiting for transfers between devices: 12.2 us -> 16 us  [per_device(): lax.ppermute(own_a, Z, [(z, z ^ 1) for z in range(lax.axis_size(Z))])]
    pallas_call x8 -> x7, Pallas kernels: 12.2 us -> 9.08 us  [call(): pl.pallas_call(body, out_shape=outs, in_specs=[smem] * scalars + [vmem] *...]
    ppermute x4, waiting for transfers between devices: 0.01 us -> 2.27 us  [other_core(): return lax.ppermute(array, CORE, [(0, 1), (1, 0)])]
    ppermute x1, starting transfers between devices: 6.17 us -> 7.81 us  [per_device(): lax.ppermute(own_a, Z, [(z, z ^ 1) for z in range(lax.axis_size(Z))])]
    ppermute x4, starting transfers between devices: 19 us -> 17.5 us  [other_core(): return lax.ppermute(array, CORE, [(0, 1), (1, 0)])]
  transfers between devices with their start and end apart: 10 -> 8, of which waited for: 5 -> 4; matrix products, arithmetic and copies ran while one was open for 1% -> 1% of each run, Pallas kernels for 12% -> 9%
where the time goes in v8:
time: 136 us; the launch traced here: 134 us
  starting transfers between devices  51.1 us (38%)
  blocking collectives  27.2 us (20%)
  waiting for transfers between devices  25.3 us (19%)
  Pallas kernels  16.4 us (12%)
  local copies, waits for them, and re-layouts  11.3 us (8%)
  other arithmetic  1.73 us (1%)
    all_to_all x1, blocking collectives, exchange(): return lax.all_to_all(peers, axes, 0, 0, tiled=True).reshape(array.shape)  27.2 us
    ppermute x4, starting transfers between devices, other_core(): return lax.ppermute(array, CORE, [(0, 1), (1, 0)])  17.5 us
    ppermute x1, waiting for transfers between devices, per_device(): lax.ppermute(own_a, Z, [(z, z ^ 1) for z in range(lax.axis_size(Z))])  16 us
    all_to_all x1, starting transfers between devices, per_device(): got = lax.all_to_all(packed, Z, 0, 0, tiled=True)  15.8 us
    unnamed x30, local copies, waits for them, and re-layouts  10.2 us
    all_to_all x2, starting transfers between devices, exchange(): return lax.all_to_all(peers, axes, 0, 0, tiled=True).reshape(array.shape)  10.1 us
    pallas_call x7, Pallas kernels, call(): pl.pallas_call(body, out_shape=outs, in_specs=[smem] * scalars + [vmem] *...  9.08 us
    ppermute x1, starting transfers between devices, per_device(): lax.ppermute(own_a, Z, [(z, z ^ 1) for z in range(lax.axis_size(Z))])  7.81 us
  transfers between devices with their start and end apart: 8, of which 4 were waited for; matrix products, arithmetic and copies ran while one was open for 1% of the time, Pallas kernels for 9%

profile of v8, /device:TPU:1, one launch (start us, length us, event | category | flops | bytes accessed | tf_op | source)
XLA Modules:
  0.0 133.9 jit_solution(4191874540519236650)
XLA Ops:
  2.1 0.9 pack_kernel.1
  3.0 15.8 %all-to-all-start = ((bf16[16,64,128]{2,1,0:T(8,128)(2,1)}), bf16[16,64,128]{2,1,0:T(8,128)(2,1)S(1)}, u32[]{:S(2)}, u32[]{:S(2)}) async-start(bf16[16,64,128]{2,1,0:T(8,128)(2,1)} %pack_kernel.1), calls=%async_computation | async-start | bytes 524288 | tf_op jit(solution)/shard_map/all_to_all | solution.py:299
  24.3 1.2 copy-done.6
  25.4 1.2 copy-done.7
  26.6 1.2 copy-done.8
  27.8 3.1 %weights_kernel.1 = (bf16[2,2,256,1024]{3,2,1,0:T(8,128)(2,1)S(1)}, bf16[2,2,128,1024]{3,2,1,0:T(8,128)(2,1)S(1)}) custom-call(s32[2]{0:T(128)S(1)} %pad_add_fusion.1.me_ref, bf16[112,4096]{1,0:T(8,128)(2,1)S(1)} %bitcast.34, bf16[112,4096]{1,0:T(8,128)(2,1)S(1)} %bitcast.35, bf16[112,4096]{1,0:T(8,128)(2,1)S(1)} %bitcast.36), custom_call_target="tpu_custom_call" | custom-call | flops 1400000000 | bytes 6000000 | tf_op jit(solution)/shard_map/weights_kernel/pallas_call | solution.py:41
  30.9 1.0 all-to-all-done.got_ref
  31.9 0.9 copy-done.1
  34.2 27.2 %all_to_all.20 = bf16[16,64,1024]{2,1,0:T(8,128)(2,1)S(1)} all-to-all(bf16[16,64,1024]{2,1,0:T(8,128)(2,1)S(1)} %bitcast.31), channel_id=1, replica_groups=mesh['expert_0'=4,'expert_1'=2,'dp_0'=16,'dp_1'=2,'dp_2'=2] {'expert_0',..., dimensions={0} | all-to-all | bytes 4194304 | tf_op jit(solution)/shard_map/all_to_all | solution.py:262
  61.3 1.2 fusion
  62.5 10.2 %collective-permute-start = (bf16[8,2,32,1024]{3,2,1,0:T(8,128)(2,1)S(1)}, bf16[8,2,32,1024]{3,2,1,0:T(8,128)(2,1)S(1)}, u32[]{:S(2)}, u32[]{:S(2)}) collective-permute-start(bf16[8,2,32,1024]{3,2,1,0:T(8,128)(2,1)S(1)} %get-tuple-element.49.own_ref), channel_id=1, source_target_pairs={{0,1},{1,0},{2,3},{3,2},{4,5},{5,4},{6,7},{7,6},{8,9},{9,8},{10,11... | collective-permute-start | bytes 3145736 | tf_op jit(solution)/shard_map/ppermute | solution.py:257
  72.7 2.3 %collective-permute-done.other_ref = bf16[8,2,32,1024]{3,2,1,0:T(8,128)(2,1)S(1)} collective-permute-done((bf16[8,2,32,1024]{3,2,1,0:T(8,128)(2,1)S(1)}, bf16[8,2,32,1024]{3,2,1,0:T(8,128)(2,1)S(1)}, u32[]{:S(2)}, u32[]{:S(2)}) %collective-permute-start) | collective-permute-done | bytes 1048608 | tf_op jit(solution)/shard_map/ppermute | solution.py:257
  75.0 1.6 %up_kernel.1 = (bf16[256,128]{1,0:T(8,128)(2,1)S(1)}, bf16[8,2,32,1024]{3,2,1,0:T(8,128)(2,1)S(1)}) custom-call(bf16[8,2,32,1024]{3,2,1,0:T(8,128)(2,1)S(1)} %get-tuple-element.49.own_ref, bf16[8,2,32,1024]{3,2,1,0:T(8,128)(2,1)S(1)} %collective-permute-done.other_ref, bf16[2,2,256,1024]{3,2,1,0:T(8,128)(2,1)S(1)} %get-tuple-element.37.gu_ref, ...), custom_call_target="tpu_custom_call" | custom-call | flops 800000000 | bytes 4000000 | tf_op jit(solution)/shard_map/up_kernel/pallas_call | solution.py:41
  76.6 2.3 %collective-permute-start.1 = (bf16[8,2,32,1024]{3,2,1,0:T(8,128)(2,1)S(1)}, bf16[8,2,32,1024]{3,2,1,0:T(8,128)(2,1)S(1)}, u32[]{:S(2)}, u32[]{:S(2)}) collective-permute-start(bf16[8,2,32,1024]{3,2,1,0:T(8,128)(2,1)S(1)} %get-tuple-element.40), channel_id=1, source_target_pairs={{0,1},{1,0},{2,3},{3,2},{4,5},{5,4},{6,7},{7,6},{8,9},{9,8},{10,11... | collective-permute-start | bytes 3145736 | tf_op jit(solution)/shard_map/ppermute | solution.py:257
  78.9 7.8 %collective-permute-start.2 = (bf16[8,2,32,1024]{3,2,1,0:T(8,128)(2,1)}, bf16[8,2,32,1024]{3,2,1,0:T(8,128)(2,1)S(1)}, u32[]{:S(2)}, u32[]{:S(2)}) collective-permute-start(bf16[8,2,32,1024]{3,2,1,0:T(8,128)(2,1)} %get-tuple-element.48.own_ref), channel_id=1, source_target_pairs={{0,4},{4,0},{8,12},{12,8},{16,20},{20,16},{24,28},{28,24},{32,36},... | collective-permute-start | bytes 3145736 | tf_op jit(solution)/shard_map/ppermute | solution.py:347
  86.7 1.4 %down_kernel.1 = bf16[8,2,32,1024]{3,2,1,0:T(8,128)(2,1)} custom-call(bf16[256,128]{1,0:T(8,128)(2,1)S(1)} %get-tuple-element.39.hidden_ref, bf16[2,2,128,1024]{3,2,1,0:T(8,128)(2,1)S(1)} %get-tuple-element.38.dn_ref, bf16[8,2,32,1024]{3,2,1,0:T(8,128)(2,1)S(1)} %collective-permute-done.1.arrived_ref), custom_call_target="tpu_custom_call" | custom-call | flops 200000000 | bytes 1000000 | tf_op jit(solution)/shard_map/down_kernel/pallas_call | solution.py:41
  88.1 3.8 %all-to-all-start.2 = ((bf16[16,32,1024]{2,1,0:T(8,128)(2,1)}), bf16[16,32,1024]{2,1,0:T(8,128)(2,1)S(1)}, u32[]{:S(2)}, u32[]{:S(2)}) async-start(bf16[16,32,1024]{2,1,0:T(8,128)(2,1)} %bitcast.14), calls=%async_computation.2 | async-start | bytes 2097152 | tf_op jit(solution)/shard_map/all_to_all | solution.py:262
  91.9 2.3 %collective-permute-start.3 = (bf16[8,2,32,1024]{3,2,1,0:T(8,128)(2,1)}, bf16[8,2,32,1024]{3,2,1,0:T(8,128)(2,1)}, u32[]{:S(2)}, u32[]{:S(2)}) collective-permute-start(bf16[8,2,32,1024]{3,2,1,0:T(8,128)(2,1)} %get-tuple-element.48.own_ref), channel_id=1, source_target_pairs={{0,1},{1,0},{2,3},{3,2},{4,5},{5,4},{6,7},{7,6},{8,9},{9,8},{10,11... | collective-permute-start | bytes 3145736 | tf_op jit(solution)/shard_map/ppermute | solution.py:257
  94.3 16.0 %collective-permute-done.2.near_ref = bf16[8,2,32,1024]{3,2,1,0:T(8,128)(2,1)S(1)} collective-permute-done((bf16[8,2,32,1024]{3,2,1,0:T(8,128)(2,1)}, bf16[8,2,32,1024]{3,2,1,0:T(8,128)(2,1)S(1)}, u32[]{:S(2)}, u32[]{:S(2)}) %collective-permute-start.2) | collective-permute-done | bytes 1048608 | tf_op jit(solution)/shard_map/ppermute | solution.py:347
  110.3 2.6 %collective-permute-start.4 = (bf16[8,2,32,1024]{3,2,1,0:T(8,128)(2,1)S(1)}, bf16[8,2,32,1024]{3,2,1,0:T(8,128)(2,1)}, u32[]{:S(2)}, u32[]{:S(2)}) collective-permute-start(bf16[8,2,32,1024]{3,2,1,0:T(8,128)(2,1)S(1)} %collective-permute-done.2.near_ref), channel_id=1, source_target_pairs={{0,1},{1,0},{2,3},{3,2},{4,5},{5,4},{6,7},{7,6},{8,9},{9,8},{10,11... | collective-permute-start | bytes 3145736 | tf_op jit(solution)/shard_map/ppermute | solution.py:257
  112.9 1.4 %mix_kernel.1 = bf16[16,32,128]{2,1,0:T(8,128)(2,1)} custom-call(bf16[3,64,256]{2,1,0:T(8,128)(2,1)S(1)} %copy-done.14, bf16[8,2,32,1024]{3,2,1,0:T(8,128)(2,1)S(1)} %bitcast.32), custom_call_target="tpu_custom_call" | custom-call | flops 400000000 | bytes 1000000 | tf_op jit(solution)/shard_map/mix_kernel/pallas_call | solution.py:41
  114.3 6.3 %all-to-all-start.3 = ((bf16[16,32,128]{2,1,0:T(8,128)(2,1)}), bf16[16,32,128]{2,1,0:T(8,128)(2,1)S(1)}, u32[]{:S(2)}, u32[]{:S(2)}) async-start(bf16[16,32,128]{2,1,0:T(8,128)(2,1)} %mix_kernel.1), calls=%async_computation.3 | async-start | bytes 262144 | tf_op jit(solution)/shard_map/all_to_all | solution.py:262
  120.7 6.4 %back_kernel.1 = (bf16[112,4096]{1,0:T(8,128)(2,1)}, bf16[112,512]{1,0:T(8,128)(2,1)}, bf16[112,512]{1,0:T(8,128)(2,1)}) custom-call(s32[2]{0:T(128)S(1)} %pad_add_fusion.1.me_ref, bf16[8,2,32,1024]{3,2,1,0:T(8,128)(2,1)} %get-tuple-element.48.own_ref, bf16[8,2,32,1024]{3,2,1,0:T(8,128)(2,1)S(1)} %collective-permute-done.2.near_ref, ...), custom_call_target="tpu_custom_call" | custom-call | flops 1500000000 | bytes 8000000 | tf_op jit(solution)/shard_map/back_kernel/pallas_call | solution.py:350
  127.1 6.0 %all-to-all-done.3.got_ref = bf16[16,32,128]{2,1,0:T(8,128)(2,1)S(1)} async-done(((bf16[16,32,128]{2,1,0:T(8,128)(2,1)}), bf16[16,32,128]{2,1,0:T(8,128)(2,1)S(1)}, u32[]{:S(2)}, u32[]{:S(2)}) %all-to-all-start.3) | async-done | bytes 131104 | tf_op jit(solution)/shard_map/all_to_all | solution.py:262
  (36 shorter events, 9.1 us)
Async XLA Ops:
  0.6 0.7 copy-start.4
  1.3 0.7 copy-start.5
  3.0 28.9 %all-to-all-start = ((bf16[16,64,128]{2,1,0:T(8,128)(2,1)}), bf16[16,64,128]{2,1,0:T(8,128)(2,1)S(1)}, u32[]{:S(2)}, u32[]{:S(2)}) async-start(bf16[16,64,128]{2,1,0:T(8,128)(2,1)} %pack_kernel.1), calls=%async_computation | async-start | bytes 524288 | tf_op jit(solution)/shard_map/all_to_all | solution.py:299
  20.4 0.7 copy-start.11
  21.1 0.7 copy-start.12
  22.2 0.7 copy-start
  22.9 0.6 copy-start.2
  23.5 0.6 copy-start.13
  24.3 1.2 copy-start.6
  25.4 1.2 copy-start.7
  26.6 1.2 copy-start.8
  31.9 1.0 copy-start.1
  32.8 0.9 copy-start.3
  62.5 12.5 %collective-permute-start = (bf16[8,2,32,1024]{3,2,1,0:T(8,128)(2,1)S(1)}, bf16[8,2,32,1024]{3,2,1,0:T(8,128)(2,1)S(1)}, u32[]{:S(2)}, u32[]{:S(2)}) collective-permute-start(bf16[8,2,32,1024]{3,2,1,0:T(8,128)(2,1)S(1)} %get-tuple-element.49.own_ref), channel_id=1, source_target_pairs={{0,1},{1,0},{2,3},{3,2},{4,5},{5,4},{6,7},{7,6},{8,9},{9,8},{10,11... | collective-permute-start | bytes 3145736 | tf_op jit(solution)/shard_map/ppermute | solution.py:257
  76.6 10.1 %collective-permute-start.1 = (bf16[8,2,32,1024]{3,2,1,0:T(8,128)(2,1)S(1)}, bf16[8,2,32,1024]{3,2,1,0:T(8,128)(2,1)S(1)}, u32[]{:S(2)}, u32[]{:S(2)}) collective-permute-start(bf16[8,2,32,1024]{3,2,1,0:T(8,128)(2,1)S(1)} %get-tuple-element.40), channel_id=1, source_target_pairs={{0,1},{1,0},{2,3},{3,2},{4,5},{5,4},{6,7},{7,6},{8,9},{9,8},{10,11... | collective-permute-start | bytes 3145736 | tf_op jit(solution)/shard_map/ppermute | solution.py:257
  78.9 31.4 %collective-permute-start.2 = (bf16[8,2,32,1024]{3,2,1,0:T(8,128)(2,1)}, bf16[8,2,32,1024]{3,2,1,0:T(8,128)(2,1)S(1)}, u32[]{:S(2)}, u32[]{:S(2)}) collective-permute-start(bf16[8,2,32,1024]{3,2,1,0:T(8,128)(2,1)} %get-tuple-element.48.own_ref), channel_id=1, source_target_pairs={{0,4},{4,0},{8,12},{12,8},{16,20},{20,16},{24,28},{28,24},{32,36},... | collective-permute-start | bytes 3145736 | tf_op jit(solution)/shard_map/ppermute | solution.py:347
  86.7 26.2 %copy-start.14 = (bf16[3,64,256]{2,1,0:T(8,128)(2,1)S(1)}, bf16[3,64,256]{2,1,0:T(8,128)(2,1)}, u32[]{:S(2)}) copy-start(bf16[3,64,256]{2,1,0:T(8,128)(2,1)} %copy-done.13) | copy-start | bytes 294916
  88.1 32.5 %copy-start.9 = (bf16[1,512,112]{1,2,0:T(8,128)(2,1)S(1)}, bf16[1,512,112]{1,2,0:T(8,128)(2,1)}, u32[]{:S(2)}) copy-start(bf16[1,512,112]{1,2,0:T(8,128)(2,1)} %param.20) | copy-start | bytes 344068
  88.1 32.5 %copy-start.10 = (bf16[1,512,112]{1,2,0:T(8,128)(2,1)S(1)}, bf16[1,512,112]{1,2,0:T(8,128)(2,1)}, u32[]{:S(2)}) copy-start(bf16[1,512,112]{1,2,0:T(8,128)(2,1)} %param.21) | copy-start | bytes 344068
  88.1 24.8 %all-to-all-start.2 = ((bf16[16,32,1024]{2,1,0:T(8,128)(2,1)}), bf16[16,32,1024]{2,1,0:T(8,128)(2,1)S(1)}, u32[]{:S(2)}, u32[]{:S(2)}) async-start(bf16[16,32,1024]{2,1,0:T(8,128)(2,1)} %bitcast.14), calls=%async_computation.2 | async-start | bytes 2097152 | tf_op jit(solution)/shard_map/all_to_all | solution.py:262
  91.9 28.7 %collective-permute-start.3 = (bf16[8,2,32,1024]{3,2,1,0:T(8,128)(2,1)}, bf16[8,2,32,1024]{3,2,1,0:T(8,128)(2,1)}, u32[]{:S(2)}, u32[]{:S(2)}) collective-permute-start(bf16[8,2,32,1024]{3,2,1,0:T(8,128)(2,1)} %get-tuple-element.48.own_ref), channel_id=1, source_target_pairs={{0,1},{1,0},{2,3},{3,2},{4,5},{5,4},{6,7},{7,6},{8,9},{9,8},{10,11... | collective-permute-start | bytes 3145736 | tf_op jit(solution)/shard_map/ppermute | solution.py:257
  110.3 10.3 %collective-permute-start.4 = (bf16[8,2,32,1024]{3,2,1,0:T(8,128)(2,1)S(1)}, bf16[8,2,32,1024]{3,2,1,0:T(8,128)(2,1)}, u32[]{:S(2)}, u32[]{:S(2)}) collective-permute-start(bf16[8,2,32,1024]{3,2,1,0:T(8,128)(2,1)S(1)} %collective-permute-done.2.near_ref), channel_id=1, source_target_pairs={{0,1},{1,0},{2,3},{3,2},{4,5},{5,4},{6,7},{7,6},{8,9},{9,8},{10,11... | collective-permute-start | bytes 3145736 | tf_op jit(solution)/shard_map/ppermute | solution.py:257
  114.3 18.8 %all-to-all-start.3 = ((bf16[16,32,128]{2,1,0:T(8,128)(2,1)}), bf16[16,32,128]{2,1,0:T(8,128)(2,1)S(1)}, u32[]{:S(2)}, u32[]{:S(2)}) async-start(bf16[16,32,128]{2,1,0:T(8,128)(2,1)} %mix_kernel.1), calls=%async_computation.3 | async-start | bytes 262144 | tf_op jit(solution)/shard_map/all_to_all | solution.py:262

commit v9 on v8

--- a/solution.py
+++ b/solution.py
@@ -117,20 +117,19 @@
     return named & (before == slot.astype(F32)), first, second
 
 
-def tables_kernel(
-    routes_b_ref, gates_b_ref, routes_a_ref, gates_a_ref, picks_b_ref, mix_ref, picks_a_ref, weight_a_ref
-):
-    def weights(hit, first, second, gates):
-        named = jnp.where(first, gates[0:1, :], 0.0) + jnp.where(second, gates[1:2, :], 0.0)
-        return jnp.where(hit, named, 0.0)
-
-    routes, gates = routes_b_ref[...], gates_b_ref[...]
+def named_weights(hit, first, second, gates):
+    named = jnp.where(first, gates[0:1, :], 0.0) + jnp.where(second, gates[1:2, :], 0.0)
+    return jnp.where(hit, named, 0.0)
+
+
+def tables_kernel(routes_ref, gates_ref, picks_ref, mix_ref):
+    routes, gates = routes_ref[...], gates_ref[...]
     toks = routes.shape[1] // 2
-    hit, first, second = placed(routes, picks_b_ref.shape[1], CAP_B, toks)
+    hit, first, second = placed(routes, picks_ref.shape[1], CAP_B, toks)
     lane = iota(hit.shape, 1) // toks
     for h in range(2):
-        picks_b_ref[h] = jnp.where(hit & (lane == h), 1.0, 0.0).astype(BF)
-    weight = weights(hit, first, second, gates).T[:toks]
+        picks_ref[h] = jnp.where(hit & (lane == h), 1.0, 0.0).astype(BF)
+    weight = named_weights(hit, first, second, gates).T[:toks]
     high = weight.astype(BF)
     rest = weight - high.astype(F32)
     middle = rest.astype(BF)
@@ -138,23 +137,21 @@
     mix_ref[1] = middle
     mix_ref[2] = (rest - middle.astype(F32)).astype(BF)
 
-    routes, gates = routes_a_ref[...], gates_a_ref[...]
-    hit, first, second = placed(routes, picks_a_ref.shape[0], CAP_A, routes.shape[1])
-    picks_a_ref[...] = jnp.where(hit, 1.0, 0.0).astype(BF)
-    weight = jnp.sum(weights(hit, first, second, gates), axis=1, keepdims=True)
-    weight_a_ref[...] = jnp.broadcast_to(weight, weight_a_ref.shape)
-
-
-def rows_kernel(picks_b_ref, picks_a_ref, weight_ref, got_ref, out_ref):
+
+def rows_kernel(picks_ref, routes_ref, gates_ref, got_ref, out_ref):
     experts, _, both, width = out_ref.shape
     slots, half = both // 2, width // 2
-    x = got_ref[:, 0:F, :].reshape(-1, picks_b_ref.shape[2])
+    x = got_ref[:, 0:F, :].reshape(-1, picks_ref.shape[2])
     for h in range(2):
-        block = dot_last(picks_b_ref[h], x).astype(BF).reshape(experts, slots, half)
+        block = dot_last(picks_ref[h], x).astype(BF).reshape(experts, slots, half)
         for xh in range(2):
             out_ref[:, xh, :slots, h * half : (h + 1) * half] = block
-    g = got_ref[:, F : 2 * F, :].reshape(-1, picks_a_ref.shape[1])
-    block = (dot_last(picks_a_ref[...], g) * weight_ref[:, 0:1]).astype(BF)
+    routes, gates = routes_ref[...], gates_ref[...]
+    toks = routes.shape[1]
+    hit, first, second = placed(routes, experts * 2 * slots, 2 * slots, toks)
+    weight = jnp.sum(named_weights(hit, first, second, gates), axis=1, keepdims=True)
+    g = got_ref[:, F : 2 * F, :].reshape(-1, toks)
+    block = (dot_last(jnp.where(hit, 1.0, 0.0).astype(BF), g) * weight).astype(BF)
     block = block.reshape(experts, 2 * slots, half)
     for xh in range(2):
         out_ref[:, xh, slots:, :half] = block[:, :slots]
@@ -185,15 +182,12 @@
 
 def mix_kernel(mix_ref, got_ref, out_ref):
     width = got_ref.shape[3] // 2
-    rows = [rows_of(got_ref, xh) for xh in range(2)]
+    parts, toks, rows = mix_ref.shape
+    mix = mix_ref[...].reshape(parts * toks, rows)
     halves = []
     for h in range(2):
-        total = None
-        for xh in range(2):
-            for part in range(3):
-                term = dot(mix_ref[part], rows[xh][:, h * width : (h + 1) * width])
-                total = term if total is None else total + term
-        halves.append(total)
+        total = sum(dot(mix, rows_of(got_ref, xh)[:, h * width : (h + 1) * width]) for xh in range(2))
+        halves.append(total[:toks] + total[toks : 2 * toks] + total[2 * toks :])
     mixed = jnp.concatenate(halves, axis=0).T.astype(BF)
     out_ref[...] = mixed.reshape(out_ref.shape)
 
@@ -309,25 +303,20 @@
         moved=6 * 10**6,
     )
 
-    picks_b, mix, picks_a, weight_a = call(
+    picks, mix = call(
         tables_kernel,
-        (
-            shape(2, rows_new, 128),
-            shape(3, x_new.shape[0], rows_new),
-            shape(rows_old, 128),
-            shape(rows_old, 128, dtype=F32),
-        ),
+        (shape(2, rows_new, 128), shape(3, x_new.shape[0], rows_new)),
         routes_b,
         gates_b,
-        routes_a,
-        gates_a,
-    )
-    got, gate_up, down, picks_b, mix, picks_a, weight_a = lax.optimization_barrier(
-        (got, gate_up, down, picks_b, mix, picks_a, weight_a)
+    )
+    got, gate_up, down, picks, mix, routes_a, gates_a = lax.optimization_barrier(
+        (got, gate_up, down, picks, mix, routes_a, gates_a)
     )
 
     rows_b = shape(experts, 2, CAP_B, 1024)
-    sent = call(rows_kernel, shape(experts, 2, 2 * CAP_B, 1024), picks_b, picks_a, weight_a, got)
+    sent = call(
+        rows_kernel, shape(experts, 2, 2 * CAP_B, 1024), picks, routes_a, gates_a, got
+    )
     arrived = exchange(sent, PLANE)
     own, own_a = arrived[:, :, :CAP_B], arrived[:, :, CAP_B:]
 

time: 136 us -> 134 us (0.985)
  local copies, waits for them, and re-layouts: 11.3 us -> 6.81 us
  waiting for transfers between devices: 25.3 us -> 28.2 us
    unnamed x30 -> x22, local copies, waits for them, and re-layouts: 10.2 us -> 5.62 us
    all_to_all x1, waiting for transfers between devices: 1 us -> 3.88 us  [per_device(): got = lax.all_to_all(packed, Z, 0, 0, tiled=True)]
where the time goes in v9:
time: 134 us; the launch traced here: 132 us
  starting transfers between devices  51.1 us (38%)
  waiting for transfers between devices  28.2 us (21%)
  blocking collectives  27.1 us (20%)
  Pallas kernels  16.1 us (12%)
  local copies, waits for them, and re-layouts  6.81 us (5%)
  other arithmetic  1.73 us (1%)
    all_to_all x1, blocking collectives, exchange(): return lax.all_to_all(peers, axes, 0, 0, tiled=True).reshape(array.shape)  27.1 us
    ppermute x4, starting transfers between devices, other_core(): return lax.ppermute(array, CORE, [(0, 1), (1, 0)])  17.5 us
    ppermute x1, waiting for transfers between devices, per_device(): lax.ppermute(own_a, Z, [(z, z ^ 1) for z in range(lax.axis_size(Z))])  16 us
    all_to_all x1, starting transfers between devices, per_device(): got = lax.all_to_all(packed, Z, 0, 0, tiled=True)  15.8 us
    all_to_all x2, starting transfers between devices, exchange(): return lax.all_to_all(peers, axes, 0, 0, tiled=True).reshape(array.shape)  10.1 us
    pallas_call x7, Pallas kernels, call(): pl.pallas_call(body, out_shape=outs, in_specs=[smem] * scalars + [vmem] *...  8.82 us
    ppermute x1, starting transfers between devices, per_device(): lax.ppermute(own_a, Z, [(z, z ^ 1) for z in range(lax.axis_size(Z))])  7.82 us
    pallas_call x1, Pallas kernels, per_device(): pl.pallas_call(back_kernel, out_shape=(shape(hidden_units, 4096), shape(h...  6.39 us
  transfers between devices with their start and end apart: 8, of which 4 were waited for; matrix products, arithmetic and copies ran while one was open for 1% of the time, Pallas kernels for 9%

profile of v9, /device:TPU:1, one launch (start us, length us, event | category | flops | bytes accessed | tf_op | source)
XLA Modules:
  0.0 131.9 jit_solution(17279498175281571101)
XLA Ops:
  2.1 0.9 pack_kernel.1
  3.0 15.8 %all-to-all-start = ((bf16[16,64,128]{2,1,0:T(8,128)(2,1)}), bf16[16,64,128]{2,1,0:T(8,128)(2,1)S(1)}, u32[]{:S(2)}, u32[]{:S(2)}) async-start(bf16[16,64,128]{2,1,0:T(8,128)(2,1)} %pack_kernel.1), calls=%async_computation | async-start | bytes 524288 | tf_op jit(solution)/shard_map/all_to_all | solution.py:293
  18.8 0.8 pad_add_fusion.routes_ref
  21.4 1.2 copy-done.4
  22.5 1.2 copy-done.5
  23.7 1.2 copy-done.6
  24.9 3.1 %weights_kernel.1 = (bf16[2,2,256,1024]{3,2,1,0:T(8,128)(2,1)S(1)}, bf16[2,2,128,1024]{3,2,1,0:T(8,128)(2,1)S(1)}) custom-call(s32[2]{0:T(128)S(1)} %pad_add_fusion.1.me_ref, bf16[112,4096]{1,0:T(8,128)(2,1)S(1)} %bitcast.36, bf16[112,4096]{1,0:T(8,128)(2,1)S(1)} %bitcast.37, bf16[112,4096]{1,0:T(8,128)(2,1)S(1)} %bitcast.38), custom_call_target="tpu_custom_call" | custom-call | flops 1400000000 | bytes 6000000 | tf_op jit(solution)/shard_map/weights_kernel/pallas_call | solution.py:41
  28.0 3.9 %all-to-all-done.got_ref = bf16[16,64,128]{2,1,0:T(8,128)(2,1)S(1)} async-done(((bf16[16,64,128]{2,1,0:T(8,128)(2,1)}), bf16[16,64,128]{2,1,0:T(8,128)(2,1)S(1)}, u32[]{:S(2)}, u32[]{:S(2)}) %all-to-all-start) | async-done | bytes 262176 | tf_op jit(solution)/shard_map/all_to_all | solution.py:293
  32.5 27.1 %all_to_all.20 = bf16[16,64,1024]{2,1,0:T(8,128)(2,1)S(1)} all-to-all(bf16[16,64,1024]{2,1,0:T(8,128)(2,1)S(1)} %bitcast.31), channel_id=1, replica_groups=mesh['expert_0'=4,'expert_1'=2,'dp_0'=16,'dp_1'=2,'dp_2'=2] {'expert_0',..., dimensions={0} | all-to-all | bytes 4194304 | tf_op jit(solution)/shard_map/all_to_all | solution.py:256
  59.6 1.2 fusion
  60.8 10.2 %collective-permute-start = (bf16[8,2,32,1024]{3,2,1,0:T(8,128)(2,1)S(1)}, bf16[8,2,32,1024]{3,2,1,0:T(8,128)(2,1)S(1)}, u32[]{:S(2)}, u32[]{:S(2)}) collective-permute-start(bf16[8,2,32,1024]{3,2,1,0:T(8,128)(2,1)S(1)} %get-tuple-element.45.own_ref), channel_id=1, source_target_pairs={{0,1},{1,0},{2,3},{3,2},{4,5},{5,4},{6,7},{7,6},{8,9},{9,8},{10,11... | collective-permute-start | bytes 3145736 | tf_op jit(solution)/shard_map/ppermute | solution.py:251
  71.1 2.3 %collective-permute-done.other_ref = bf16[8,2,32,1024]{3,2,1,0:T(8,128)(2,1)S(1)} collective-permute-done((bf16[8,2,32,1024]{3,2,1,0:T(8,128)(2,1)S(1)}, bf16[8,2,32,1024]{3,2,1,0:T(8,128)(2,1)S(1)}, u32[]{:S(2)}, u32[]{:S(2)}) %collective-permute-start) | collective-permute-done | bytes 1048608 | tf_op jit(solution)/shard_map/ppermute | solution.py:251
  73.3 1.6 %up_kernel.1 = (bf16[256,128]{1,0:T(8,128)(2,1)S(1)}, bf16[8,2,32,1024]{3,2,1,0:T(8,128)(2,1)S(1)}) custom-call(bf16[8,2,32,1024]{3,2,1,0:T(8,128)(2,1)S(1)} %get-tuple-element.45.own_ref, bf16[8,2,32,1024]{3,2,1,0:T(8,128)(2,1)S(1)} %collective-permute-done.other_ref, bf16[2,2,256,1024]{3,2,1,0:T(8,128)(2,1)S(1)} %get-tuple-element.33.gu_ref, ...), custom_call_target="tpu_custom_call" | custom-call | flops 800000000 | bytes 4000000 | tf_op jit(solution)/shard_map/up_kernel/pallas_call | solution.py:41
  74.9 2.3 %collective-permute-start.1 = (bf16[8,2,32,1024]{3,2,1,0:T(8,128)(2,1)S(1)}, bf16[8,2,32,1024]{3,2,1,0:T(8,128)(2,1)S(1)}, u32[]{:S(2)}, u32[]{:S(2)}) collective-permute-start(bf16[8,2,32,1024]{3,2,1,0:T(8,128)(2,1)S(1)} %get-tuple-element.36), channel_id=1, source_target_pairs={{0,1},{1,0},{2,3},{3,2},{4,5},{5,4},{6,7},{7,6},{8,9},{9,8},{10,11... | collective-permute-start | bytes 3145736 | tf_op jit(solution)/shard_map/ppermute | solution.py:251
  77.2 7.8 %collective-permute-start.2 = (bf16[8,2,32,1024]{3,2,1,0:T(8,128)(2,1)}, bf16[8,2,32,1024]{3,2,1,0:T(8,128)(2,1)S(1)}, u32[]{:S(2)}, u32[]{:S(2)}) collective-permute-start(bf16[8,2,32,1024]{3,2,1,0:T(8,128)(2,1)} %get-tuple-element.44.own_ref), channel_id=1, source_target_pairs={{0,4},{4,0},{8,12},{12,8},{16,20},{20,16},{24,28},{28,24},{32,36},... | collective-permute-start | bytes 3145736 | tf_op jit(solution)/shard_map/ppermute | solution.py:336
  85.1 1.4 %down_kernel.1 = bf16[8,2,32,1024]{3,2,1,0:T(8,128)(2,1)} custom-call(bf16[256,128]{1,0:T(8,128)(2,1)S(1)} %get-tuple-element.35.hidden_ref, bf16[2,2,128,1024]{3,2,1,0:T(8,128)(2,1)S(1)} %get-tuple-element.34.dn_ref, bf16[8,2,32,1024]{3,2,1,0:T(8,128)(2,1)S(1)} %collective-permute-done.1.arrived_ref), custom_call_target="tpu_custom_call" | custom-call | flops 200000000 | bytes 1000000 | tf_op jit(solution)/shard_map/down_kernel/pallas_call | solution.py:41
  86.5 3.8 %all-to-all-start.2 = ((bf16[16,32,1024]{2,1,0:T(8,128)(2,1)}), bf16[16,32,1024]{2,1,0:T(8,128)(2,1)S(1)}, u32[]{:S(2)}, u32[]{:S(2)}) async-start(bf16[16,32,1024]{2,1,0:T(8,128)(2,1)} %bitcast.14), calls=%async_computation.2 | async-start | bytes 2097152 | tf_op jit(solution)/shard_map/all_to_all | solution.py:256
  90.2 2.3 %collective-permute-start.3 = (bf16[8,2,32,1024]{3,2,1,0:T(8,128)(2,1)}, bf16[8,2,32,1024]{3,2,1,0:T(8,128)(2,1)}, u32[]{:S(2)}, u32[]{:S(2)}) collective-permute-start(bf16[8,2,32,1024]{3,2,1,0:T(8,128)(2,1)} %get-tuple-element.44.own_ref), channel_id=1, source_target_pairs={{0,1},{1,0},{2,3},{3,2},{4,5},{5,4},{6,7},{7,6},{8,9},{9,8},{10,11... | collective-permute-start | bytes 3145736 | tf_op jit(solution)/shard_map/ppermute | solution.py:251
  92.6 16.0 %collective-permute-done.2.near_ref = bf16[8,2,32,1024]{3,2,1,0:T(8,128)(2,1)S(1)} collective-permute-done((bf16[8,2,32,1024]{3,2,1,0:T(8,128)(2,1)}, bf16[8,2,32,1024]{3,2,1,0:T(8,128)(2,1)S(1)}, u32[]{:S(2)}, u32[]{:S(2)}) %collective-permute-start.2) | collective-permute-done | bytes 1048608 | tf_op jit(solution)/shard_map/ppermute | solution.py:336
  108.6 2.6 %collective-permute-start.4 = (bf16[8,2,32,1024]{3,2,1,0:T(8,128)(2,1)S(1)}, bf16[8,2,32,1024]{3,2,1,0:T(8,128)(2,1)}, u32[]{:S(2)}, u32[]{:S(2)}) collective-permute-start(bf16[8,2,32,1024]{3,2,1,0:T(8,128)(2,1)S(1)} %collective-permute-done.2.near_ref), channel_id=1, source_target_pairs={{0,1},{1,0},{2,3},{3,2},{4,5},{5,4},{6,7},{7,6},{8,9},{9,8},{10,11... | collective-permute-start | bytes 3145736 | tf_op jit(solution)/shard_map/ppermute | solution.py:251
  111.3 1.1 mix_kernel.1
  112.4 6.3 %all-to-all-start.3 = ((bf16[16,32,128]{2,1,0:T(8,128)(2,1)}), bf16[16,32,128]{2,1,0:T(8,128)(2,1)S(1)}, u32[]{:S(2)}, u32[]{:S(2)}) async-start(bf16[16,32,128]{2,1,0:T(8,128)(2,1)} %mix_kernel.1), calls=%async_computation.3 | async-start | bytes 262144 | tf_op jit(solution)/shard_map/all_to_all | solution.py:256
  118.7 6.4 %back_kernel.1 = (bf16[112,4096]{1,0:T(8,128)(2,1)}, bf16[112,512]{1,0:T(8,128)(2,1)}, bf16[112,512]{1,0:T(8,128)(2,1)}) custom-call(s32[2]{0:T(128)S(1)} %pad_add_fusion.1.me_ref, bf16[8,2,32,1024]{3,2,1,0:T(8,128)(2,1)} %get-tuple-element.44.own_ref, bf16[8,2,32,1024]{3,2,1,0:T(8,128)(2,1)S(1)} %collective-permute-done.2.near_ref, ...), custom_call_target="tpu_custom_call" | custom-call | flops 1500000000 | bytes 8000000 | tf_op jit(solution)/shard_map/back_kernel/pallas_call | solution.py:339
  125.1 6.0 %all-to-all-done.3.got_ref = bf16[16,32,128]{2,1,0:T(8,128)(2,1)S(1)} async-done(((bf16[16,32,128]{2,1,0:T(8,128)(2,1)}), bf16[16,32,128]{2,1,0:T(8,128)(2,1)S(1)}, u32[]{:S(2)}, u32[]{:S(2)}) %all-to-all-start.3) | async-done | bytes 131104 | tf_op jit(solution)/shard_map/all_to_all | solution.py:256
  (28 shorter events, 4.6 us)
Async XLA Ops:
  0.6 0.7 copy-start
  1.3 0.7 copy-start.1
  3.0 28.9 %all-to-all-start = ((bf16[16,64,128]{2,1,0:T(8,128)(2,1)}), bf16[16,64,128]{2,1,0:T(8,128)(2,1)S(1)}, u32[]{:S(2)}, u32[]{:S(2)}) async-start(bf16[16,64,128]{2,1,0:T(8,128)(2,1)} %pack_kernel.1), calls=%async_computation | async-start | bytes 524288 | tf_op jit(solution)/shard_map/all_to_all | solution.py:293
  20.6 0.6 copy-start.9
  21.4 1.2 copy-start.4
  22.5 1.2 copy-start.5
  23.7 1.2 copy-start.6
  24.9 7.0 %copy-start.2 = (s32[128,2]{0,1:T(2,128)S(1)}, s32[128,2]{0,1:T(2,128)}, u32[]{:S(2)}) copy-start(s32[128,2]{0,1:T(2,128)} %param.18) | copy-start | bytes 3076
  24.9 7.0 %copy-start.3 = (f32[128,2]{0,1:T(2,128)S(1)}, f32[128,2]{0,1:T(2,128)}, u32[]{:S(2)}) copy-start(f32[128,2]{0,1:T(2,128)} %param.19) | copy-start | bytes 3076
  60.8 12.5 %collective-permute-start = (bf16[8,2,32,1024]{3,2,1,0:T(8,128)(2,1)S(1)}, bf16[8,2,32,1024]{3,2,1,0:T(8,128)(2,1)S(1)}, u32[]{:S(2)}, u32[]{:S(2)}) collective-permute-start(bf16[8,2,32,1024]{3,2,1,0:T(8,128)(2,1)S(1)} %get-tuple-element.45.own_ref), channel_id=1, source_target_pairs={{0,1},{1,0},{2,3},{3,2},{4,5},{5,4},{6,7},{7,6},{8,9},{9,8},{10,11... | collective-permute-start | bytes 3145736 | tf_op jit(solution)/shard_map/ppermute | solution.py:251
  74.9 10.1 %collective-permute-start.1 = (bf16[8,2,32,1024]{3,2,1,0:T(8,128)(2,1)S(1)}, bf16[8,2,32,1024]{3,2,1,0:T(8,128)(2,1)S(1)}, u32[]{:S(2)}, u32[]{:S(2)}) collective-permute-start(bf16[8,2,32,1024]{3,2,1,0:T(8,128)(2,1)S(1)} %get-tuple-element.36), channel_id=1, source_target_pairs={{0,1},{1,0},{2,3},{3,2},{4,5},{5,4},{6,7},{7,6},{8,9},{9,8},{10,11... | collective-permute-start | bytes 3145736 | tf_op jit(solution)/shard_map/ppermute | solution.py:251
  77.2 31.4 %collective-permute-start.2 = (bf16[8,2,32,1024]{3,2,1,0:T(8,128)(2,1)}, bf16[8,2,32,1024]{3,2,1,0:T(8,128)(2,1)S(1)}, u32[]{:S(2)}, u32[]{:S(2)}) collective-permute-start(bf16[8,2,32,1024]{3,2,1,0:T(8,128)(2,1)} %get-tuple-element.44.own_ref), channel_id=1, source_target_pairs={{0,4},{4,0},{8,12},{12,8},{16,20},{20,16},{24,28},{28,24},{32,36},... | collective-permute-start | bytes 3145736 | tf_op jit(solution)/shard_map/ppermute | solution.py:336
  85.1 26.2 %copy-start.10 = (bf16[3,64,256]{2,1,0:T(8,128)(2,1)S(1)}, bf16[3,64,256]{2,1,0:T(8,128)(2,1)}, u32[]{:S(2)}) copy-start(bf16[3,64,256]{2,1,0:T(8,128)(2,1)} %copy-done.9) | copy-start | bytes 294916
  86.4 32.3 %copy-start.7 = (bf16[1,512,112]{1,2,0:T(8,128)(2,1)S(1)}, bf16[1,512,112]{1,2,0:T(8,128)(2,1)}, u32[]{:S(2)}) copy-start(bf16[1,512,112]{1,2,0:T(8,128)(2,1)} %param.20) | copy-start | bytes 344068
  86.5 32.3 %copy-start.8 = (bf16[1,512,112]{1,2,0:T(8,128)(2,1)S(1)}, bf16[1,512,112]{1,2,0:T(8,128)(2,1)}, u32[]{:S(2)}) copy-start(bf16[1,512,112]{1,2,0:T(8,128)(2,1)} %param.21) | copy-start | bytes 344068
  86.5 24.8 %all-to-all-start.2 = ((bf16[16,32,1024]{2,1,0:T(8,128)(2,1)}), bf16[16,32,1024]{2,1,0:T(8,128)(2,1)S(1)}, u32[]{:S(2)}, u32[]{:S(2)}) async-start(bf16[16,32,1024]{2,1,0:T(8,128)(2,1)} %bitcast.14), calls=%async_computation.2 | async-start | bytes 2097152 | tf_op jit(solution)/shard_map/all_to_all | solution.py:256
  90.2 28.5 %collective-permute-start.3 = (bf16[8,2,32,1024]{3,2,1,0:T(8,128)(2,1)}, bf16[8,2,32,1024]{3,2,1,0:T(8,128)(2,1)}, u32[]{:S(2)}, u32[]{:S(2)}) collective-permute-start(bf16[8,2,32,1024]{3,2,1,0:T(8,128)(2,1)} %get-tuple-element.44.own_ref), channel_id=1, source_target_pairs={{0,1},{1,0},{2,3},{3,2},{4,5},{5,4},{6,7},{7,6},{8,9},{9,8},{10,11... | collective-permute-start | bytes 3145736 | tf_op jit(solution)/shard_map/ppermute | solution.py:251
  108.6 10.1 %collective-permute-start.4 = (bf16[8,2,32,1024]{3,2,1,0:T(8,128)(2,1)S(1)}, bf16[8,2,32,1024]{3,2,1,0:T(8,128)(2,1)}, u32[]{:S(2)}, u32[]{:S(2)}) collective-permute-start(bf16[8,2,32,1024]{3,2,1,0:T(8,128)(2,1)S(1)} %collective-permute-done.2.near_ref), channel_id=1, source_target_pairs={{0,1},{1,0},{2,3},{3,2},{4,5},{5,4},{6,7},{7,6},{8,9},{9,8},{10,11... | collective-permute-start | bytes 3145736 | tf_op jit(solution)/shard_map/ppermute | solution.py:251
  112.4 18.8 %all-to-all-start.3 = ((bf16[16,32,128]{2,1,0:T(8,128)(2,1)}), bf16[16,32,128]{2,1,0:T(8,128)(2,1)S(1)}, u32[]{:S(2)}, u32[]{:S(2)}) async-start(bf16[16,32,128]{2,1,0:T(8,128)(2,1)} %mix_kernel.1), calls=%async_computation.3 | async-start | bytes 262144 | tf_op jit(solution)/shard_map/all_to_all | solution.py:256

commit v10 on v9

--- a/solution.py
+++ b/solution.py
@@ -333,7 +333,14 @@
     summed = call(down_kernel, rows_b, hidden, down, other_core(partial), flops=2 * 10**8)
     returned = exchange(summed, PLANE)
 
-    near_a = lax.ppermute(own_a, Z, [(z, z ^ 1) for z in range(lax.axis_size(Z))])
+    planes, half = lax.axis_size(Z), experts // 2
+    near_a = jnp.concatenate(
+        [
+            lax.ppermute(own_a[:half], Z, [(z, (z + 1) % planes) for z in range(planes)]),
+            lax.ppermute(own_a[half:], Z, [(z, (z - 1) % planes) for z in range(planes)]),
+        ],
+        axis=0,
+    )
     other_a, other_near = other_core(own_a), other_core(near_a)
     vmem = pl.BlockSpec(memory_space=pltpu.VMEM)
     weight_grad, gate_grad, up_grad = pl.pallas_call(

time: 134 us -> 133 us (level)
  the two profiles are of different devices: /device:TPU:1 before, /device:TPU:4 now
where the time goes in v10:
time: 133 us; the launch traced here: 132 us
  starting transfers between devices  46.2 us (35%)
  waiting for transfers between devices  27.9 us (21%)
  blocking collectives  27.9 us (21%)
  Pallas kernels  16.1 us (12%)
  local copies, waits for them, and re-layouts  11.5 us (9%)
  other arithmetic  1.73 us (1%)
    all_to_all x1, blocking collectives, exchange(): return lax.all_to_all(peers, axes, 0, 0, tiled=True).reshape(array.shape)  27.9 us
    all_to_all x1, starting transfers between devices, per_device(): got = lax.all_to_all(packed, Z, 0, 0, tiled=True)  15.2 us
    all_to_all x2, starting transfers between devices, exchange(): return lax.all_to_all(peers, axes, 0, 0, tiled=True).reshape(array.shape)  13.1 us
    all_to_all x2, waiting for transfers between devices, exchange(): return lax.all_to_all(peers, axes, 0, 0, tiled=True).reshape(array.shape)  12.9 us
    all_to_all x1, waiting for transfers between devices, per_device(): got = lax.all_to_all(packed, Z, 0, 0, tiled=True)  9.11 us
    pallas_call x7, Pallas kernels, call(): pl.pallas_call(body, out_shape=outs, in_specs=[smem] * scalars + [vmem] *...  8.83 us
    ppermute x1, starting transfers between devices, per_device(): lax.ppermute(own_a[:half], Z, [(z, (z + 1) % planes) for z in range(plane...  8.1 us
    ppermute x4, starting transfers between devices, other_core(): return lax.ppermute(array, CORE, [(0, 1), (1, 0)])  7.92 us
  transfers between devices with their start and end apart: 9, of which 6 were waited for; matrix products, arithmetic and copies ran while one was open for 5% of the time, Pallas kernels for 9%

profile of v10, /device:TPU:4, one launch (start us, length us, event | category | flops | bytes accessed | tf_op | source)
XLA Modules:
  0.0 132.3 jit_solution(1197353543288902356)
XLA Ops:
  3.0 15.2 %all-to-all-start = ((bf16[16,64,128]{2,1,0:T(8,128)(2,1)}), bf16[16,64,128]{2,1,0:T(8,128)(2,1)S(1)}, u32[]{:S(2)}, u32[]{:S(2)}) async-start(bf16[16,64,128]{2,1,0:T(8,128)(2,1)} %pack_kernel.1), calls=%async_computation | async-start | bytes 524288 | tf_op jit(solution)/shard_map/all_to_all | solution.py:293
  20.8 1.2 copy-done.5
  22.0 1.2 copy-done.6
  24.4 3.1 %weights_kernel.1 = (bf16[2,2,256,1024]{3,2,1,0:T(8,128)(2,1)S(1)}, bf16[2,2,128,1024]{3,2,1,0:T(8,128)(2,1)S(1)}) custom-call(s32[2]{0:T(128)S(1)} %pad_add_fusion.1.me_ref, bf16[112,4096]{1,0:T(8,128)(2,1)S(1)} %bitcast.36, bf16[112,4096]{1,0:T(8,128)(2,1)S(1)} %bitcast.37, bf16[112,4096]{1,0:T(8,128)(2,1)S(1)} %bitcast.38), custom_call_target="tpu_custom_call" | custom-call | flops 1400000000 | bytes 6000000 | tf_op jit(solution)/shard_map/weights_kernel/pallas_call | solution.py:41
  27.4 9.1 %all-to-all-done.got_ref = bf16[16,64,128]{2,1,0:T(8,128)(2,1)S(1)} async-done(((bf16[16,64,128]{2,1,0:T(8,128)(2,1)}), bf16[16,64,128]{2,1,0:T(8,128)(2,1)S(1)}, u32[]{:S(2)}, u32[]{:S(2)}) %all-to-all-start) | async-done | bytes 262176 | tf_op jit(solution)/shard_map/all_to_all | solution.py:293
  37.2 27.9 %all_to_all.20 = bf16[16,64,1024]{2,1,0:T(8,128)(2,1)S(1)} all-to-all(bf16[16,64,1024]{2,1,0:T(8,128)(2,1)S(1)} %bitcast.31), channel_id=1, replica_groups=mesh['expert_0'=4,'expert_1'=2,'dp_0'=16,'dp_1'=2,'dp_2'=2] {'expert_0',..., dimensions={0} | all-to-all | bytes 4194304 | tf_op jit(solution)/shard_map/all_to_all | solution.py:256
  66.2 1.9 %collective-permute-start = (bf16[8,2,32,1024]{3,2,1,0:T(8,128)(2,1)S(1)}, bf16[8,2,32,1024]{3,2,1,0:T(8,128)(2,1)S(1)}, u32[]{:S(2)}, u32[]{:S(2)}) collective-permute-start(bf16[8,2,32,1024]{3,2,1,0:T(8,128)(2,1)S(1)} %get-tuple-element.47.own_ref), channel_id=1, source_target_pairs={{0,1},{1,0},{2,3},{3,2},{4,5},{5,4},{6,7},{7,6},{8,9},{9,8},{10,11... | collective-permute-start | bytes 3145736 | tf_op jit(solution)/shard_map/ppermute | solution.py:251
  68.2 2.6 %collective-permute-done.other_ref = bf16[8,2,32,1024]{3,2,1,0:T(8,128)(2,1)S(1)} collective-permute-done((bf16[8,2,32,1024]{3,2,1,0:T(8,128)(2,1)S(1)}, bf16[8,2,32,1024]{3,2,1,0:T(8,128)(2,1)S(1)}, u32[]{:S(2)}, u32[]{:S(2)}) %collective-permute-start) | collective-permute-done | bytes 1048608 | tf_op jit(solution)/shard_map/ppermute | solution.py:251
  70.8 1.6 %up_kernel.1 = (bf16[256,128]{1,0:T(8,128)(2,1)S(1)}, bf16[8,2,32,1024]{3,2,1,0:T(8,128)(2,1)S(1)}) custom-call(bf16[8,2,32,1024]{3,2,1,0:T(8,128)(2,1)S(1)} %get-tuple-element.47.own_ref, bf16[8,2,32,1024]{3,2,1,0:T(8,128)(2,1)S(1)} %collective-permute-done.other_ref, bf16[2,2,256,1024]{3,2,1,0:T(8,128)(2,1)S(1)} %get-tuple-element.33.gu_ref, ...), custom_call_target="tpu_custom_call" | custom-call | flops 800000000 | bytes 4000000 | tf_op jit(solution)/shard_map/up_kernel/pallas_call | solution.py:41
  72.4 2.0 %collective-permute-start.1 = (bf16[8,2,32,1024]{3,2,1,0:T(8,128)(2,1)S(1)}, bf16[8,2,32,1024]{3,2,1,0:T(8,128)(2,1)S(1)}, u32[]{:S(2)}, u32[]{:S(2)}) collective-permute-start(bf16[8,2,32,1024]{3,2,1,0:T(8,128)(2,1)S(1)} %get-tuple-element.36), channel_id=1, source_target_pairs={{0,1},{1,0},{2,3},{3,2},{4,5},{5,4},{6,7},{7,6},{8,9},{9,8},{10,11... | collective-permute-start | bytes 3145736 | tf_op jit(solution)/shard_map/ppermute | solution.py:251
  75.5 8.1 %collective-permute-start.2 = (bf16[4,2,32,1024]{3,2,1,0:T(8,128)(2,1)}, bf16[4,2,32,1024]{3,2,1,0:T(8,128)(2,1)}, u32[]{:S(2)}, u32[]{:S(2)}) collective-permute-start(bf16[4,2,32,1024]{3,2,1,0:T(8,128)(2,1)} %get-tuple-element.45), channel_id=1, source_target_pairs={{0,4},{4,8},{8,12},{12,16},{16,20},{20,24},{24,28},{28,32},{32,36}... | collective-permute-start | bytes 1572872 | tf_op jit(solution)/shard_map/ppermute | solution.py:339
  83.6 2.0 %collective-permute-start.3 = (bf16[4,2,32,1024]{3,2,1,0:T(8,128)(2,1)}, bf16[4,2,32,1024]{3,2,1,0:T(8,128)(2,1)}, u32[]{:S(2)}, u32[]{:S(2)}) collective-permute-start(bf16[4,2,32,1024]{3,2,1,0:T(8,128)(2,1)} %get-tuple-element.44), channel_id=1, source_target_pairs={{0,60},{4,0},{8,4},{12,8},{16,12},{20,16},{24,20},{28,24},{32,28},... | collective-permute-start | bytes 1572872 | tf_op jit(solution)/shard_map/ppermute | solution.py:340
  85.6 1.4 %down_kernel.1 = bf16[8,2,32,1024]{3,2,1,0:T(8,128)(2,1)} custom-call(bf16[256,128]{1,0:T(8,128)(2,1)S(1)} %get-tuple-element.35.hidden_ref, bf16[2,2,128,1024]{3,2,1,0:T(8,128)(2,1)S(1)} %get-tuple-element.34.dn_ref, bf16[8,2,32,1024]{3,2,1,0:T(8,128)(2,1)S(1)} %collective-permute-done.1.arrived_ref), custom_call_target="tpu_custom_call" | custom-call | flops 200000000 | bytes 1000000 | tf_op jit(solution)/shard_map/down_kernel/pallas_call | solution.py:41
  87.0 5.5 %all-to-all-start.2 = ((bf16[16,32,1024]{2,1,0:T(8,128)(2,1)}), bf16[16,32,1024]{2,1,0:T(8,128)(2,1)S(1)}, u32[]{:S(2)}, u32[]{:S(2)}) async-start(bf16[16,32,1024]{2,1,0:T(8,128)(2,1)} %bitcast.14), calls=%async_computation.2 | async-start | bytes 2097152 | tf_op jit(solution)/shard_map/all_to_all | solution.py:256
  92.5 2.1 %collective-permute-start.4 = (bf16[8,2,32,1024]{3,2,1,0:T(8,128)(2,1)S(1)}, bf16[8,2,32,1024]{3,2,1,0:T(8,128)(2,1)}, u32[]{:S(2)}, u32[]{:S(2)}) collective-permute-start(bf16[8,2,32,1024]{3,2,1,0:T(8,128)(2,1)S(1)} %copy-done), channel_id=1, source_target_pairs={{0,1},{1,0},{2,3},{3,2},{4,5},{5,4},{6,7},{7,6},{8,9},{9,8},{10,11... | collective-permute-start | bytes 3145736 | tf_op jit(solution)/shard_map/ppermute | solution.py:251
  94.6 1.8 %collective-permute-done.2 = bf16[4,2,32,1024]{3,2,1,0:T(8,128)(2,1)} collective-permute-done((bf16[4,2,32,1024]{3,2,1,0:T(8,128)(2,1)}, bf16[4,2,32,1024]{3,2,1,0:T(8,128)(2,1)}, u32[]{:S(2)}, u32[]{:S(2)}) %collective-permute-start.2) | collective-permute-done | bytes 524320 | tf_op jit(solution)/shard_map/ppermute | solution.py:339
  96.4 1.9 %constant_dynamic-update-slice_fusion.1 = bf16[8,2,32,1024]{3,2,1,0:T(8,128)(2,1)} fusion(bf16[4,2,32,1024]{3,2,1,0:T(8,128)(2,1)} %collective-permute-done.2), kind=kLoop, calls=%fused_computation.1 | loop fusion | bytes 1048576
  98.3 1.4 %collective-permute-done.3 = bf16[4,2,32,1024]{3,2,1,0:T(8,128)(2,1)} collective-permute-done((bf16[4,2,32,1024]{3,2,1,0:T(8,128)(2,1)}, bf16[4,2,32,1024]{3,2,1,0:T(8,128)(2,1)}, u32[]{:S(2)}, u32[]{:S(2)}) %collective-permute-start.3) | collective-permute-done | bytes 524320 | tf_op jit(solution)/shard_map/ppermute | solution.py:340
  99.7 1.9 %constant_dynamic-update-slice_fusion.near_ref = bf16[8,2,32,1024]{3,2,1,0:T(8,128)(2,1)} fusion(bf16[8,2,32,1024]{3,2,1,0:T(8,128)(2,1)} %constant_dynamic-update-slice_fusion.1, bf16[4,2,32,1024]{3,2,1,0:T(8,128)(2,1)} %collective-permute-done.3), kind=kLoop, calls=%fused_computation | loop fusion | bytes 1048576 | tf_op jit(solution)/shard_map/concatenate | solution.py:337
  101.6 1.9 %collective-permute-start.5 = (bf16[8,2,32,1024]{3,2,1,0:T(8,128)(2,1)}, bf16[8,2,32,1024]{3,2,1,0:T(8,128)(2,1)}, u32[]{:S(2)}, u32[]{:S(2)}) collective-permute-start(bf16[8,2,32,1024]{3,2,1,0:T(8,128)(2,1)} %constant_dynamic-update-slice_fusion.near_ref), channel_id=1, source_target_pairs={{0,1},{1,0},{2,3},{3,2},{4,5},{5,4},{6,7},{7,6},{8,9},{9,8},{10,11... | collective-permute-start | bytes 3145736 | tf_op jit(solution)/shard_map/ppermute | solution.py:251
  103.5 5.3 %all-to-all-done.2 = bf16[16,32,1024]{2,1,0:T(8,128)(2,1)S(1)} async-done(((bf16[16,32,1024]{2,1,0:T(8,128)(2,1)}), bf16[16,32,1024]{2,1,0:T(8,128)(2,1)S(1)}, u32[]{:S(2)}, u32[]{:S(2)}) %all-to-all-start.2) | async-done | bytes 1048608 | tf_op jit(solution)/shard_map/all_to_all | solution.py:256
  109.9 7.6 %all-to-all-start.3 = ((bf16[16,32,128]{2,1,0:T(8,128)(2,1)}), bf16[16,32,128]{2,1,0:T(8,128)(2,1)S(1)}, u32[]{:S(2)}, u32[]{:S(2)}) async-start(bf16[16,32,128]{2,1,0:T(8,128)(2,1)} %mix_kernel.1), calls=%async_computation.3 | async-start | bytes 262144 | tf_op jit(solution)/shard_map/all_to_all | solution.py:256
  117.5 6.4 %back_kernel.1 = (bf16[112,4096]{1,0:T(8,128)(2,1)}, bf16[112,512]{1,0:T(8,128)(2,1)}, bf16[112,512]{1,0:T(8,128)(2,1)}) custom-call(s32[2]{0:T(128)S(1)} %pad_add_fusion.1.me_ref, bf16[8,2,32,1024]{3,2,1,0:T(8,128)(2,1)S(1)} %copy-done, bf16[8,2,32,1024]{3,2,1,0:T(8,128)(2,1)} %constant_dynamic-update-slice_fusion.near_ref, ...), custom_call_target="tpu_custom_call" | custom-call | flops 1500000000 | bytes 8000000 | tf_op jit(solution)/shard_map/back_kernel/pallas_call | solution.py:346
  123.9 7.6 %all-to-all-done.3.got_ref = bf16[16,32,128]{2,1,0:T(8,128)(2,1)S(1)} async-done(((bf16[16,32,128]{2,1,0:T(8,128)(2,1)}), bf16[16,32,128]{2,1,0:T(8,128)(2,1)S(1)}, u32[]{:S(2)}, u32[]{:S(2)}) %all-to-all-start.3) | async-done | bytes 131104 | tf_op jit(solution)/shard_map/all_to_all | solution.py:256
  (35 shorter events, 10.8 us)
Async XLA Ops:
  0.6 0.7 copy-start.1
  1.3 0.7 copy-start.2
  3.0 33.6 %all-to-all-start = ((bf16[16,64,128]{2,1,0:T(8,128)(2,1)}), bf16[16,64,128]{2,1,0:T(8,128)(2,1)S(1)}, u32[]{:S(2)}, u32[]{:S(2)}) async-start(bf16[16,64,128]{2,1,0:T(8,128)(2,1)} %pack_kernel.1), calls=%async_computation | async-start | bytes 524288 | tf_op jit(solution)/shard_map/all_to_all | solution.py:293
  20.1 0.6 copy-start.10
  20.8 1.2 copy-start.5
  22.0 1.2 copy-start.6
  23.2 1.2 copy-start.7
  24.4 12.2 %copy-start.3 = (s32[128,2]{0,1:T(2,128)S(1)}, s32[128,2]{0,1:T(2,128)}, u32[]{:S(2)}) copy-start(s32[128,2]{0,1:T(2,128)} %param.18) | copy-start | bytes 3076
  24.4 12.2 %copy-start.4 = (f32[128,2]{0,1:T(2,128)S(1)}, f32[128,2]{0,1:T(2,128)}, u32[]{:S(2)}) copy-start(f32[128,2]{0,1:T(2,128)} %param.19) | copy-start | bytes 3076
  66.2 4.5 %collective-permute-start = (bf16[8,2,32,1024]{3,2,1,0:T(8,128)(2,1)S(1)}, bf16[8,2,32,1024]{3,2,1,0:T(8,128)(2,1)S(1)}, u32[]{:S(2)}, u32[]{:S(2)}) collective-permute-start(bf16[8,2,32,1024]{3,2,1,0:T(8,128)(2,1)S(1)} %get-tuple-element.47.own_ref), channel_id=1, source_target_pairs={{0,1},{1,0},{2,3},{3,2},{4,5},{5,4},{6,7},{7,6},{8,9},{9,8},{10,11... | collective-permute-start | bytes 3145736 | tf_op jit(solution)/shard_map/ppermute | solution.py:251
  72.4 13.2 %collective-permute-start.1 = (bf16[8,2,32,1024]{3,2,1,0:T(8,128)(2,1)S(1)}, bf16[8,2,32,1024]{3,2,1,0:T(8,128)(2,1)S(1)}, u32[]{:S(2)}, u32[]{:S(2)}) collective-permute-start(bf16[8,2,32,1024]{3,2,1,0:T(8,128)(2,1)S(1)} %get-tuple-element.36), channel_id=1, source_target_pairs={{0,1},{1,0},{2,3},{3,2},{4,5},{5,4},{6,7},{7,6},{8,9},{9,8},{10,11... | collective-permute-start | bytes 3145736 | tf_op jit(solution)/shard_map/ppermute | solution.py:251
  75.5 20.9 %collective-permute-start.2 = (bf16[4,2,32,1024]{3,2,1,0:T(8,128)(2,1)}, bf16[4,2,32,1024]{3,2,1,0:T(8,128)(2,1)}, u32[]{:S(2)}, u32[]{:S(2)}) collective-permute-start(bf16[4,2,32,1024]{3,2,1,0:T(8,128)(2,1)} %get-tuple-element.45), channel_id=1, source_target_pairs={{0,4},{4,8},{8,12},{12,16},{16,20},{20,24},{24,28},{28,32},{32,36}... | collective-permute-start | bytes 1572872 | tf_op jit(solution)/shard_map/ppermute | solution.py:339
  83.6 16.1 %collective-permute-start.3 = (bf16[4,2,32,1024]{3,2,1,0:T(8,128)(2,1)}, bf16[4,2,32,1024]{3,2,1,0:T(8,128)(2,1)}, u32[]{:S(2)}, u32[]{:S(2)}) collective-permute-start(bf16[4,2,32,1024]{3,2,1,0:T(8,128)(2,1)} %get-tuple-element.44), channel_id=1, source_target_pairs={{0,60},{4,0},{8,4},{12,8},{16,12},{20,16},{24,20},{28,24},{32,28},... | collective-permute-start | bytes 1572872 | tf_op jit(solution)/shard_map/ppermute | solution.py:340
  85.6 6.9 %copy-start = (bf16[8,2,32,1024]{3,2,1,0:T(8,128)(2,1)S(1)}, bf16[8,2,32,1024]{3,2,1,0:T(8,128)(2,1)}, u32[]{:S(2)}) copy-start(bf16[8,2,32,1024]{3,2,1,0:T(8,128)(2,1)} %get-tuple-element.46.own_ref) | copy-start | bytes 3145732
  87.0 21.8 %copy-start.11 = (bf16[3,64,256]{2,1,0:T(8,128)(2,1)S(1)}, bf16[3,64,256]{2,1,0:T(8,128)(2,1)}, u32[]{:S(2)}) copy-start(bf16[3,64,256]{2,1,0:T(8,128)(2,1)} %copy-done.10) | copy-start | bytes 294916
  87.0 21.8 %all-to-all-start.2 = ((bf16[16,32,1024]{2,1,0:T(8,128)(2,1)}), bf16[16,32,1024]{2,1,0:T(8,128)(2,1)S(1)}, u32[]{:S(2)}, u32[]{:S(2)}) async-start(bf16[16,32,1024]{2,1,0:T(8,128)(2,1)} %bitcast.14), calls=%async_computation.2 | async-start | bytes 2097152 | tf_op jit(solution)/shard_map/all_to_all | solution.py:256
  92.5 25.0 %copy-start.8 = (bf16[1,512,112]{1,2,0:T(8,128)(2,1)S(1)}, bf16[1,512,112]{1,2,0:T(8,128)(2,1)}, u32[]{:S(2)}) copy-start(bf16[1,512,112]{1,2,0:T(8,128)(2,1)} %param.20) | copy-start | bytes 344068
  92.5 25.0 %copy-start.9 = (bf16[1,512,112]{1,2,0:T(8,128)(2,1)S(1)}, bf16[1,512,112]{1,2,0:T(8,128)(2,1)}, u32[]{:S(2)}) copy-start(bf16[1,512,112]{1,2,0:T(8,128)(2,1)} %param.21) | copy-start | bytes 344068
  92.5 24.9 %collective-permute-start.4 = (bf16[8,2,32,1024]{3,2,1,0:T(8,128)(2,1)S(1)}, bf16[8,2,32,1024]{3,2,1,0:T(8,128)(2,1)}, u32[]{:S(2)}, u32[]{:S(2)}) collective-permute-start(bf16[8,2,32,1024]{3,2,1,0:T(8,128)(2,1)S(1)} %copy-done), channel_id=1, source_target_pairs={{0,1},{1,0},{2,3},{3,2},{4,5},{5,4},{6,7},{7,6},{8,9},{9,8},{10,11... | collective-permute-start | bytes 3145736 | tf_op jit(solution)/shard_map/ppermute | solution.py:251
  101.6 15.9 %collective-permute-start.5 = (bf16[8,2,32,1024]{3,2,1,0:T(8,128)(2,1)}, bf16[8,2,32,1024]{3,2,1,0:T(8,128)(2,1)}, u32[]{:S(2)}, u32[]{:S(2)}) collective-permute-start(bf16[8,2,32,1024]{3,2,1,0:T(8,128)(2,1)} %constant_dynamic-update-slice_fusion.near_ref), channel_id=1, source_target_pairs={{0,1},{1,0},{2,3},{3,2},{4,5},{5,4},{6,7},{7,6},{8,9},{9,8},{10,11... | collective-permute-start | bytes 3145736 | tf_op jit(solution)/shard_map/ppermute | solution.py:251
  109.9 21.6 %all-to-all-start.3 = ((bf16[16,32,128]{2,1,0:T(8,128)(2,1)}), bf16[16,32,128]{2,1,0:T(8,128)(2,1)S(1)}, u32[]{:S(2)}, u32[]{:S(2)}) async-start(bf16[16,32,128]{2,1,0:T(8,128)(2,1)} %mix_kernel.1), calls=%async_computation.3 | async-start | bytes 262144 | tf_op jit(solution)/shard_map/all_to_all | solution.py:256

commit v11 on v9

--- a/solution.py
+++ b/solution.py
@@ -84,15 +84,7 @@
                         ]
 
 
-def pack_kernel(x_hbm, g_hbm, out_ref, x_ref, g_ref, sems):
-    copies = [
-        pltpu.make_async_copy(x_hbm, x_ref, sems.at[0]),
-        pltpu.make_async_copy(g_hbm, g_ref, sems.at[1]),
-    ]
-    for copy in copies:
-        copy.start()
-    for copy in copies:
-        copy.wait()
+def pack_kernel(x_ref, g_ref, out_ref):
     x = x_ref[...]
     toks, feats = x.shape
     twice = jnp.concatenate([x, x], axis=0)
@@ -277,16 +269,13 @@
     routes_b, gates_b = twice(routes_new), twice(gates_new)
     routes_a, gates_a = routes_old.T, gates_old.T
 
+    whole = lambda *dims: pl.BlockSpec(dims, lambda i: (0,) * len(dims))
     packed = pl.pallas_call(
         pack_kernel,
         out_shape=shape(16, 2 * F, 128),
-        in_specs=[pl.BlockSpec(memory_space=pltpu.HBM)] * 2,
-        out_specs=pl.BlockSpec(memory_space=pltpu.VMEM),
-        scratch_shapes=[
-            pltpu.VMEM(x_new.shape, BF),
-            pltpu.VMEM(grad_out.shape[::-1], BF),
-            pltpu.SemaphoreType.DMA((2,)),
-        ],
+        grid=(1,),
+        in_specs=[whole(*x_new.shape), whole(*grad_out.shape[::-1])],
+        out_specs=whole(16, 2 * F, 128),
         compiler_params=pltpu.CompilerParams(vmem_limit_bytes=16 * MIB),
         name="pack_kernel",
     )(x_new, grad_out.T)
@@ -318,7 +307,7 @@
         rows_kernel, shape(experts, 2, 2 * CAP_B, 1024), picks, routes_a, gates_a, got
     )
     arrived = exchange(sent, PLANE)
-    own, own_a = arrived[:, :, :CAP_B], arrived[:, :, CAP_B:]
+    own = arrived[:, :, :CAP_B]
 
     hidden, partial = call(
         up_kernel,
@@ -330,6 +319,8 @@
         flops=8 * 10**8,
         moved=4 * 10**6,
     )
+    arrived, partial = lax.optimization_barrier((arrived, partial))
+    own_a = arrived[:, :, CAP_B:]
     summed = call(down_kernel, rows_b, hidden, down, other_core(partial), flops=2 * 10**8)
     returned = exchange(summed, PLANE)
 

time: 134 us -> 132 us (0.985)
  no operation moved by 1% of the time
where the time goes in v11:
time: 132 us; the launch traced here: 131 us
  starting transfers between devices  51.2 us (39%)
  waiting for transfers between devices  28.1 us (21%)
  blocking collectives  27.1 us (21%)
  Pallas kernels  16.1 us (12%)
  local copies, waits for them, and re-layouts  5.8 us (4%)
  other arithmetic  1.73 us (1%)
    all_to_all x1, blocking collectives, exchange(): return lax.all_to_all(peers, axes, 0, 0, tiled=True).reshape(array.shape)  27.1 us
    ppermute x4, starting transfers between devices, other_core(): return lax.ppermute(array, CORE, [(0, 1), (1, 0)])  17.5 us
    ppermute x1, waiting for transfers between devices, per_device(): lax.ppermute(own_a, Z, [(z, z ^ 1) for z in range(lax.axis_size(Z))])  15.9 us
    all_to_all x1, starting transfers between devices, per_device(): got = lax.all_to_all(packed, Z, 0, 0, tiled=True)  15.7 us
    all_to_all x2, starting transfers between devices, exchange(): return lax.all_to_all(peers, axes, 0, 0, tiled=True).reshape(array.shape)  10.1 us
    pallas_call x7, Pallas kernels, call(): pl.pallas_call(body, out_shape=outs, in_specs=[smem] * scalars + [vmem] *...  8.8 us
    ppermute x1, starting transfers between devices, per_device(): lax.ppermute(own_a, Z, [(z, z ^ 1) for z in range(lax.axis_size(Z))])  7.82 us
    pallas_call x1, Pallas kernels, per_device(): pl.pallas_call(back_kernel, out_shape=(shape(hidden_units, 4096), shape(h...  6.39 us
  transfers between devices with their start and end apart: 8, of which 4 were waited for; matrix products, arithmetic and copies ran while one was open for 1% of the time, Pallas kernels for 9%

profile of v11, /device:TPU:1, one launch (start us, length us, event | category | flops | bytes accessed | tf_op | source)
XLA Modules:
  0.0 130.8 jit_solution(14348398511293504912)
XLA Ops:
  2.1 0.9 pack_kernel.1
  2.9 15.7 %all-to-all-start = ((bf16[16,64,128]{2,1,0:T(8,128)(2,1)}), bf16[16,64,128]{2,1,0:T(8,128)(2,1)S(1)}, u32[]{:S(2)}, u32[]{:S(2)}) async-start(bf16[16,64,128]{2,1,0:T(8,128)(2,1)} %pack_kernel.1), calls=%async_computation | async-start | bytes 524288 | tf_op jit(solution)/shard_map/all_to_all | solution.py:282
  18.7 0.8 pad_add_fusion.routes_ref
  19.5 0.8 pad_maximum_fusion.gates_ref
  21.3 1.2 copy-done.4
  22.5 1.2 copy-done.5
  23.7 1.2 copy-done.6
  24.9 3.1 %weights_kernel.1 = (bf16[2,2,256,1024]{3,2,1,0:T(8,128)(2,1)S(1)}, bf16[2,2,128,1024]{3,2,1,0:T(8,128)(2,1)S(1)}) custom-call(s32[2]{0:T(128)S(1)} %pad_add_fusion.1.me_ref, bf16[112,4096]{1,0:T(8,128)(2,1)S(1)} %bitcast.36, bf16[112,4096]{1,0:T(8,128)(2,1)S(1)} %bitcast.37, bf16[112,4096]{1,0:T(8,128)(2,1)S(1)} %bitcast.38), custom_call_target="tpu_custom_call" | custom-call | flops 1400000000 | bytes 6000000 | tf_op jit(solution)/shard_map/weights_kernel/pallas_call | solution.py:41
  27.9 3.9 %all-to-all-done.got_ref = bf16[16,64,128]{2,1,0:T(8,128)(2,1)S(1)} async-done(((bf16[16,64,128]{2,1,0:T(8,128)(2,1)}), bf16[16,64,128]{2,1,0:T(8,128)(2,1)S(1)}, u32[]{:S(2)}, u32[]{:S(2)}) %all-to-all-start) | async-done | bytes 262176 | tf_op jit(solution)/shard_map/all_to_all | solution.py:282
  32.4 27.1 %all_to_all.20 = bf16[16,64,1024]{2,1,0:T(8,128)(2,1)S(1)} all-to-all(bf16[16,64,1024]{2,1,0:T(8,128)(2,1)S(1)} %bitcast.31), channel_id=1, replica_groups=mesh['expert_0'=4,'expert_1'=2,'dp_0'=16,'dp_1'=2,'dp_2'=2] {'expert_0',..., dimensions={0} | all-to-all | bytes 4194304 | tf_op jit(solution)/shard_map/all_to_all | solution.py:248
  59.7 10.3 %collective-permute-start = (bf16[8,2,32,1024]{3,2,1,0:T(8,128)(2,1)S(1)}, bf16[8,2,32,1024]{3,2,1,0:T(8,128)(2,1)S(1)}, u32[]{:S(2)}, u32[]{:S(2)}) collective-permute-start(bf16[8,2,32,1024]{3,2,1,0:T(8,128)(2,1)S(1)} %slice.8.own_ref), channel_id=1, source_target_pairs={{0,1},{1,0},{2,3},{3,2},{4,5},{5,4},{6,7},{7,6},{8,9},{9,8},{10,11... | collective-permute-start | bytes 3145736 | tf_op jit(solution)/shard_map/ppermute | solution.py:243
  69.9 2.3 %collective-permute-done.other_ref = bf16[8,2,32,1024]{3,2,1,0:T(8,128)(2,1)S(1)} collective-permute-done((bf16[8,2,32,1024]{3,2,1,0:T(8,128)(2,1)S(1)}, bf16[8,2,32,1024]{3,2,1,0:T(8,128)(2,1)S(1)}, u32[]{:S(2)}, u32[]{:S(2)}) %collective-permute-start) | collective-permute-done | bytes 1048608 | tf_op jit(solution)/shard_map/ppermute | solution.py:243
  72.2 1.6 %up_kernel.1 = (bf16[256,128]{1,0:T(8,128)(2,1)S(1)}, bf16[8,2,32,1024]{3,2,1,0:T(8,128)(2,1)S(1)}) custom-call(bf16[8,2,32,1024]{3,2,1,0:T(8,128)(2,1)S(1)} %slice.8.own_ref, bf16[8,2,32,1024]{3,2,1,0:T(8,128)(2,1)S(1)} %collective-permute-done.other_ref, bf16[2,2,256,1024]{3,2,1,0:T(8,128)(2,1)S(1)} %get-tuple-element.35.gu_ref, ...), custom_call_target="tpu_custom_call" | custom-call | flops 800000000 | bytes 4000000 | tf_op jit(solution)/shard_map/up_kernel/pallas_call | solution.py:41
  73.8 2.3 %collective-permute-start.1 = (bf16[8,2,32,1024]{3,2,1,0:T(8,128)(2,1)S(1)}, bf16[8,2,32,1024]{3,2,1,0:T(8,128)(2,1)S(1)}, u32[]{:S(2)}, u32[]{:S(2)}) collective-permute-start(bf16[8,2,32,1024]{3,2,1,0:T(8,128)(2,1)S(1)} %get-tuple-element.39), channel_id=1, source_target_pairs={{0,1},{1,0},{2,3},{3,2},{4,5},{5,4},{6,7},{7,6},{8,9},{9,8},{10,11... | collective-permute-start | bytes 3145736 | tf_op jit(solution)/shard_map/ppermute | solution.py:243
  76.2 7.8 %collective-permute-start.2 = (bf16[8,2,32,1024]{3,2,1,0:T(8,128)(2,1)S(1)}, bf16[8,2,32,1024]{3,2,1,0:T(8,128)(2,1)}, u32[]{:S(2)}, u32[]{:S(2)}) collective-permute-start(bf16[8,2,32,1024]{3,2,1,0:T(8,128)(2,1)S(1)} %slice.7.own_ref), channel_id=1, source_target_pairs={{0,4},{4,0},{8,12},{12,8},{16,20},{20,16},{24,28},{28,24},{32,36},... | collective-permute-start | bytes 3145736 | tf_op jit(solution)/shard_map/ppermute | solution.py:327
  84.0 1.4 %down_kernel.1 = bf16[8,2,32,1024]{3,2,1,0:T(8,128)(2,1)} custom-call(bf16[256,128]{1,0:T(8,128)(2,1)S(1)} %get-tuple-element.37.hidden_ref, bf16[2,2,128,1024]{3,2,1,0:T(8,128)(2,1)S(1)} %get-tuple-element.36.dn_ref, bf16[8,2,32,1024]{3,2,1,0:T(8,128)(2,1)S(1)} %collective-permute-done.1.arrived_ref), custom_call_target="tpu_custom_call" | custom-call | flops 200000000 | bytes 1000000 | tf_op jit(solution)/shard_map/down_kernel/pallas_call | solution.py:41
  85.4 3.8 %all-to-all-start.2 = ((bf16[16,32,1024]{2,1,0:T(8,128)(2,1)}), bf16[16,32,1024]{2,1,0:T(8,128)(2,1)S(1)}, u32[]{:S(2)}, u32[]{:S(2)}) async-start(bf16[16,32,1024]{2,1,0:T(8,128)(2,1)} %bitcast.14), calls=%async_computation.2 | async-start | bytes 2097152 | tf_op jit(solution)/shard_map/all_to_all | solution.py:248
  89.2 2.3 %collective-permute-start.3 = (bf16[8,2,32,1024]{3,2,1,0:T(8,128)(2,1)S(1)}, bf16[8,2,32,1024]{3,2,1,0:T(8,128)(2,1)}, u32[]{:S(2)}, u32[]{:S(2)}) collective-permute-start(bf16[8,2,32,1024]{3,2,1,0:T(8,128)(2,1)S(1)} %slice.7.own_ref), channel_id=1, source_target_pairs={{0,1},{1,0},{2,3},{3,2},{4,5},{5,4},{6,7},{7,6},{8,9},{9,8},{10,11... | collective-permute-start | bytes 3145736 | tf_op jit(solution)/shard_map/ppermute | solution.py:243
  91.6 15.9 %collective-permute-done.2.near_ref = bf16[8,2,32,1024]{3,2,1,0:T(8,128)(2,1)} collective-permute-done((bf16[8,2,32,1024]{3,2,1,0:T(8,128)(2,1)S(1)}, bf16[8,2,32,1024]{3,2,1,0:T(8,128)(2,1)}, u32[]{:S(2)}, u32[]{:S(2)}) %collective-permute-start.2) | collective-permute-done | bytes 1048608 | tf_op jit(solution)/shard_map/ppermute | solution.py:327
  107.5 2.6 %collective-permute-start.4 = (bf16[8,2,32,1024]{3,2,1,0:T(8,128)(2,1)}, bf16[8,2,32,1024]{3,2,1,0:T(8,128)(2,1)}, u32[]{:S(2)}, u32[]{:S(2)}) collective-permute-start(bf16[8,2,32,1024]{3,2,1,0:T(8,128)(2,1)} %collective-permute-done.2.near_ref), channel_id=1, source_target_pairs={{0,1},{1,0},{2,3},{3,2},{4,5},{5,4},{6,7},{7,6},{8,9},{9,8},{10,11... | collective-permute-start | bytes 3145736 | tf_op jit(solution)/shard_map/ppermute | solution.py:243
  110.1 1.1 mix_kernel.1
  111.2 6.3 %all-to-all-start.3 = ((bf16[16,32,128]{2,1,0:T(8,128)(2,1)}), bf16[16,32,128]{2,1,0:T(8,128)(2,1)S(1)}, u32[]{:S(2)}, u32[]{:S(2)}) async-start(bf16[16,32,128]{2,1,0:T(8,128)(2,1)} %mix_kernel.1), calls=%async_computation.3 | async-start | bytes 262144 | tf_op jit(solution)/shard_map/all_to_all | solution.py:248
  117.6 6.4 %back_kernel.1 = (bf16[112,4096]{1,0:T(8,128)(2,1)}, bf16[112,512]{1,0:T(8,128)(2,1)}, bf16[112,512]{1,0:T(8,128)(2,1)}) custom-call(s32[2]{0:T(128)S(1)} %pad_add_fusion.1.me_ref, bf16[8,2,32,1024]{3,2,1,0:T(8,128)(2,1)S(1)} %slice.7.own_ref, bf16[8,2,32,1024]{3,2,1,0:T(8,128)(2,1)} %collective-permute-done.2.near_ref, ...), custom_call_target="tpu_custom_call" | custom-call | flops 1500000000 | bytes 8000000 | tf_op jit(solution)/shard_map/back_kernel/pallas_call | solution.py:330
  124.0 6.0 %all-to-all-done.3.got_ref = bf16[16,32,128]{2,1,0:T(8,128)(2,1)S(1)} async-done(((bf16[16,32,128]{2,1,0:T(8,128)(2,1)}), bf16[16,32,128]{2,1,0:T(8,128)(2,1)S(1)}, u32[]{:S(2)}, u32[]{:S(2)}) %all-to-all-start.3) | async-done | bytes 131104 | tf_op jit(solution)/shard_map/all_to_all | solution.py:248
  (29 shorter events, 4.0 us)
Async XLA Ops:
  0.6 0.7 copy-start
  1.3 0.7 copy-start.1
  2.9 28.9 %all-to-all-start = ((bf16[16,64,128]{2,1,0:T(8,128)(2,1)}), bf16[16,64,128]{2,1,0:T(8,128)(2,1)S(1)}, u32[]{:S(2)}, u32[]{:S(2)}) async-start(bf16[16,64,128]{2,1,0:T(8,128)(2,1)} %pack_kernel.1), calls=%async_computation | async-start | bytes 524288 | tf_op jit(solution)/shard_map/all_to_all | solution.py:282
  20.6 0.6 copy-start.9
  21.3 1.2 copy-start.4
  22.5 1.2 copy-start.5
  23.7 1.2 copy-start.6
  24.9 7.0 %copy-start.2 = (s32[128,2]{0,1:T(2,128)S(1)}, s32[128,2]{0,1:T(2,128)}, u32[]{:S(2)}) copy-start(s32[128,2]{0,1:T(2,128)} %param.18) | copy-start | bytes 3076
  24.9 7.0 %copy-start.3 = (f32[128,2]{0,1:T(2,128)S(1)}, f32[128,2]{0,1:T(2,128)}, u32[]{:S(2)}) copy-start(f32[128,2]{0,1:T(2,128)} %param.19) | copy-start | bytes 3076
  59.7 12.5 %collective-permute-start = (bf16[8,2,32,1024]{3,2,1,0:T(8,128)(2,1)S(1)}, bf16[8,2,32,1024]{3,2,1,0:T(8,128)(2,1)S(1)}, u32[]{:S(2)}, u32[]{:S(2)}) collective-permute-start(bf16[8,2,32,1024]{3,2,1,0:T(8,128)(2,1)S(1)} %slice.8.own_ref), channel_id=1, source_target_pairs={{0,1},{1,0},{2,3},{3,2},{4,5},{5,4},{6,7},{7,6},{8,9},{9,8},{10,11... | collective-permute-start | bytes 3145736 | tf_op jit(solution)/shard_map/ppermute | solution.py:243
  73.8 10.2 %collective-permute-start.1 = (bf16[8,2,32,1024]{3,2,1,0:T(8,128)(2,1)S(1)}, bf16[8,2,32,1024]{3,2,1,0:T(8,128)(2,1)S(1)}, u32[]{:S(2)}, u32[]{:S(2)}) collective-permute-start(bf16[8,2,32,1024]{3,2,1,0:T(8,128)(2,1)S(1)} %get-tuple-element.39), channel_id=1, source_target_pairs={{0,1},{1,0},{2,3},{3,2},{4,5},{5,4},{6,7},{7,6},{8,9},{9,8},{10,11... | collective-permute-start | bytes 3145736 | tf_op jit(solution)/shard_map/ppermute | solution.py:243
  76.2 31.3 %collective-permute-start.2 = (bf16[8,2,32,1024]{3,2,1,0:T(8,128)(2,1)S(1)}, bf16[8,2,32,1024]{3,2,1,0:T(8,128)(2,1)}, u32[]{:S(2)}, u32[]{:S(2)}) collective-permute-start(bf16[8,2,32,1024]{3,2,1,0:T(8,128)(2,1)S(1)} %slice.7.own_ref), channel_id=1, source_target_pairs={{0,4},{4,0},{8,12},{12,8},{16,20},{20,16},{24,28},{28,24},{32,36},... | collective-permute-start | bytes 3145736 | tf_op jit(solution)/shard_map/ppermute | solution.py:327
  84.0 26.1 %copy-start.10 = (bf16[3,64,256]{2,1,0:T(8,128)(2,1)S(1)}, bf16[3,64,256]{2,1,0:T(8,128)(2,1)}, u32[]{:S(2)}) copy-start(bf16[3,64,256]{2,1,0:T(8,128)(2,1)} %copy-done.9) | copy-start | bytes 294916
  85.4 32.2 %copy-start.7 = (bf16[1,512,112]{1,2,0:T(8,128)(2,1)S(1)}, bf16[1,512,112]{1,2,0:T(8,128)(2,1)}, u32[]{:S(2)}) copy-start(bf16[1,512,112]{1,2,0:T(8,128)(2,1)} %param.20) | copy-start | bytes 344068
  85.4 32.2 %copy-start.8 = (bf16[1,512,112]{1,2,0:T(8,128)(2,1)S(1)}, bf16[1,512,112]{1,2,0:T(8,128)(2,1)}, u32[]{:S(2)}) copy-start(bf16[1,512,112]{1,2,0:T(8,128)(2,1)} %param.21) | copy-start | bytes 344068
  85.4 24.7 %all-to-all-start.2 = ((bf16[16,32,1024]{2,1,0:T(8,128)(2,1)}), bf16[16,32,1024]{2,1,0:T(8,128)(2,1)S(1)}, u32[]{:S(2)}, u32[]{:S(2)}) async-start(bf16[16,32,1024]{2,1,0:T(8,128)(2,1)} %bitcast.14), calls=%async_computation.2 | async-start | bytes 2097152 | tf_op jit(solution)/shard_map/all_to_all | solution.py:248
  89.2 28.3 %collective-permute-start.3 = (bf16[8,2,32,1024]{3,2,1,0:T(8,128)(2,1)S(1)}, bf16[8,2,32,1024]{3,2,1,0:T(8,128)(2,1)}, u32[]{:S(2)}, u32[]{:S(2)}) collective-permute-start(bf16[8,2,32,1024]{3,2,1,0:T(8,128)(2,1)S(1)} %slice.7.own_ref), channel_id=1, source_target_pairs={{0,1},{1,0},{2,3},{3,2},{4,5},{5,4},{6,7},{7,6},{8,9},{9,8},{10,11... | collective-permute-start | bytes 3145736 | tf_op jit(solution)/shard_map/ppermute | solution.py:243
  107.5 10.1 %collective-permute-start.4 = (bf16[8,2,32,1024]{3,2,1,0:T(8,128)(2,1)}, bf16[8,2,32,1024]{3,2,1,0:T(8,128)(2,1)}, u32[]{:S(2)}, u32[]{:S(2)}) collective-permute-start(bf16[8,2,32,1024]{3,2,1,0:T(8,128)(2,1)} %collective-permute-done.2.near_ref), channel_id=1, source_target_pairs={{0,1},{1,0},{2,3},{3,2},{4,5},{5,4},{6,7},{7,6},{8,9},{9,8},{10,11... | collective-permute-start | bytes 3145736 | tf_op jit(solution)/shard_map/ppermute | solution.py:243
  111.2 18.8 %all-to-all-start.3 = ((bf16[16,32,128]{2,1,0:T(8,128)(2,1)}), bf16[16,32,128]{2,1,0:T(8,128)(2,1)S(1)}, u32[]{:S(2)}, u32[]{:S(2)}) async-start(bf16[16,32,128]{2,1,0:T(8,128)(2,1)} %mix_kernel.1), calls=%async_computation.3 | async-start | bytes 262144 | tf_op jit(solution)/shard_map/all_to_all | solution.py:248
